TPU v7x, 32 devices: a whole 2x2x4 slice. The times are simulated.
32 devices in a mesh: row: 4 (over y, x), col: 8 (over z, core).
Axes of the slice: x: 2, y: 2, z: 4, core: 2. Of those that a mesh axis runs over, the one named last changes fastest.
Arguments:
- tokens: bfloat16 [8192, 1024], P(('row', 'col')), may hold values from -6 to 6
- block_ids: int32 [4, 2048], P('row', 'col'), may hold values from 0 to 7, never falling along the last dimension, each value on 1 to 512 neighbouring positions
- expert_ids: int32 [8192], P(('row', 'col')), may hold values from 0 to 7, as said below
- cotangent: bfloat16 [8192, 1024], P(('row', 'col')), may hold values from -6 to 6
- norm_gain: bfloat16 [1024], P(('row', 'col')), may hold values from 0.5 to 1.5
- norm_shift: bfloat16 [1024], P(('row', 'col')), may hold values from -0.059814453 to 0.059814453
- w_query: bfloat16 [1024, 1024], P('row', 'col'), may hold values from -0.1875 to 0.1875
- w_key: bfloat16 [1024, 1024], P('row', 'col'), may hold values from -0.1875 to 0.1875
- w_value: bfloat16 [1024, 1024], P('row', 'col'), may hold values from -0.1875 to 0.1875
- w_output: bfloat16 [1024, 1024], P('row', 'col'), may hold values from -2 to 2
- centroids: bfloat16 [8, 1024], P('col', 'row'), may hold values from -0.09375 to 0.09375
- expert_gain: bfloat16 [8, 2, 1024], P('col', None, 'row'), may hold values from 0.5 to 1.5
- expert_shift: bfloat16 [8, 2, 1024], P('col', None, 'row'), may hold values from -0.59765625 to 0.59765625
- w_in: bfloat16 [8, 2, 1024, 4096], P('col', None, None, 'row'), may hold values from -0.1875 to 0.1875
- b_in: bfloat16 [8, 2, 4096], P('col', None, 'row'), may hold values from -0.59765625 to 0.59765625
- w_back: bfloat16 [8, 2, 4096, 1024], P('col', None, 'row'), may hold values from -0.09375 to 0.09375
- b_back: bfloat16 [8, 2, 1024], P('col', None, 'row'), may hold values from -0.59765625 to 0.59765625
Outputs:
- output: bfloat16 [8192, 1024], P(('row', 'col'))
- tokens_grad: float32 [8192, 1024], P(('row', 'col'))
- norm_gain_grad: float32 [1024], P(('row', 'col'))
- norm_shift_grad: float32 [1024], P(('row', 'col'))
- w_query_grad: float32 [1024, 1024], P('row', 'col')
- w_key_grad: float32 [1024, 1024], P('row', 'col')
- w_value_grad: float32 [1024, 1024], P('row', 'col')
- w_output_grad: float32 [1024, 1024], P('row', 'col')
- centroids_grad: float32 [8, 1024], P('col', 'row')
- expert_gain_grad: float32 [8, 2, 1024], P('col', None, 'row')
- expert_shift_grad: float32 [8, 2, 1024], P('col', None, 'row')
- w_in_grad: float32 [8, 2, 1024, 4096], P('col', None, None, 'row')
- b_in_grad: float32 [8, 2, 4096], P('col', None, 'row')
- w_back_grad: float32 [8, 2, 4096, 1024], P('col', None, 'row')
- b_back_grad: float32 [8, 2, 1024], P('col', None, 'row')
Inputs may be any that keep to these rules, and one draw needn't show every extreme that they name: `block_ids`: in each sequence the block numbers start at 0, never fall and rise by one at each new block; a block holds 1 to 512 positions. `expert_ids`: the rows of one device (256 aligned rows) name every expert exactly 32 times.
All inputs are finite; a program needn't handle non-finite values.
Results may differ from a plain program's by a relative error of at most 0.02.
Values may be sent and summed in bfloat16 or wider, within the bound.
No kernel may reach another device: no remote copies, remote signals or barrier semaphores. Data moves between devices by JAX's collectives and lax.ppermute only.
A program may use at most 320 MiB of HBM per device.

v0:
```python
import math

import jax
import jax.numpy as jnp
from jax import lax
from jax.sharding import PartitionSpec as P

HEADS = 16


EPS = 1e-05
NEG = -1e30
BLOCK_LIMIT = 512


def layer_stats(stream):
    center = stream - jnp.mean(stream, axis=-1, keepdims=True)
    inv_root = lax.rsqrt(jnp.mean(center * center, axis=-1, keepdims=True) + EPS)
    return (center * inv_root, inv_root)


def norm_back(grad_normed, unit_rows, inv_root, gain_full):
    grad_unit = grad_normed * gain_full
    mean_first = jnp.mean(grad_unit, axis=-1, keepdims=True)
    mean_second = jnp.mean(grad_unit * unit_rows, axis=-1, keepdims=True)
    return inv_root * (grad_unit - mean_first - unit_rows * mean_second)


def gelu_slope(pre_act):
    return (
        0.5 * (1.0 + lax.erf(pre_act * 0.7071067811865476))
        + pre_act * jnp.exp(-0.5 * pre_act * pre_act) * 0.3989422804014327
    )


def unblock(gathered, row_total, col_total):
    block_rows = gathered.shape[0] // (row_total * col_total)
    block_cols = gathered.shape[1]
    tiles = gathered.reshape(row_total, col_total, block_rows, block_cols)
    return tiles.transpose(0, 2, 1, 3).reshape(row_total * block_rows, col_total * block_cols)


def blockify(full_matrix, row_total, col_total):
    block_rows = full_matrix.shape[0] // row_total
    block_cols = full_matrix.shape[1] // col_total
    tiles = full_matrix.reshape(row_total, block_rows, col_total, block_cols)
    return tiles.transpose(0, 2, 1, 3).reshape(row_total * col_total * block_rows, block_cols)


def head_view(matrix_rows, head_count):
    return matrix_rows.reshape(matrix_rows.shape[0], head_count, matrix_rows.shape[1] // head_count)


def key_blocks(key_part, value_part, seg_part, head_count):
    key_total = key_part.shape[0]
    block_rows = math.gcd(key_total, BLOCK_LIMIT)
    width_head = key_part.shape[1] // head_count
    shape_four = (key_total // block_rows, block_rows, head_count, width_head)
    return (
        key_part.reshape(shape_four),
        value_part.reshape(shape_four),
        seg_part.reshape(key_total // block_rows, block_rows),
    )


def masked_scores(query_heads, key_rows, seg_query, seg_rows):
    scale_factor = query_heads.shape[2] ** (-0.5)
    scores = (
        jnp.einsum("qhd,khd->hqk", query_heads, key_rows, preferred_element_type=jnp.float32)
        * scale_factor
    )
    allowed = seg_rows[None, None, :] <= seg_query[None, :, None]
    return (scores, allowed)


def attend(query_heads, key_all, value_all, seg_query, seg_keys, head_count):
    tok_rows = query_heads.shape[0]
    width_head = query_heads.shape[2]
    key_split, value_split, seg_split = key_blocks(key_all, value_all, seg_keys, head_count)

    def update(state_now, key_rows, value_rows, seg_rows):
        run_max, run_sum, running = state_now
        scores, allowed = masked_scores(query_heads, key_rows, seg_query, seg_rows)
        new_max = jnp.maximum(run_max, jnp.max(jnp.where(allowed, scores, NEG), axis=2))
        weights = jnp.exp(jnp.where(allowed, scores - new_max[:, :, None], NEG))
        factor = jnp.exp(run_max - new_max)
        new_sum = run_sum * factor + jnp.sum(weights, axis=2)
        new_running = running * factor[:, :, None] + jnp.einsum(
            "hqk,khd->hqd",
            weights.astype(jnp.bfloat16),
            value_rows,
            preferred_element_type=jnp.float32,
        )
        return (new_max, new_sum, new_running)

    def attend_visit(state_now, members):
        key_rows, value_rows, seg_rows = members

        def attend_compute(state_in):
            return update(state_in, key_rows, value_rows, seg_rows)

        def attend_unchanged(state_in):
            return state_in

        return (
            lax.cond(seg_rows[0] <= seg_query[-1], attend_compute, attend_unchanged, state_now),
            None,
        )

    initial = (
        jnp.full((head_count, tok_rows), NEG, jnp.float32),
        jnp.zeros((head_count, tok_rows), jnp.float32),
        jnp.zeros((head_count, tok_rows, width_head), jnp.float32),
    )
    finished, unused = lax.scan(attend_visit, initial, (key_split, value_split, seg_split))
    run_max, run_sum, running = finished
    context = (
        (running / run_sum[:, :, None])
        .transpose(1, 0, 2)
        .reshape(tok_rows, head_count * width_head)
    )
    return (context, run_max + jnp.log(run_sum))


def score_grads(
    query_heads, grad_heads, logsum, row_delta, key_rows, value_rows, seg_query, seg_rows
):
    scores, allowed = masked_scores(query_heads, key_rows, seg_query, seg_rows)
    probs_full = jnp.exp(jnp.where(allowed, scores - logsum[:, :, None], NEG))
    grad_probs = jnp.einsum(
        "qhd,khd->hqk", grad_heads, value_rows, preferred_element_type=jnp.float32
    )
    grad_scores = (probs_full * (grad_probs - row_delta[:, :, None])).astype(jnp.bfloat16)
    return (probs_full, grad_scores)


def query_grads(
    query_heads, grad_heads, logsum, row_delta, key_all, value_all, seg_query, seg_keys, head_count
):
    key_split, value_split, seg_split = key_blocks(key_all, value_all, seg_keys, head_count)
    scale_factor = query_heads.shape[2] ** (-0.5)

    def query_visit(running, members):
        key_rows, value_rows, seg_rows = members

        def query_compute(running_in):
            unused_probs, grad_scores = score_grads(
                query_heads,
                grad_heads,
                logsum,
                row_delta,
                key_rows,
                value_rows,
                seg_query,
                seg_rows,
            )
            return (
                running_in
                + jnp.einsum(
                    "hqk,khd->qhd", grad_scores, key_rows, preferred_element_type=jnp.float32
                )
                * scale_factor
            )

        def query_unchanged(running_in):
            return running_in

        return (
            lax.cond(seg_rows[0] <= seg_query[-1], query_compute, query_unchanged, running),
            None,
        )

    summed, unused = lax.scan(
        query_visit, jnp.zeros(query_heads.shape, jnp.float32), (key_split, value_split, seg_split)
    )
    return summed.reshape(query_heads.shape[0], query_heads.shape[1] * query_heads.shape[2])


def shards(
    tokens,
    block_ids,
    expert_ids,
    cotangent,
    norm_gain,
    norm_shift,
    w_query,
    w_key,
    w_value,
    w_output,
    centroids,
    expert_gain,
    expert_shift,
    w_in,
    b_in,
    w_back,
    b_back,
):
    row_total = lax.axis_size("row")
    col_total = lax.axis_size("col")
    tok_rows, model_width = tokens.shape
    head_count = HEADS
    params = (
        lax.all_gather(w_query, ("row", "col"), axis=0, tiled=True),
        lax.all_gather(w_key, ("row", "col"), axis=0, tiled=True),
        lax.all_gather(w_value, ("row", "col"), axis=0, tiled=True),
        lax.all_gather(w_output, ("row", "col"), axis=0, tiled=True),
        lax.all_gather(norm_gain, ("row", "col"), axis=0, tiled=True),
        lax.all_gather(norm_shift, ("row", "col"), axis=0, tiled=True),
        lax.all_gather(centroids, ("row", "col"), axis=0, tiled=True),
    )
    full_query = unblock(params[0], row_total, col_total)
    full_key = unblock(params[1], row_total, col_total)
    full_value = unblock(params[2], row_total, col_total)
    full_output = unblock(params[3], row_total, col_total)
    gain_attn = params[4].astype(jnp.float32)
    shift_attn = params[5].astype(jnp.float32)
    cent_local = centroids.shape[0]
    cent_cols = params[6].shape[1]
    cent_tiles = params[6].reshape(row_total, col_total, cent_local, cent_cols)
    full_centroids = cent_tiles.transpose(1, 2, 0, 3).reshape(
        col_total * cent_local, row_total * cent_cols
    )
    expert_total = full_centroids.shape[0]
    slot_rows = tok_rows // col_total
    inputs = tokens.astype(jnp.float32)
    unit_attn, inv_attn = layer_stats(inputs)
    normed = (unit_attn * gain_attn + shift_attn).astype(jnp.bfloat16)
    queries = jnp.dot(normed, full_query, preferred_element_type=jnp.float32).astype(jnp.bfloat16)
    key_local = jnp.dot(normed, full_key, preferred_element_type=jnp.float32).astype(jnp.bfloat16)
    value_local = jnp.dot(normed, full_value, preferred_element_type=jnp.float32).astype(
        jnp.bfloat16
    )
    seg_local = block_ids.reshape(tok_rows)
    key_all, value_all, seg_all = (
        lax.all_gather(key_local, "col", axis=0, tiled=True),
        lax.all_gather(value_local, "col", axis=0, tiled=True),
        lax.all_gather(seg_local.astype(jnp.bfloat16), "col", axis=0, tiled=True),
    )
    seg_query = seg_local.astype(jnp.float32)
    seg_keys = seg_all.astype(jnp.float32)
    query_heads = head_view(queries, head_count)
    context, logsum = attend(query_heads, key_all, value_all, seg_query, seg_keys, head_count)
    context_low = context.astype(jnp.bfloat16)
    residual = inputs + jnp.dot(context_low, full_output, preferred_element_type=jnp.float32)
    shared = residual.astype(jnp.bfloat16)
    shared_full = shared.astype(jnp.float32)
    onehot = expert_ids[:, None] == jnp.arange(expert_total, dtype=jnp.int32)[None, :]
    cent_rows = jnp.dot(
        onehot.astype(jnp.bfloat16), full_centroids, preferred_element_type=jnp.float32
    )
    gate_vals = jax.nn.sigmoid(jnp.sum(shared_full * cent_rows, axis=1))
    sorting = jnp.argsort(expert_ids, stable=True)
    inverse = jnp.argsort(sorting, stable=True)
    arrived = lax.all_to_all(
        jnp.take(shared, sorting, axis=0).reshape(col_total, slot_rows, model_width),
        "col",
        split_axis=0,
        concat_axis=0,
        tiled=True,
    ).reshape(tok_rows, model_width)
    stream = arrived.astype(jnp.float32)
    stored = []
    for sublayer in range(2):
        full_in, full_back, bias_in, gain_expert, shift_expert, bias_back = (
            lax.all_gather(w_in[0, sublayer], "row", axis=1, tiled=True),
            lax.all_gather(w_back[0, sublayer], "row", axis=0, tiled=True),
            lax.all_gather(b_in[0, sublayer], "row", axis=0, tiled=True),
            lax.all_gather(expert_gain[0, sublayer], "row", axis=0, tiled=True),
            lax.all_gather(expert_shift[0, sublayer], "row", axis=0, tiled=True),
            lax.all_gather(b_back[0, sublayer], "row", axis=0, tiled=True),
        )
        unit_rows, inv_root = layer_stats(stream)
        gain_full = gain_expert.astype(jnp.float32)
        normed_expert = (unit_rows * gain_full + shift_expert.astype(jnp.float32)).astype(
            jnp.bfloat16
        )
        pre_act = jnp.dot(
            normed_expert, full_in, preferred_element_type=jnp.float32
        ) + bias_in.astype(jnp.float32)
        hidden = jax.nn.gelu(pre_act, approximate=False).astype(jnp.bfloat16)
        branch = jnp.dot(hidden, full_back, preferred_element_type=jnp.float32)
        stored.append(
            (full_in, full_back, gain_full, unit_rows, inv_root, normed_expert, pre_act, hidden)
        )
        stream = stream + branch + bias_back.astype(jnp.float32)
    expert_low = stream.astype(jnp.bfloat16)
    returned = lax.all_to_all(
        expert_low.reshape(col_total, slot_rows, model_width),
        "col",
        split_axis=0,
        concat_axis=0,
        tiled=True,
    ).reshape(tok_rows, model_width)
    back_vals = jnp.take(returned, inverse, axis=0).astype(jnp.float32)
    output = (residual + gate_vals[:, None] * back_vals).astype(jnp.bfloat16)
    grad_out = cotangent.astype(jnp.float32)
    grad_logit = jnp.sum(grad_out * back_vals, axis=1) * gate_vals * (1.0 - gate_vals)
    grad_back = (grad_out * gate_vals[:, None]).astype(jnp.bfloat16)
    sent_grad = lax.all_to_all(
        jnp.take(grad_back, sorting, axis=0).reshape(col_total, slot_rows, model_width),
        "col",
        split_axis=0,
        concat_axis=0,
        tiled=True,
    ).reshape(tok_rows, model_width)
    grad_stream = sent_grad.astype(jnp.float32)
    grad_lists = ([], [], [], [], [], [])
    for sublayer in (1, 0):
        full_in, full_back, gain_full, unit_rows, inv_root, normed_expert, pre_act, hidden = stored[
            sublayer
        ]
        grad_branch = grad_stream.astype(jnp.bfloat16)
        part_back = jnp.einsum("tf,td->fd", hidden, grad_branch, preferred_element_type=jnp.float32)
        grad_hidden = jnp.einsum(
            "td,fd->tf", grad_branch, full_back, preferred_element_type=jnp.float32
        )
        grad_pre = (grad_hidden * gelu_slope(pre_act)).astype(jnp.bfloat16)
        part_in = jnp.einsum(
            "td,tf->df", normed_expert, grad_pre, preferred_element_type=jnp.float32
        )
        grad_normed = jnp.einsum("tf,df->td", grad_pre, full_in, preferred_element_type=jnp.float32)
        summed = (
            lax.psum_scatter(
                part_in.astype(jnp.bfloat16), "row", scatter_dimension=1, tiled=True
            ).astype(jnp.float32),
            lax.psum_scatter(
                part_back.astype(jnp.bfloat16), "row", scatter_dimension=0, tiled=True
            ).astype(jnp.float32),
            lax.psum_scatter(
                jnp.sum(grad_pre.astype(jnp.float32), axis=0).astype(jnp.bfloat16),
                "row",
                scatter_dimension=0,
                tiled=True,
            ).astype(jnp.float32),
            lax.psum_scatter(
                jnp.sum(grad_normed * unit_rows, axis=0).astype(jnp.bfloat16),
                "row",
                scatter_dimension=0,
                tiled=True,
            ).astype(jnp.float32),
            lax.psum_scatter(
                jnp.sum(grad_normed, axis=0).astype(jnp.bfloat16),
                "row",
                scatter_dimension=0,
                tiled=True,
            ).astype(jnp.float32),
            lax.psum_scatter(
                jnp.sum(grad_stream, axis=0).astype(jnp.bfloat16),
                "row",
                scatter_dimension=0,
                tiled=True,
            ).astype(jnp.float32),
        )
        for position in range(6):
            grad_lists[position].insert(0, summed[position])
        grad_stream = grad_stream + norm_back(grad_normed, unit_rows, inv_root, gain_full)
    w_in_grad = jnp.stack(grad_lists[0])[None]
    w_back_grad = jnp.stack(grad_lists[1])[None]
    b_in_grad = jnp.stack(grad_lists[2])[None]
    expert_gain_grad = jnp.stack(grad_lists[3])[None]
    expert_shift_grad = jnp.stack(grad_lists[4])[None]
    b_back_grad = jnp.stack(grad_lists[5])[None]
    returned_grad = lax.all_to_all(
        grad_stream.astype(jnp.bfloat16).reshape(col_total, slot_rows, model_width),
        "col",
        split_axis=0,
        concat_axis=0,
        tiled=True,
    ).reshape(tok_rows, model_width)
    grad_shared = (
        jnp.take(returned_grad, inverse, axis=0).astype(jnp.float32)
        + grad_logit[:, None] * cent_rows
    )
    grad_residual = grad_out + grad_shared
    part_cent = jnp.einsum(
        "te,td->ed",
        onehot.astype(jnp.float32),
        grad_logit[:, None] * shared_full,
        precision=lax.Precision.HIGHEST,
    )
    grad_attended = grad_residual.astype(jnp.bfloat16)
    part_output = jnp.einsum(
        "td,te->de", context_low, grad_attended, preferred_element_type=jnp.float32
    )
    grad_context = jnp.einsum(
        "te,de->td", grad_attended, full_output, preferred_element_type=jnp.float32
    ).astype(jnp.bfloat16)
    grad_heads = head_view(grad_context, head_count)
    row_delta = jnp.sum(
        grad_heads.astype(jnp.float32) * head_view(context, head_count), axis=2
    ).transpose(1, 0)
    grad_query = query_grads(
        query_heads,
        grad_heads,
        logsum,
        row_delta,
        key_all,
        value_all,
        seg_query,
        seg_keys,
        head_count,
    ).astype(jnp.bfloat16)
    scale_factor = query_heads.shape[2] ** (-0.5)
    key_split, value_split, seg_split = key_blocks(key_all, value_all, seg_keys, head_count)
    block_rows = seg_split.shape[1]

    def one_block(members):

        def one_compute(operands):
            probs_full, grad_scores = score_grads(
                query_heads,
                grad_heads,
                logsum,
                row_delta,
                operands[0],
                operands[1],
                seg_query,
                operands[2],
            )
            grad_key_rows = (
                jnp.einsum(
                    "hqk,qhd->khd", grad_scores, query_heads, preferred_element_type=jnp.float32
                )
                * scale_factor
            )
            grad_value_rows = jnp.einsum(
                "hqk,qhd->khd",
                probs_full.astype(jnp.bfloat16),
                grad_heads,
                preferred_element_type=jnp.float32,
            )
            return jnp.concatenate(
                [
                    grad_key_rows.reshape(block_rows, model_width),
                    grad_value_rows.reshape(block_rows, model_width),
                ],
                axis=1,
            )

        def vacant(operands):
            return jnp.zeros((block_rows, 2 * model_width), jnp.float32)

        return lax.cond(members[2][0] <= seg_query[-1], one_compute, vacant, members)

    key_value_grads = lax.psum_scatter(
        lax.map(one_block, (key_split, value_split, seg_split))
        .reshape(tok_rows * lax.axis_size("col"), 2 * model_width)
        .astype(jnp.bfloat16),
        "col",
        scatter_dimension=0,
        tiled=True,
    ).astype(jnp.float32)
    grad_key = key_value_grads[:, :model_width].astype(jnp.bfloat16)
    grad_value = key_value_grads[:, model_width:].astype(jnp.bfloat16)
    part_query = jnp.einsum("td,te->de", normed, grad_query, preferred_element_type=jnp.float32)
    part_key = jnp.einsum("td,te->de", normed, grad_key, preferred_element_type=jnp.float32)
    part_value = jnp.einsum("td,te->de", normed, grad_value, preferred_element_type=jnp.float32)
    grad_normed_attn = jnp.einsum(
        "te,de->td", grad_query, full_query, preferred_element_type=jnp.float32
    )
    grad_normed_attn = grad_normed_attn + jnp.einsum(
        "te,de->td", grad_key, full_key, preferred_element_type=jnp.float32
    )
    grad_normed_attn = grad_normed_attn + jnp.einsum(
        "te,de->td", grad_value, full_value, preferred_element_type=jnp.float32
    )
    part_gain = jnp.sum(grad_normed_attn * unit_attn, axis=0)
    part_shift = jnp.sum(grad_normed_attn, axis=0)
    tokens_grad = grad_residual + norm_back(grad_normed_attn, unit_attn, inv_attn, gain_attn)
    cent_arranged = (
        part_cent.reshape(col_total, cent_local, row_total, cent_cols)
        .transpose(2, 0, 1, 3)
        .reshape(row_total * col_total * cent_local, cent_cols)
    )
    attn_summed = (
        lax.psum_scatter(
            blockify(part_query, row_total, col_total),
            ("row", "col"),
            scatter_dimension=0,
            tiled=True,
        ),
        lax.psum_scatter(
            blockify(part_key, row_total, col_total),
            ("row", "col"),
            scatter_dimension=0,
            tiled=True,
        ),
        lax.psum_scatter(
            blockify(part_value, row_total, col_total),
            ("row", "col"),
            scatter_dimension=0,
            tiled=True,
        ),
        lax.psum_scatter(
            blockify(part_output, row_total, col_total),
            ("row", "col"),
            scatter_dimension=0,
            tiled=True,
        ),
        lax.psum_scatter(part_gain, ("row", "col"), scatter_dimension=0, tiled=True),
        lax.psum_scatter(part_shift, ("row", "col"), scatter_dimension=0, tiled=True),
        lax.psum_scatter(cent_arranged, ("row", "col"), scatter_dimension=0, tiled=True),
    )
    return (
        output,
        tokens_grad,
        attn_summed[4],
        attn_summed[5],
        attn_summed[0],
        attn_summed[1],
        attn_summed[2],
        attn_summed[3],
        attn_summed[6],
        expert_gain_grad,
        expert_shift_grad,
        w_in_grad,
        b_in_grad,
        w_back_grad,
        b_back_grad,
    )


def solution(mesh):
    placed = (
        P(("row", "col"), None),
        P("row", "col"),
        P(("row", "col")),
        P(("row", "col"), None),
        P(("row", "col")),
        P(("row", "col")),
        P("row", "col"),
        P("row", "col"),
        P("row", "col"),
        P("row", "col"),
        P("col", "row"),
        P("col", None, "row"),
        P("col", None, "row"),
        P("col", None, None, "row"),
        P("col", None, "row"),
        P("col", None, "row", None),
        P("col", None, "row"),
    )
    return jax.shard_map(
        shards,
        mesh=mesh,
        in_specs=placed,
        out_specs=(
            P(("row", "col"), None),
            P(("row", "col"), None),
            P(("row", "col")),
            P(("row", "col")),
            P("row", "col"),
            P("row", "col"),
            P("row", "col"),
            P("row", "col"),
            P("col", "row"),
            P("col", None, "row"),
            P("col", None, "row"),
            P("col", None, None, "row"),
            P("col", None, "row"),
            P("col", None, "row", None),
            P("col", None, "row"),
        ),
        check_vma=False,
    )
```

profile of v0, /device:TPU:0, one launch (start us, length us, event | category | flops | bytes accessed | tf_op | source)
XLA Modules:
  0.0 1930.3 jit_solution(7551427072085658731)
XLA Ops:
  11.7 42.0 %all-reduce.14 = (bf16[1024]{0:T(1024)(128)(2,1)S(1)}, bf16[1024]{0:T(1024)(128)(2,1)S(1)}) all-reduce(bf16[1024]{0:T(1024)(128)(2,1)S(1)} %dynamic-update-slice.1, bf16[1024]{0:T(1024)(128)(2,1)S(1)} %dynamic-update-slice), channel_id=1, replica_groups=mesh['row'=4,'col'=8] {'row','col'}, use_global_device_ids=true, to_apply=%add.1 | all-reduce | flops 2048 | bytes 8192
  56.3 14.0 all-gather.25.cloned.1.call-done
  76.2 52.4 %all-gather.31.cloned.1.call-done = bf16[8192,128]{1,0:T(8,128)(2,1)} async-done(((bf16[256,128]{1,0:T(8,128)(2,1)}), bf16[8192,128]{1,0:T(8,128)(2,1)}) %all-gather.31.cloned.1.call-update) | async-done | bytes 2097168 | tf_op jit(solution)/shard_map/all_gather | solution.py:205
  156.0 37.2 %all-gather.13 = bf16[32,1,256]{2,1,0:T(2,128)(2,1)S(1)} all-gather(bf16[1,1,256]{2,1,0:T(2,128)(2,1)S(1)} %bitcast.446), channel_id=1, replica_groups=mesh['row'=4,'col'=8] {'row','col'}, dimensions={0}, use_global_device_ids=true | all-gather | bytes 16896 | tf_op jit(solution)/shard_map/all_gather | solution.py:209
  201.7 44.2 %all-gather.35.cloned.1.call-done = bf16[8192,128]{1,0:T(8,128)(2,1)} async-done(((bf16[256,128]{1,0:T(8,128)(2,1)}), bf16[8192,128]{1,0:T(8,128)(2,1)}) %all-gather.35.cloned.1.call-update) | async-done | bytes 2097168 | tf_op jit(solution)/shard_map/all_gather | solution.py:206
  250.2 43.7 %all-gather.27.cloned.1.call-done = bf16[2048,1024]{1,0:T(8,128)(2,1)} async-done(((bf16[256,1024]{1,0:T(8,128)(2,1)}), bf16[2048,1024]{1,0:T(8,128)(2,1)}) %all-gather.27.cloned.1.call-update) | async-done | bytes 4194320 | tf_op jit(solution)/shard_map/all_gather | solution.py:235
  315.5 26.3 %all-gather.33.cloned.1.call-done = bf16[2048,1024]{1,0:T(8,128)(2,1)} async-done(((bf16[256,1024]{1,0:T(8,128)(2,1)}), bf16[2048,1024]{1,0:T(8,128)(2,1)}) %all-gather.33.cloned.1.call-update) | async-done | bytes 4194320 | tf_op jit(solution)/shard_map/all_gather | solution.py:236
  363.6 17.9 while.37
  389.4 26.1 %all-to-all-start = ((bf16[8,32,1024]{2,1,0:T(8,128)(2,1)}), bf16[8,32,1024]{2,1,0:T(8,128)(2,1)S(1)}, u32[]{:S(2)}, u32[]{:S(2)}) async-start(bf16[8,32,1024]{2,1,0:T(8,128)(2,1)} %bitcast.41), calls=%async_computation | async-start | bytes 1048576 | tf_op jit(solution)/shard_map/all_to_all | solution.py:254
  479.0 15.3 fusion.117
  494.3 25.5 %all-gather.39.cloned.1.call-done = bf16[1,1,4096,1024]{3,2,1,0:T(8,128)(2,1)} async-done(((bf16[1,1,1024,1024]{3,2,1,0:T(8,128)(2,1)}), bf16[1,1,4096,1024]{3,2,1,0:T(8,128)(2,1)}) %all-gather.39.cloned.1.call-update) | async-done | bytes 8388624 | tf_op jit(solution)/shard_map/all_gather | solution.py:266
  526.5 83.3 %all-gather.41.cloned.1.call-done = bf16[1,1,1024,4096]{3,2,1,0:T(8,128)(2,1)} async-done(((bf16[1,1,1024,1024]{3,2,1,0:T(8,128)(2,1)}), bf16[1,1,1024,4096]{3,2,1,0:T(8,128)(2,1)}) %all-gather.41.cloned.1.call-update) | async-done | bytes 8388624 | tf_op jit(solution)/shard_map/all_gather | solution.py:265
  609.9 15.5 fusion.120
  625.4 73.8 %all-gather.43.cloned.1.call-done = bf16[1,1,4096,1024]{3,2,1,0:T(8,128)(2,1)} async-done(((bf16[1,1,1024,1024]{3,2,1,0:T(8,128)(2,1)}), bf16[1,1,4096,1024]{3,2,1,0:T(8,128)(2,1)}) %all-gather.43.cloned.1.call-update) | async-done | bytes 8388624 | tf_op jit(solution)/shard_map/all_gather | solution.py:266
  714.2 12.2 all-to-all-done.1
  732.7 18.2 all_to_all.20
  778.1 15.2 all-to-all-done.3
  802.4 50.9 %while.39 = (s32[]{:T(128)}, bf16[4,512,2048]{2,1,0:T(8,128)(2,1)}, f32[4,512]{1,0:T(4,128)S(1)}, f32[256]{0:T(256)S(1)}, bf16[4,512,16,64]{1,3,2,0:T(8,128)(2,1...) while((s32[]{:T(128)}, bf16[4,512,2048]{2,1,0:T(8,128)(2,1)}, ...), condition=%wide.region_28.30_spmd, body=%wide.region_25.29_spmd.sunk | while | flops 1100087296 | bytes 86434600 | solution.py:446
  805.3 17.3 conditional.8
  890.3 23.8 %while.38 = (s32[]{:T(128)}, f32[256,16,64]{0,2,1:T(8,128)S(1)}, f32[4,512]{1,0:T(4,128)S(1)}, f32[256]{0:T(256)S(1)}, bf16[4,512,16,64]{1,3,2,0:T(8,128)(2,1)},...) while((s32[]{:T(128)}, f32[256,16,64]{0,2,1:T(8,128)S(1)}, ...), condition=%wide.region_24.26_spmd, body=%wide.region_21.25_spmd.sunk | while | flops 818544640 | bytes 23372532 | solution.py:173
  892.9 13.5 conditional.7
  917.7 74.8 %reduce-scatter.10.cloned.1.call-done = bf16[256,2048]{1,0:T(8,128)(2,1)} async-done(((bf16[2048,2048]{1,0:T(8,128)(2,1)}), bf16[256,2048]{1,0:T(8,128)(2,1)}) %reduce-scatter.10.cloned.1.call-update) | async-done | bytes 1048592 | tf_op jit(solution)/shard_map/reduce_scatter | solution.py:445
  1018.5 17.2 all-reduce.15
  1038.6 43.1 %reduce-scatter.22.cloned.1.call-done = bf16[1024,1024]{1,0:T(8,128)(2,1)} async-done(((bf16[1024,4096]{1,0:T(8,128)(2,1)}), bf16[1024,1024]{1,0:T(8,128)(2,1)}) %reduce-scatter.22.cloned.1.call-update) | async-done | bytes 2097168 | tf_op jit(solution)/shard_map/reduce_scatter | solution.py:323
  1081.7 89.8 %reduce-scatter.20.cloned.1.call-done = bf16[1024,1024]{1,0:T(8,128)(2,1)} async-done(((bf16[1024,4096]{1,0:T(8,128)(2,1)}), bf16[1024,1024]{1,0:T(8,128)(2,1)}) %reduce-scatter.20.cloned.1.call-update) | async-done | bytes 2097168 | tf_op jit(solution)/shard_map/reduce_scatter | solution.py:323
  1177.6 83.2 %reduce-scatter.26.cloned.1.call-done = bf16[1024,1024]{1,0:T(8,128)(2,1)} async-done(((bf16[4096,1024]{1,0:T(8,128)(2,1)}), bf16[1024,1024]{1,0:T(8,128)(2,1)}) %reduce-scatter.26.cloned.1.call-update) | async-done | bytes 2097168 | tf_op jit(solution)/shard_map/reduce_scatter | solution.py:326
  1260.8 89.6 %reduce-scatter.24.cloned.1.call-done = bf16[1024,1024]{1,0:T(8,128)(2,1)} async-done(((bf16[4096,1024]{1,0:T(8,128)(2,1)}), bf16[1024,1024]{1,0:T(8,128)(2,1)}) %reduce-scatter.24.cloned.1.call-update) | async-done | bytes 2097168 | tf_op jit(solution)/shard_map/reduce_scatter | solution.py:326
  1356.7 40.5 %all-reduce.13 = (f32[1024]{0:T(1024)S(1)}, f32[1024]{0:T(1024)S(1)}, f32[32,256]{1,0:T(8,128)S(1)}) all-reduce(f32[1024]{0:T(1024)S(1)} %get-tuple-element.518, f32[1024]{0:T(1024)S(1)} %get-tuple-element.525, f32[32,256]{1,0:T(8,128)S(1)} %bitcast.433), channel_id=16, replica_groups=mesh['row'=4,'col'=8] {'row','col'}, use_global_device_ids=true, to_apply=%region_33.35.clone | all-reduce | flops 10240 | bytes 81920
  1400.3 95.8 %reduce-scatter.18.cloned.1.call-done = f32[256,128]{1,0:T(8,128)} async-done(((f32[8192,128]{1,0:T(8,128)}), f32[256,128]{1,0:T(8,128)}) %reduce-scatter.18.cloned.1.call-update) | async-done | bytes 131088 | tf_op jit(solution)/shard_map/reduce_scatter | solution.py:494
  1496.2 142.2 %reduce-scatter.12.cloned.1.call-done = f32[256,128]{1,0:T(8,128)} async-done(((f32[8192,128]{1,0:T(8,128)}), f32[256,128]{1,0:T(8,128)}) %reduce-scatter.12.cloned.1.call-update) | async-done | bytes 131088 | tf_op jit(solution)/shard_map/reduce_scatter | solution.py:476
  1638.3 142.4 %reduce-scatter.14.cloned.1.call-done = f32[256,128]{1,0:T(8,128)} async-done(((f32[8192,128]{1,0:T(8,128)}), f32[256,128]{1,0:T(8,128)}) %reduce-scatter.14.cloned.1.call-update) | async-done | bytes 131088 | tf_op jit(solution)/shard_map/reduce_scatter | solution.py:482
  1780.8 142.5 %reduce-scatter.16.cloned.1.call-done = f32[256,128]{1,0:T(8,128)} async-done(((f32[8192,128]{1,0:T(8,128)}), f32[256,128]{1,0:T(8,128)}) %reduce-scatter.16.cloned.1.call-update) | async-done | bytes 131088 | tf_op jit(solution)/shard_map/reduce_scatter | solution.py:488
  (395 shorter events, 399.2 us)
Async XLA Ops:
  7.2 63.1 %all-gather.25.cloned.1.call-start = ((), (), s32[]{:S(2)}) async-start(), calls=%async_computation.13 | async-start | bytes 2162688 | tf_op jit(solution)/shard_map/all_gather | solution.py:204
  7.9 120.7 %all-gather.31.cloned.1.call-start = ((), (), s32[]{:S(2)}) async-start(), calls=%async_computation.16 | async-start | bytes 2162688 | tf_op jit(solution)/shard_map/all_gather | solution.py:205
  8.7 187.7 %all-gather.29.cloned.1.call-start = ((), (), s32[]{:S(2)}) async-start(), calls=%async_computation.15 | async-start | bytes 2162688 | tf_op jit(solution)/shard_map/all_gather | solution.py:203
  9.4 236.4 %all-gather.35.cloned.1.call-start = ((), (), s32[]{:S(2)}) async-start(), calls=%async_computation.18 | async-start | bytes 2162688 | tf_op jit(solution)/shard_map/all_gather | solution.py:206
  10.0 283.9 %all-gather.27.cloned.1.call-start = ((), (), s32[]{:S(2)}) async-start(), calls=%async_computation.14 | async-start | bytes 4718592 | tf_op jit(solution)/shard_map/all_gather | solution.py:235
  53.8 145.6 %copy-start.31 = (f32[1024]{0:T(1024)}, f32[1024]{0:T(1024)S(1)}, u32[]{:S(2)}) copy-start(f32[1024]{0:T(1024)S(1)} %convert_element_type.233) | copy-start | bytes 12292
  53.8 145.6 %copy-start.29 = (f32[1024]{0:T(1024)}, f32[1024]{0:T(1024)S(1)}, u32[]{:S(2)}) copy-start(f32[1024]{0:T(1024)S(1)} %convert_element_type.232) | copy-start | bytes 12292
  55.0 144.4 %copy-start.33 = (f32[256]{0:T(256)}, f32[256]{0:T(256)S(1)}, u32[]{:S(2)}) copy-start(f32[256]{0:T(256)S(1)} %broadcast_multiply_fusion.8) | copy-start | bytes 3076
  56.3 143.1 %copy-start.35 = (f32[256]{0:T(256)}, f32[256]{0:T(256)S(1)}, u32[]{:S(2)}) copy-start(f32[256]{0:T(256)S(1)} %add_rsqrt_fusion.2) | copy-start | bytes 3076
  76.1 265.7 %all-gather.33.cloned.1.call-start = ((), (), s32[]{:S(2)}) async-start(), calls=%async_computation.17 | async-start | bytes 4718592 | tf_op jit(solution)/shard_map/all_gather | solution.py:236
  134.5 344.5 %all-gather.37.cloned.1.call-start = ((), (), s32[]{:S(2)}) async-start(), calls=%async_computation.28 | async-start | bytes 10485760 | tf_op jit(solution)/shard_map/all_gather | solution.py:265
  139.3 380.5 %all-gather.39.cloned.1.call-start = ((), (), s32[]{:S(2)}) async-start(), calls=%async_computation.29 | async-start | bytes 10485760 | tf_op jit(solution)/shard_map/all_gather | solution.py:266
  144.0 465.9 %all-gather.41.cloned.1.call-start = ((), (), s32[]{:S(2)}) async-start(), calls=%async_computation.30 | async-start | bytes 10485760 | tf_op jit(solution)/shard_map/all_gather | solution.py:265
  144.7 554.5 %all-gather.43.cloned.1.call-start = ((), (), s32[]{:S(2)}) async-start(), calls=%async_computation.31 | async-start | bytes 10485760 | tf_op jit(solution)/shard_map/all_gather | solution.py:266
  387.3 91.6 %copy-start.2 = (bf16[256,1024]{1,0:T(8,128)(2,1)}, bf16[256,1024]{1,0:T(8,128)(2,1)S(1)}, u32[]{:S(2)}) copy-start(bf16[256,1024]{1,0:T(8,128)(2,1)S(1)} %get-tuple-element.606) | copy-start | bytes 1572868
  389.4 88.6 %all-to-all-start = ((bf16[8,32,1024]{2,1,0:T(8,128)(2,1)}), bf16[8,32,1024]{2,1,0:T(8,128)(2,1)S(1)}, u32[]{:S(2)}, u32[]{:S(2)}) async-start(bf16[8,32,1024]{2,1,0:T(8,128)(2,1)} %bitcast.41), calls=%async_computation | async-start | bytes 1048576 | tf_op jit(solution)/shard_map/all_to_all | solution.py:254
  526.2 235.2 %copy-start.6 = (f32[256,1024]{1,0:T(8,128)}, f32[256,1024]{1,0:T(8,128)S(1)}, u32[]{:S(2)}) copy-start(f32[256,1024]{1,0:T(8,128)S(1)} %get-tuple-element.630) | copy-start | bytes 3145732
  706.4 20.0 %all-to-all-start.1 = ((bf16[8,32,1024]{2,1,0:T(8,128)(2,1)}), bf16[8,32,1024]{2,1,0:T(8,128)(2,1)S(1)}, u32[]{:S(2)}, u32[]{:S(2)}) async-start(bf16[8,32,1024]{2,1,0:T(8,128)(2,1)} %bitcast.55), calls=%async_computation.1 | async-start | bytes 1048576 | tf_op jit(solution)/shard_map/all_to_all | solution.py:287
  774.5 18.8 all-to-all-start.3
  778.0 214.5 %reduce-scatter.10.cloned.1.call-start = ((), (), s32[]{:S(2)}) async-start(), calls=%async_computation.19 | async-start | bytes 9437184 | tf_op jit(solution)/shard_map/reduce_scatter | solution.py:445
  853.3 228.4 %reduce-scatter.22.cloned.1.call-start = ((), (), s32[]{:S(2)}) async-start(), calls=%async_computation.25 | async-start | bytes 10485760 | tf_op jit(solution)/shard_map/reduce_scatter | solution.py:323
  862.1 309.4 %reduce-scatter.20.cloned.1.call-start = ((), (), s32[]{:S(2)}) async-start(), calls=%async_computation.24 | async-start | bytes 10485760 | tf_op jit(solution)/shard_map/reduce_scatter | solution.py:323
  870.4 390.5 %reduce-scatter.26.cloned.1.call-start = ((), (), s32[]{:S(2)}) async-start(), calls=%async_computation.27 | async-start | bytes 10485760 | tf_op jit(solution)/shard_map/reduce_scatter | solution.py:326
  877.6 472.9 %reduce-scatter.24.cloned.1.call-start = ((), (), s32[]{:S(2)}) async-start(), calls=%async_computation.26 | async-start | bytes 10485760 | tf_op jit(solution)/shard_map/reduce_scatter | solution.py:326
  886.0 610.1 %reduce-scatter.18.cloned.1.call-start = ((), (), s32[]{:S(2)}) async-start(), calls=%async_computation.23 | async-start | bytes 4325376 | tf_op jit(solution)/shard_map/reduce_scatter | solution.py:494
  890.0 748.4 %reduce-scatter.12.cloned.1.call-start = ((), (), s32[]{:S(2)}) async-start(), calls=%async_computation.20 | async-start | bytes 4325376 | tf_op jit(solution)/shard_map/reduce_scatter | solution.py:476
  917.7 79.9 %copy-start.30 = (f32[1024]{0:T(1024)S(1)}, f32[1024]{0:T(1024)}, u32[]{:S(2)}) copy-start(f32[1024]{0:T(1024)} %copy-done.29) | copy-start | bytes 12292
  917.7 79.9 %copy-start.32 = (f32[1024]{0:T(1024)S(1)}, f32[1024]{0:T(1024)}, u32[]{:S(2)}) copy-start(f32[1024]{0:T(1024)} %copy-done.31) | copy-start | bytes 12292
  917.7 79.9 %copy-start.34 = (f32[256]{0:T(256)S(1)}, f32[256]{0:T(256)}, u32[]{:S(2)}) copy-start(f32[256]{0:T(256)} %copy-done.33) | copy-start | bytes 3076
  917.7 79.9 %copy-start.36 = (f32[256]{0:T(256)S(1)}, f32[256]{0:T(256)}, u32[]{:S(2)}) copy-start(f32[256]{0:T(256)} %copy-done.35) | copy-start | bytes 3076
  1002.9 777.9 %reduce-scatter.14.cloned.1.call-start = ((), (), s32[]{:S(2)}) async-start(), calls=%async_computation.21 | async-start | bytes 4325376 | tf_op jit(solution)/shard_map/reduce_scatter | solution.py:482
  1008.9 914.4 %reduce-scatter.16.cloned.1.call-start = ((), (), s32[]{:S(2)}) async-start(), calls=%async_computation.22 | async-start | bytes 4325376 | tf_op jit(solution)/shard_map/reduce_scatter | solution.py:488
  (52 other events, 675.7 us)
Sparse Core Ops, SparseCore 0:
  11.0 59.2 all-gather.24
  73.3 55.3 all-gather.30
  131.6 55.4 all-gather.28
  189.9 55.8 all-gather.34
  247.9 45.9 all-gather.26
  295.9 45.8 all-gather.32
  343.7 86.4 all-gather.36
  432.0 87.7 all-gather.38
  522.2 87.6 all-gather.40
  611.6 87.6 all-gather.42
  853.5 139.0 reduce-scatter.9
  996.0 85.6 reduce-scatter.21
  1085.1 86.3 reduce-scatter.19
  1174.4 86.3 reduce-scatter.25
  1264.0 86.3 reduce-scatter.23
  1353.2 142.9 reduce-scatter.17
  1498.9 139.4 reduce-scatter.11
  1641.0 139.7 reduce-scatter.13
  1783.6 139.6 reduce-scatter.15
where the time goes:
time: 1940 us; the launch traced here: 1930 us
  waiting for transfers between devices  1300 us (67%)
  blocking collectives  228 us (12%)
  matrix products  157 us (8%)
  local copies, waits for them, and re-layouts  136 us (7%)
  other arithmetic  42.2 us (2%)
  starting transfers between devices  35.7 us (2%)
    reduce_scatter x2, waiting for transfers between devices, shards(): lax.psum_scatter(part_back.astype(jnp.bfloat16), 'row', scatter_dimension...  173 us
    reduce_scatter x1, waiting for transfers between devices, shards(): lax.psum_scatter(blockify(part_value, row_total, col_total), ('row', 'col...  143 us
    reduce_scatter x1, waiting for transfers between devices, shards(): lax.psum_scatter(blockify(part_key, row_total, col_total), ('row', 'col')...  142 us
    reduce_scatter x1, waiting for transfers between devices, shards(): lax.psum_scatter(blockify(part_query, row_total, col_total), ('row', 'col...  142 us
    reduce_scatter x2, waiting for transfers between devices, shards(): lax.psum_scatter(part_in.astype(jnp.bfloat16), 'row', scatter_dimension=1...  133 us
    unnamed x3, blocking collectives  99.7 us
    all_gather x2, waiting for transfers between devices, shards(): lax.all_gather(w_back[0, sublayer], 'row', axis=0, tiled=True)  99.3 us
    reduce_scatter x1, waiting for transfers between devices, shards(): lax.psum_scatter(blockify(part_output, row_total, col_total), ('row', 'co...  95.8 us
  transfers between devices with their start and end apart: 22, of which 19 were waited for; matrix products, arithmetic and copies ran while one was open for 12% of the time, Pallas kernels for 0%

commit v1 on v0

v1 whole, which is shorter than its diff:
```python
import functools

import jax
import jax.numpy as jnp
from jax import lax
from jax.experimental import pallas as pl
from jax.experimental.pallas import tpu as pltpu
from jax.sharding import PartitionSpec as P

HEADS = 16
EPS = 1e-05
NEG = -1e30
BF = jnp.bfloat16
F32 = jnp.float32
NT = (((1,), (1,)), ((), ()))
NN = (((1,), (0,)), ((), ()))
VMEM_BYTES = 56 * 1024 * 1024


def dot(left, right, dims=NN):
    return lax.dot_general(left, right, dims, preferred_element_type=F32)


def add_low(left, right):
    return (left.astype(F32) + right.astype(F32)).astype(BF)


def send_xor(value, axis, size, mask):
    return lax.ppermute(value, axis, [(i, i ^ mask) for i in range(size)])


def bits_of(size):
    return list(range(size.bit_length() - 1))


def gather_path(value, axis, size, bits):
    held = {0: value}
    for bit in bits:
        held.update({m | (1 << bit): send_xor(v, axis, size, 1 << bit) for m, v in list(held.items())})
    return [held[m] for m in range(size)]


def scatter_path(blocks, axis, size, bits):
    held = dict(enumerate(blocks))
    for bit in bits:
        leaving = {m: v for m, v in held.items() if (m >> bit) & 1}
        held = {m: v for m, v in held.items() if not (m >> bit) & 1}
        for m, v in leaving.items():
            keep = m & ~(1 << bit)
            held[keep] = add_low(held[keep], send_xor(v, axis, size, 1 << bit))
    return held[0]


def dual_gather(value, axis, size):
    half = value.shape[0] // 2
    bits = bits_of(size)
    first = gather_path(value[:half], axis, size, bits)
    second = gather_path(value[half:], axis, size, bits[::-1])
    return jnp.concatenate(first + second)


def dual_scatter(partial, axis, size):
    half = partial.shape[0] // (2 * size)
    pieces = partial.reshape(2 * size, half, partial.shape[1])
    bits = bits_of(size)
    first = scatter_path([pieces[m] for m in range(size)], axis, size, bits)
    second = scatter_path([pieces[size + m] for m in range(size)], axis, size, bits[::-1])
    return jnp.concatenate([first, second])


def direct_gather(value, axis, size):
    return [value] + [send_xor(value, axis, size, m) for m in range(1, size)]


def direct_exchange(blocks, axis, size):
    return [blocks[0]] + [send_xor(blocks[m], axis, size, m) for m in range(1, size)]


def reorder(stacked, mine, size):
    return jnp.concatenate(
        [lax.dynamic_index_in_dim(stacked, mine ^ j, 0, keepdims=True) for j in range(size)]
    )


def swap_core(value, size):
    return send_xor(value, "col", size, 1)


def right_pairs(first, last, size):
    return [(i, i + 2) for i in range(size) if first <= i // 2 <= last]


def left_pairs(first, last, size):
    return [(i, i - 2) for i in range(size) if first <= i // 2 <= last]


def line_order(mine, size):
    chips = size // 2
    return [
        ((mine // 2 + turn) % chips) * 2 + ((mine % 2) ^ core)
        for turn in range(chips)
        for core in range(2)
    ]


def line_gather(value, size):
    chips = size // 2
    right, left = [value], [value]
    for step in range(1, chips):
        from_left = lax.ppermute(right[-1], "col", right_pairs(step - 1, chips - 2, size))
        from_right = lax.ppermute(left[-1], "col", left_pairs(1, chips - step, size))
        from_left, from_right = lax.optimization_barrier((from_left, from_right))
        right.append(from_left)
        left.append(from_right)
    merged = [value] + [left[s] + right[chips - s] for s in range(1, chips)]
    return [v for m in merged for v in (m, swap_core(m, size))]


def line_scatter(blocks, size):
    chips = size // 2
    halves = [
        add_low(blocks[2 * turn], swap_core(blocks[2 * turn + 1], size)) for turn in range(chips)
    ]
    from_left = from_right = None
    for step in range(1, chips):
        to_right = halves[chips - step] if step == 1 else add_low(from_left, halves[chips - step])
        to_left = halves[step] if step == 1 else add_low(from_right, halves[step])
        to_right, to_left = lax.optimization_barrier((to_right, to_left))
        from_left = lax.ppermute(to_right, "col", right_pairs(0, min(step - 1, chips - 2), size))
        from_right = lax.ppermute(to_left, "col", left_pairs(max(chips - step, 1), chips - 1, size))
        from_left, from_right = lax.optimization_barrier((from_left, from_right))
    return halves[0].astype(F32) + from_left.astype(F32) + from_right.astype(F32)


def col_order(mine, size):
    return line_order(mine, size) if size == 8 else [mine ^ m for m in range(size)]


def col_gather(value, size):
    if size == 8:
        return line_gather(value, size)
    return gather_path(value, "col", size, bits_of(size))


def col_scatter(blocks, size):
    if size == 8:
        return line_scatter(blocks, size)
    return scatter_path(blocks, "col", size, bits_of(size)).astype(F32)


def layer_stats(stream):
    center = stream - jnp.mean(stream, axis=-1, keepdims=True)
    inv_root = lax.rsqrt(jnp.mean(center * center, axis=-1, keepdims=True) + EPS)
    return (center * inv_root, inv_root)


def norm_back(grad_normed, unit_rows, inv_root, gain_full):
    grad_unit = grad_normed * gain_full
    mean_first = jnp.mean(grad_unit, axis=-1, keepdims=True)
    mean_second = jnp.mean(grad_unit * unit_rows, axis=-1, keepdims=True)
    return inv_root * (grad_unit - mean_first - unit_rows * mean_second)


def project_kernel(scale, x_ref, gain_ref, shift_ref, wq_ref, wk_ref, wv_ref, normed_ref, q_ref, k_ref, v_ref, kt_ref, vt_ref):
    unit_rows, unused = layer_stats(x_ref[...].astype(F32))
    normed = (unit_rows * gain_ref[...] + shift_ref[...]).astype(BF)
    normed_ref[...] = normed
    q_ref[...] = (dot(normed, wq_ref[...]).astype(BF).astype(F32) * scale).astype(BF)
    keys = dot(normed, wk_ref[...])
    values = dot(normed, wv_ref[...])
    k_ref[...] = keys.astype(BF)
    v_ref[...] = values.astype(BF)
    kt_ref[...] = keys.T.astype(BF)
    vt_ref[...] = values.T.astype(BF)


def project(block, gain, shift, wq, wk, wv, rows, scale):
    width = block.shape[1]
    fw = wq.shape[1]
    fixed = lambda *shape: pl.BlockSpec(shape, lambda i: (0,) * len(shape))
    return pl.pallas_call(
        functools.partial(project_kernel, scale),
        grid=(1,),
        in_specs=[
            fixed(rows, width),
            fixed(1, width),
            fixed(1, width),
            fixed(width, fw),
            fixed(width, fw),
            fixed(width, fw),
        ],
        out_specs=[
            fixed(rows, width),
            fixed(rows, fw),
            fixed(rows, fw),
            fixed(rows, fw),
            fixed(fw, rows),
            fixed(fw, rows),
        ],
        out_shape=[
            jax.ShapeDtypeStruct((rows, width), BF),
            jax.ShapeDtypeStruct((rows, fw), BF),
            jax.ShapeDtypeStruct((rows, fw), BF),
            jax.ShapeDtypeStruct((rows, fw), BF),
            jax.ShapeDtypeStruct((fw, rows), BF),
            jax.ShapeDtypeStruct((fw, rows), BF),
        ],
        cost_estimate=pl.CostEstimate(
            flops=2 * rows * width * fw * 3 + 10 * rows * width,
            bytes_accessed=2 * (2 * rows * width + 3 * width * fw + 5 * rows * fw),
            transcendentals=0,
        ),
        name="project",
    )(block, gain, shift, wq, wk, wv)


def split_lanes(rows, count):
    width = rows.shape[1] // count
    if count == 1:
        return rows
    head_of = lax.broadcasted_iota(jnp.int32, rows.shape, 1) // width
    return jnp.concatenate(
        [jnp.where(head_of == h, rows, jnp.zeros_like(rows)) for h in range(count)], axis=0
    )


def split_rows(cols, count):
    width = cols.shape[0] // count
    if count == 1:
        return cols
    head_of = lax.broadcasted_iota(jnp.int32, cols.shape, 0) // width
    return jnp.concatenate(
        [jnp.where(head_of == h, cols, jnp.zeros_like(cols)) for h in range(count)], axis=1
    )


def attend_kernel(heads, pos_ref, out_ref_index, count_ref, q_ref, k_ref, vt_ref, row_ids_ref, col_ids_ref, ctx_ref, low_ref, lse_ref):
    i = pl.program_id(0)
    queries = split_lanes(q_ref[0], heads)
    rows = q_ref.shape[1]
    fw = q_ref.shape[2]
    head = fw // heads
    row_ids = jnp.concatenate([row_ids_ref[0]] * heads, axis=1)

    def step(j, state):
        run_max, run_sum, held = state
        at = pos_ref[j]
        scores = dot(k_ref[at], queries, NT)
        scores = jnp.where(col_ids_ref[at] <= row_ids, scores, NEG)
        new_max = jnp.maximum(run_max, jnp.max(scores, axis=0, keepdims=True))
        weights = jnp.exp(scores - new_max)
        factor = jnp.exp(run_max - new_max)
        new_sum = run_sum * factor + jnp.sum(weights, axis=0, keepdims=True)
        low = weights.astype(BF)
        values = vt_ref[at]
        new_held = tuple(
            held[h] * factor[:, h * rows : (h + 1) * rows]
            + dot(values[h * head : (h + 1) * head], low[:, h * rows : (h + 1) * rows])
            for h in range(heads)
        )
        return new_max, new_sum, new_held

    start = (
        jnp.full((1, heads * rows), NEG, F32),
        jnp.zeros((1, heads * rows), F32),
        tuple(jnp.zeros((head, rows), F32) for h in range(heads)),
    )
    run_max, run_sum, held = lax.fori_loop(0, count_ref[i], step, start)
    for h in range(heads):
        result = held[h] / run_sum[:, h * rows : (h + 1) * rows]
        ctx_ref[0, h * head : (h + 1) * head, :] = result
        low_ref[0, h * head : (h + 1) * head, :] = result.astype(BF)
    lse_ref[0] = run_max + jnp.log(run_sum)


def attend(q, k, vt, row_ids, col_ids, pos, rel, counts, heads):
    total, rows, fw = q.shape
    whole = lambda *shape: pl.BlockSpec(shape, lambda i, pos, rel, counts: (0,) * len(shape))
    pairs = total * rows * total * rows * heads
    return pl.pallas_call(
        functools.partial(attend_kernel, heads),
        grid_spec=pltpu.PrefetchScalarGridSpec(
            num_scalar_prefetch=3,
            grid=(total,),
            in_specs=[
                pl.BlockSpec((1, rows, fw), lambda i, pos, rel, counts: (pos[i], 0, 0)),
                whole(total, rows, fw),
                whole(total, fw, rows),
                pl.BlockSpec((1, 1, rows), lambda i, pos, rel, counts: (pos[i], 0, 0)),
                whole(total, rows, 1),
            ],
            out_specs=[
                pl.BlockSpec((1, fw, rows), lambda i, pos, rel, counts: (i, 0, 0)),
                pl.BlockSpec((1, fw, rows), lambda i, pos, rel, counts: (rel[i], 0, 0)),
                pl.BlockSpec((1, 1, heads * rows), lambda i, pos, rel, counts: (i, 0, 0)),
            ],
        ),
        out_shape=[
            jax.ShapeDtypeStruct((total, fw, rows), F32),
            jax.ShapeDtypeStruct((total, fw, rows), BF),
            jax.ShapeDtypeStruct((total, 1, heads * rows), F32),
        ],
        compiler_params=pltpu.CompilerParams(vmem_limit_bytes=VMEM_BYTES),
        cost_estimate=pl.CostEstimate(
            flops=2 * pairs * 128, bytes_accessed=10 * total * rows * fw, transcendentals=pairs // 2
        ),
        name="attend",
    )(pos, rel, counts, q, k, vt, row_ids, col_ids)


def attend_back_kernel(
    heads, scale, pos_ref, rel_ref, first_ref,
    q_ref, k_ref, v_ref, kt_ref, ctx_ref, grad_ref, lse_ref, row_ids_ref, col_ids_ref,
    dq_ref, dk_ref, dv_ref, q_all, grad_all, delta_all, dq_all,
):
    j = pl.program_id(0)
    total, rows, fw = q_ref.shape
    head = fw // heads

    @pl.when(j == 0)
    def prepare():
        def one(i, unused):
            at = pos_ref[i]
            q_all[i] = split_lanes(q_ref[at], heads)
            grad = grad_ref[rel_ref[i]]
            grad_all[i] = split_rows(grad, heads)
            product = grad.astype(F32) * ctx_ref[i]
            delta_all[i] = jnp.concatenate(
                [
                    jnp.sum(product[h * head : (h + 1) * head], axis=0, keepdims=True)
                    for h in range(heads)
                ],
                axis=1,
            )
            dq_all[i] = jnp.zeros((fw, rows), F32)
            return unused

        lax.fori_loop(0, total, one, 0)

    at_key = pos_ref[j]
    keys = k_ref[at_key]
    values = v_ref[at_key]
    keys_t = kt_ref[at_key]
    col_ids = col_ids_ref[at_key]

    def step(i, state):
        dk, dv = state
        queries = q_all[i]
        grads = grad_all[i]
        row_ids = jnp.concatenate([row_ids_ref[pos_ref[i]]] * heads, axis=1)
        scores = dot(keys, queries, NT)
        probs = jnp.exp(jnp.where(col_ids <= row_ids, scores - lse_ref[i], NEG))
        grad_probs = dot(values, grads)
        grad_scores = (probs * (grad_probs - delta_all[i])).astype(BF)
        dv = dv + dot(probs.astype(BF), grads, NT)
        dk = dk + dot(grad_scores, queries)
        for h in range(heads):
            dq_all[i, h * head : (h + 1) * head, :] += dot(
                keys_t[h * head : (h + 1) * head], grad_scores[:, h * rows : (h + 1) * rows]
            )
        return dk, dv

    zero = jnp.zeros((rows, fw), F32)
    dk, dv = lax.fori_loop(first_ref[j], total, step, (zero, zero))
    dk_ref[0] = dk.astype(BF)
    dv_ref[0] = dv.astype(BF)

    @pl.when(j == total - 1)
    def finish():
        def one(i, unused):
            dq_ref[pos_ref[i]] = (dq_all[i] * scale).T.astype(BF)
            return unused

        lax.fori_loop(0, total, one, 0)


def attend_back(q, k, v, kt, ctx, grad, lse, row_ids, col_ids, pos, rel, first, heads, scale):
    total, rows, fw = q.shape
    whole = lambda *shape: pl.BlockSpec(shape, lambda j, pos, rel, first: (0,) * len(shape))
    at_pos = pl.BlockSpec((1, rows, fw), lambda j, pos, rel, first: (pos[j], 0, 0))
    pairs = total * rows * total * rows * heads
    return pl.pallas_call(
        functools.partial(attend_back_kernel, heads, scale),
        grid_spec=pltpu.PrefetchScalarGridSpec(
            num_scalar_prefetch=3,
            grid=(total,),
            in_specs=[
                whole(total, rows, fw),
                whole(total, rows, fw),
                whole(total, rows, fw),
                whole(total, fw, rows),
                whole(total, fw, rows),
                whole(total, fw, rows),
                whole(total, 1, heads * rows),
                whole(total, 1, rows),
                whole(total, rows, 1),
            ],
            out_specs=[whole(total, rows, fw), at_pos, at_pos],
            scratch_shapes=[
                pltpu.VMEM((total, heads * rows, fw), BF),
                pltpu.VMEM((total, fw, heads * rows), BF),
                pltpu.VMEM((total, 1, heads * rows), F32),
                pltpu.VMEM((total, fw, rows), F32),
            ],
        ),
        out_shape=[jax.ShapeDtypeStruct((total, rows, fw), BF)] * 3,
        compiler_params=pltpu.CompilerParams(vmem_limit_bytes=VMEM_BYTES),
        cost_estimate=pl.CostEstimate(
            flops=5 * pairs * 128, bytes_accessed=20 * total * rows * fw, transcendentals=pairs // 2
        ),
        name="attend_back",
    )(pos, rel, first, q, k, v, kt, ctx, grad, lse, row_ids, col_ids)


def gelu_slope(pre_act):
    return (
        0.5 * (1.0 + lax.erf(pre_act * 0.7071067811865476))
        + pre_act * jnp.exp(-0.5 * pre_act * pre_act) * 0.3989422804014327
    )


def shards(
    tokens,
    block_ids,
    expert_ids,
    cotangent,
    norm_gain,
    norm_shift,
    w_query,
    w_key,
    w_value,
    w_output,
    centroids,
    expert_gain,
    expert_shift,
    w_in,
    b_in,
    w_back,
    b_back,
):
    rows_n = lax.axis_size("row")
    cols_n = lax.axis_size("col")
    r = lax.axis_index("row")
    c = lax.axis_index("col")
    tok, width = tokens.shape
    fw = width // cols_n
    heads = HEADS // cols_n
    scale = float(width // HEADS) ** (-0.5)
    part = width // rows_n
    own = norm_gain.shape[0]
    slot = tok // cols_n

    packet = jnp.concatenate([norm_gain, norm_shift, centroids[0]])[None]
    packet = jnp.concatenate(direct_gather(packet, "row", rows_n))[None]
    packet = reorder(jnp.concatenate(direct_gather(packet, "col", cols_n)), c, cols_n)
    packet = reorder(packet.transpose(1, 0, 2), r, rows_n)
    gain_attn = packet[:, :, :own].reshape(1, width).astype(F32)
    shift_attn = packet[:, :, own : 2 * own].reshape(1, width).astype(F32)
    full_centroids = packet[:, :, 2 * own :].transpose(1, 0, 2).reshape(cols_n, width)
    experts = jnp.concatenate([expert_gain[0], expert_shift[0], b_back[0]])
    experts = jnp.stack(direct_gather(experts, "row", rows_n))
    experts = reorder(experts, r, rows_n).transpose(1, 0, 2).reshape(6, width).astype(F32)

    ids = jnp.pad(block_ids.astype(BF), ((0, 15), (0, width - tok)))
    blocks = col_gather(jnp.concatenate([tokens, ids]), cols_n)
    order = jnp.stack(col_order(c, cols_n))
    w_cat = jnp.concatenate([w_query, w_key, w_value], axis=1)
    w_cat = jnp.stack(direct_gather(w_cat, "row", rows_n))
    w_cat = reorder(w_cat, r, rows_n).reshape(width, 3 * fw)
    wq, wk, wv = w_cat[:, :fw], w_cat[:, fw : 2 * fw], w_cat[:, 2 * fw :]
    projected = [project(b, gain_attn, shift_attn, wq, wk, wv, tok, scale) for b in blocks]
    normed, q, k, v, kt, vt = [jnp.stack([p[n] for p in projected]) for n in range(6)]
    row_ids = jnp.stack([b[tok, :tok] for b in blocks]).astype(F32)
    pos = jnp.zeros((cols_n,), jnp.int32).at[order].set(jnp.arange(cols_n, dtype=jnp.int32))
    rel = jnp.arange(cols_n, dtype=jnp.int32) ^ c
    lowest = row_ids[:, 0][pos]
    highest = row_ids[:, -1][pos]
    counts = jnp.sum((lowest[None, :] <= highest[:, None]).astype(jnp.int32), axis=1)
    first = jnp.sum((highest[None, :] < lowest[:, None]).astype(jnp.int32), axis=1)
    col_ids = row_ids[:, :, None]
    row_ids = row_ids[:, None, :]

    pieces = direct_gather(w_output, "row", rows_n)
    pieces = jnp.stack(pieces)
    pieces = reorder(pieces, r, rows_n).reshape(width, fw)
    full_output = jnp.stack(direct_gather(pieces, "col", cols_n))
    full_output = reorder(full_output, c, cols_n)
    full_output = full_output.reshape(cols_n, cols_n, fw, fw).transpose(1, 2, 0, 3)
    full_output = full_output.reshape(cols_n, fw, width)
    full_output = reorder(full_output, c, cols_n).reshape(width, width)

    ctx, ctx_low, lse = attend(q, k, vt, row_ids, col_ids, pos, rel, counts, heads)
    ctx_mine = jnp.concatenate(direct_exchange([ctx_low[m] for m in range(cols_n)], "col", cols_n))
    inputs = tokens.astype(F32)
    residual = inputs + lax.dot_general(
        ctx_mine, full_output, (((0,), (0,)), ((), ())), preferred_element_type=F32
    )
    shared = residual.astype(BF)
    shared_full = shared.astype(F32)

    onehot = expert_ids[:, None] == jnp.arange(cols_n, dtype=jnp.int32)[None, :]
    onehot_low = onehot.astype(BF)
    below = (jnp.arange(tok)[:, None] > jnp.arange(tok)[None, :]).astype(BF)
    before = dot(below, onehot_low)
    rank = jnp.sum(jnp.where(onehot, before, 0.0), axis=1).astype(jnp.int32)
    place = (expert_ids ^ c) * slot + rank
    route = (jnp.arange(tok, dtype=jnp.int32)[:, None] == place[None, :]).astype(BF)
    unroute = (place[:, None] == jnp.arange(tok, dtype=jnp.int32)[None, :]).astype(BF)
    cent_rows = dot(onehot_low, full_centroids)
    gate = jax.nn.sigmoid(jnp.sum(shared_full * cent_rows, axis=1, keepdims=True))
    grad_out = cotangent.astype(F32)
    grad_back = (grad_out * gate).astype(BF)

    def to_experts(rows):
        moved = dot(route, rows).astype(BF).reshape(cols_n, slot, width)
        return jnp.concatenate(direct_exchange([moved[m] for m in range(cols_n)], "col", cols_n))

    def from_experts(rows):
        moved = rows.reshape(cols_n, slot, width)
        back = direct_exchange([moved[m] for m in range(cols_n)], "col", cols_n)
        return dot(unroute, jnp.concatenate(back))

    stream = to_experts(shared).astype(F32)
    grad_stream = to_experts(grad_back).astype(F32)

    stored = []
    for sub in range(2):
        unit_rows, inv_root = layer_stats(stream)
        own_normed = (unit_rows * experts[sub] + experts[2 + sub]).astype(BF)
        normed_all = dual_gather(own_normed, "row", rows_n)
        pre_act = dot(normed_all, w_in[0, sub]) + b_in[0, sub].astype(F32)
        hidden = jax.nn.gelu(pre_act, approximate=False).astype(BF)
        branch = dual_scatter(dot(hidden, w_back[0, sub]).astype(BF), "row", rows_n)
        stored.append((unit_rows, inv_root, normed_all, pre_act, hidden))
        stream = stream + branch.astype(F32) + experts[4 + sub]
    back_vals = from_experts(stream.astype(BF))
    output = (residual + gate * back_vals).astype(BF)
    grad_logit = jnp.sum(grad_out * back_vals, axis=1, keepdims=True) * gate * (1.0 - gate)

    grads_in, grads_back, grads_bias, small_parts = [None] * 2, [None] * 2, [None] * 2, [None] * 6
    for sub in (1, 0):
        unit_rows, inv_root, normed_all, pre_act, hidden = stored[sub]
        small_parts[4 + sub] = jnp.sum(grad_stream, axis=0)
        grad_branch = dual_gather(grad_stream.astype(BF), "row", rows_n)
        grads_back[sub] = lax.dot_general(
            hidden, grad_branch, (((0,), (0,)), ((), ())), preferred_element_type=F32
        )
        grad_pre_full = dot(grad_branch, w_back[0, sub], NT) * gelu_slope(pre_act)
        grad_pre = grad_pre_full.astype(BF)
        grads_bias[sub] = jnp.sum(grad_pre.astype(F32), axis=0)
        grads_in[sub] = lax.dot_general(
            normed_all, grad_pre, (((0,), (0,)), ((), ())), preferred_element_type=F32
        )
        grad_normed = dual_scatter(dot(grad_pre, w_in[0, sub], NT).astype(BF), "row", rows_n)
        grad_normed = grad_normed.astype(F32)
        small_parts[sub] = jnp.sum(grad_normed * unit_rows, axis=0)
        small_parts[2 + sub] = jnp.sum(grad_normed, axis=0)
        grad_stream = grad_stream + norm_back(grad_normed, unit_rows, inv_root, experts[sub])

    grad_shared = from_experts(grad_stream.astype(BF)) + grad_logit * cent_rows
    grad_residual = grad_out + grad_shared
    part_cent = lax.dot_general(
        onehot.astype(F32),
        grad_logit * shared_full,
        (((0,), (0,)), ((), ())),
        precision=lax.Precision.HIGHEST,
        preferred_element_type=F32,
    )
    grad_attended = grad_residual.astype(BF)

    grad_ctx = dot(full_output, grad_attended, NT).astype(BF).reshape(cols_n, fw, tok)
    grad_ctx = jnp.stack(direct_exchange([grad_ctx[m] for m in range(cols_n)], "col", cols_n))
    dq, dk, dv = attend_back(
        q, k, v, kt, ctx, grad_ctx, lse, row_ids, col_ids, pos, rel, first, heads, scale
    )
    dqkv = jnp.concatenate([dq, dk, dv], axis=2)
    partial = lax.dot_general(
        dqkv, w_cat, (((2,), (1,)), ((), ())), preferred_element_type=F32
    ).astype(BF)
    grad_normed_attn = col_scatter([partial[m] for m in range(cols_n)], cols_n)
    unit_attn, inv_attn = layer_stats(inputs)
    tokens_grad = grad_residual + norm_back(grad_normed_attn, unit_attn, inv_attn, gain_attn)
    part_gain = jnp.sum(grad_normed_attn * unit_attn, axis=0)
    part_shift = jnp.sum(grad_normed_attn, axis=0)

    part_qkv = lax.dot_general(
        normed.reshape(cols_n * tok, width),
        dqkv.reshape(cols_n * tok, 3 * fw),
        (((0,), (0,)), ((), ())),
        preferred_element_type=F32,
    )
    part_qkv = reorder(part_qkv.astype(BF).reshape(rows_n, part, 3 * fw), r, rows_n)
    part_qkv = direct_exchange([part_qkv[m] for m in range(rows_n)], "row", rows_n)
    grad_qkv = sum(p.astype(F32) for p in part_qkv)

    part_output = dot(ctx_mine, grad_attended).astype(BF).reshape(cols_n, fw, width)
    part_output = reorder(part_output, c, cols_n).reshape(rows_n, part, cols_n, fw)
    part_output = reorder(part_output.transpose(2, 0, 1, 3), c, cols_n)
    part_output = direct_exchange([part_output[m] for m in range(cols_n)], "col", cols_n)
    part_output = sum(p.astype(F32) for p in part_output).astype(BF)
    part_output = reorder(part_output, r, rows_n)
    part_output = direct_exchange([part_output[m] for m in range(rows_n)], "row", rows_n)
    grad_output = sum(p.astype(F32) for p in part_output)

    all_rows = jnp.concatenate(
        [
            part_gain.reshape(rows_n, cols_n, own),
            part_shift.reshape(rows_n, cols_n, own),
            part_cent.reshape(cols_n, rows_n, part).transpose(1, 0, 2),
        ],
        axis=2,
    ).reshape(rows_n, cols_n * (2 * own + part))
    expert_rows = jnp.stack(small_parts).reshape(6, rows_n, part).transpose(1, 0, 2)
    packed = jnp.concatenate([all_rows, expert_rows.reshape(rows_n, 6 * part)], axis=1)[:, None]
    packed = reorder(packed, r, rows_n)
    packed = sum(direct_exchange([packed[m] for m in range(rows_n)], "row", rows_n))
    expert_sums = packed[0, cols_n * (2 * own + part) :].reshape(3, 2, part)
    packed = packed[0, : cols_n * (2 * own + part)].reshape(cols_n, 1, 2 * own + part)
    packed = reorder(packed, c, cols_n)
    packed = sum(direct_exchange([packed[m] for m in range(cols_n)], "col", cols_n))[0]

    return (
        output,
        tokens_grad,
        packed[:own],
        packed[own : 2 * own],
        grad_qkv[:, :fw],
        grad_qkv[:, fw : 2 * fw],
        grad_qkv[:, 2 * fw :],
        grad_output,
        packed[None, 2 * own :],
        expert_sums[None, 0],
        expert_sums[None, 1],
        jnp.stack(grads_in)[None],
        jnp.stack(grads_bias)[None],
        jnp.stack(grads_back)[None],
        expert_sums[None, 2],
    )


def solution(mesh):
    placed = (
        P(("row", "col"), None),
        P("row", "col"),
        P(("row", "col")),
        P(("row", "col"), None),
        P(("row", "col")),
        P(("row", "col")),
        P("row", "col"),
        P("row", "col"),
        P("row", "col"),
        P("row", "col"),
        P("col", "row"),
        P("col", None, "row"),
        P("col", None, "row"),
        P("col", None, None, "row"),
        P("col", None, "row"),
        P("col", None, "row", None),
        P("col", None, "row"),
    )
    return jax.shard_map(
        shards,
        mesh=mesh,
        in_specs=placed,
        out_specs=(
            P(("row", "col"), None),
            P(("row", "col"), None),
            P(("row", "col")),
            P(("row", "col")),
            P("row", "col"),
            P("row", "col"),
            P("row", "col"),
            P("row", "col"),
            P("col", "row"),
            P("col", None, "row"),
            P("col", None, "row"),
            P("col", None, None, "row"),
            P("col", None, "row"),
            P("col", None, "row", None),
            P("col", None, "row"),
        ),
        check_vma=False,
    )
```

time: 1940 us -> 744 us (0.38)
  waiting for transfers between devices: 1300 us -> 291 us
  blocking collectives: 228 us -> 0 us
  starting transfers between devices: 35.7 us -> 186 us
  matrix products: 157 us -> 66.6 us
  local copies, waits for them, and re-layouts: 136 us -> 75.6 us
  Pallas kernels: 0 us -> 55.6 us
    reduce_scatter x9 -> x0, waiting for transfers between devices: 903 us -> none  [the longest x2 173 us: shards(): lax.psum_scatter(part_back.astype(jnp.bfloat16), 'row', scatter_dimension...]
    all_gather x10 -> x0, waiting for transfers between devices: 363 us -> none  [the longest x2 99.3 us: shards(): lax.all_gather(w_back[0, sublayer], 'row', axis=0, tiled=True)]
    ppermute x0 -> x159, waiting for transfers between devices: none -> 291 us  [the longest x147 232 us: send_xor(): return lax.ppermute(value, axis, [(i, i ^ mask) for i in range(size)])]
    ppermute x0 -> x159, starting transfers between devices: none -> 186 us  [the longest x147 162 us: send_xor(): return lax.ppermute(value, axis, [(i, i ^ mask) for i in range(size)])]
    all_gather x10 -> x0, blocking collectives: 110 us -> none  [the longest x1 37.2 us: shards(): lax.all_gather(centroids, ('row', 'col'), axis=0, tiled=True)]
    unnamed x3 -> x0, blocking collectives: 99.7 us -> none
    dot_general x33 -> x24, matrix products: 157 us -> 66.6 us  [the longest x16 50.8 us: dot(): return lax.dot_general(left, right, dims, preferred_element_type=F32)]
    pallas_call x0 -> x3, Pallas kernels: none -> 55.6 us  [the longest x1 27.5 us: attend_back(): pl.pallas_call(functools.partial(attend_back_kernel, heads, scale), grid_...]
  transfers between devices with their start and end apart: 22 -> 159, of which waited for: 19 -> 73; matrix products, arithmetic and copies ran while one was open for 12% -> 13% of each run, Pallas kernels for 0% -> 0%
where the time goes in v1:
time: 744 us; the launch traced here: 736 us
  waiting for transfers between devices  291 us (39%)
  starting transfers between devices  186 us (25%)
  local copies, waits for them, and re-layouts  75.6 us (10%)
  matrix products  66.6 us (9%)
  other arithmetic  57.5 us (8%)
  Pallas kernels  55.6 us (7%)
    ppermute x147, waiting for transfers between devices, send_xor(): return lax.ppermute(value, axis, [(i, i ^ mask) for i in range(size)])  232 us
    ppermute x147, starting transfers between devices, send_xor(): return lax.ppermute(value, axis, [(i, i ^ mask) for i in range(size)])  162 us
    dot_general x16, matrix products, dot(): return lax.dot_general(left, right, dims, preferred_element_type=F32)  50.8 us
    unnamed x330, local copies, waits for them, and re-layouts  44.5 us
    ppermute x3, waiting for transfers between devices, line_gather(): lax.ppermute(left[-1], 'col', left_pairs(1, chips - step, size))  33.2 us
    pallas_call x1, Pallas kernels, attend_back(): pl.pallas_call(functools.partial(attend_back_kernel, heads, scale), grid_...  27.5 us
    pallas_call x1, Pallas kernels, attend(): pl.pallas_call(functools.partial(attend_kernel, heads), grid_spec=pltpu.P...  25.3 us
    ppermute x3, waiting for transfers between devices, line_scatter(): lax.ppermute(to_right, 'col', right_pairs(0, min(step - 1, chips - 2), si...  21.7 us
  transfers between devices with their start and end apart: 159, of which 73 were waited for; matrix products, arithmetic and copies ran while one was open for 13% of the time, Pallas kernels for 0%

profile of v1, /device:TPU:0, one launch (start us, length us, event | category | flops | bytes accessed | tf_op | source)
XLA Modules:
  0.0 736.2 jit_solution(7760141872650969637)
XLA Ops:
  3.1 5.3 collective-permute-start.1
  50.7 4.8 collective-permute-done.19
  61.3 5.0 collective-permute-done.22
  86.2 7.2 collective-permute-done.35
  93.5 12.6 %collective-permute-done.36 = bf16[1024,128]{1,0:T(8,128)(2,1)S(1)} collective-permute-done((bf16[1024,128]{1,0:T(8,128)(2,1)S(1)}, bf16[1024,128]{1,0:T(8,128)(2,1)S(1)}, u32[]{:S(2)}, u32[]{:S(2)}) %collective-permute-start.36) | collective-permute-done | bytes 262176 | tf_op jit(solution)/shard_map/ppermute | solution.py:29
  110.7 5.5 collective-permute-start.39
  116.3 4.9 collective-permute-done.39
  142.5 20.7 %collective-permute-done.4 = bf16[272,1024]{1,0:T(8,128)(2,1)} collective-permute-done((bf16[272,1024]{1,0:T(8,128)(2,1)}, bf16[272,1024]{1,0:T(8,128)(2,1)}, u32[]{:S(2)}, u32[]{:S(2)}) %collective-permute-start.4) | collective-permute-done | bytes 557088 | tf_op jit(solution)/shard_map/ppermute | solution.py:111
  168.2 12.5 %collective-permute-done.6 = bf16[272,1024]{1,0:T(8,128)(2,1)} collective-permute-done((bf16[272,1024]{1,0:T(8,128)(2,1)}, bf16[272,1024]{1,0:T(8,128)(2,1)}, u32[]{:S(2)}, u32[]{:S(2)}) %collective-permute-start.6) | collective-permute-done | bytes 557088 | tf_op jit(solution)/shard_map/ppermute | solution.py:111
  216.6 25.3 %attend.1 = (f32[8,128,256]{2,1,0:T(8,128)}, bf16[8,128,256]{2,1,0:T(8,128)(2,1)}, f32[8,1,512]{2,1,0:T(1,128)}) custom-call(s32[8]{0:T(128)} %copy-done.79, s32[8]{0:T(128)} %iota_xor_fusion.out_ref_index.rel_ref, s32[8]{0:T(128)} %get-tuple-element.261.count_ref, bf16[8,256,128]{2,1,0:T(8,128)(2,1)} %get-tuple-element.233.q_ref, ...), custom_call_target="tpu_custom_call" | custom-call | flops 2147483648 | bytes 2621440 | tf_op jit(solution)/shard_map/attend/pallas_call | solution.py:280
  269.4 5.9 collective-permute-done.44
  280.1 5.5 collective-permute-done.50
  302.7 14.5 %fusion.2 = (bf16[1024,1024]{1,0:T(8,128)(2,1)S(1)}, f32[1024,1024]{1,0:T(8,128)}) fusion(f32[1024]{0:T(1024)S(1)} %bitcast.511, bf16[1024,1024]{1,0:T(8,128)(2,1)} %constant_dynamic-update-slice_fusion.99, bf16[1,2,1024,1024]{3,2,1,0:T(8,128)(2,1)} %param.30), kind=kOutput, calls=%fused_computation.11 | convolution fusion | flops 2216689664 | bytes 10489856 | tf_op jit(solution)/shard_map/dot_general | solution.py:21
  323.3 5.7 collective-permute-done.57
  332.6 4.8 collective-permute-done.58
  340.2 6.4 collective-permute-done.61
  351.0 6.1 collective-permute-done.62
  367.6 11.9 %fusion.5 = (bf16[1024,1024]{1,0:T(8,128)(2,1)S(1)}, f32[1024,1024]{1,0:T(8,128)S(1)}) fusion(f32[1024]{0:T(1024)S(1)} %bitcast.513, bf16[1024,1024]{1,0:T(8,128)(2,1)S(1)} %constant_dynamic-update-slice_fusion.107, bf16[1,2,1024,1024]{3,2,1,0:T(8,128)(2,1)S(1)} %copy-done.78), kind=kOutput, calls=%fused_computation.14 | convolution fusion | flops 2216689664 | bytes 10489856 | tf_op jit(solution)/shard_map/dot_general | solution.py:21
  385.0 5.3 collective-permute-done.69
  415.2 6.3 collective-permute-done.78
  439.3 5.2 collective-permute-done.89
  452.3 6.1 collective-permute-done.92
  459.7 5.8 collective-permute-done.93
  474.9 6.6 collective-permute-done.95
  484.2 5.1 collective-permute-done.96
  492.3 5.7 collective-permute-done.99
  584.2 5.6 collective-permute-done.123
  590.6 27.5 %attend_back.1 = (bf16[8,256,128]{2,1,0:T(8,128)(2,1)}, bf16[8,256,128]{2,1,0:T(8,128)(2,1)}, bf16[8,256,128]{2,1,0:T(8,128)(2,1)}) custom-call(s32[8]{0:T(128)} %copy-done.79, s32[8]{0:T(128)} %iota_xor_fusion.out_ref_index.rel_ref, s32[8]{0:T(128)} %get-tuple-element.260.first_ref, bf16[8,256,128]{2,1,0:T(8,128)(2,1)} %get-tuple-element.233.q_ref, ...), custom_call_target="tpu_custom_call" | custom-call | flops 5368709120 | bytes 5242880 | tf_op jit(solution)/shard_map/attend_back/pallas_call | solution.py:382
  624.5 5.2 constant_dynamic-slice_fusion.6
  641.1 13.9 %collective-permute-done.129 = bf16[256,1024]{1,0:T(8,128)(2,1)S(1)} collective-permute-done((bf16[256,1024]{1,0:T(8,128)(2,1)S(1)}, bf16[256,1024]{1,0:T(8,128)(2,1)S(1)}, u32[]{:S(2)}, u32[]{:S(2)}) %collective-permute-start.129) | collective-permute-done | bytes 524320 | tf_op jit(solution)/shard_map/ppermute | solution.py:129
  660.5 15.3 %collective-permute-done.153 = bf16[4,256,128]{2,1,0:T(8,128)(2,1)S(1)} collective-permute-done((bf16[4,256,128]{2,1,0:T(8,128)(2,1)S(1)}, bf16[4,256,128]{2,1,0:T(8,128)(2,1)S(1)}, u32[]{:S(2)}, u32[]{:S(2)}) %collective-permute-start.153) | collective-permute-done | bytes 262176 | tf_op jit(solution)/shard_map/ppermute | solution.py:29
  694.9 5.6 collective-permute-start.134
  (825 shorter events, 448.8 us)
Async XLA Ops:
  2.6 135.2 %collective-permute-start = (bf16[272,1024]{1,0:T(8,128)(2,1)S(1)}, bf16[272,1024]{1,0:T(8,128)(2,1)}, u32[]{:S(2)}, u32[]{:S(2)}) collective-permute-start(bf16[272,1024]{1,0:T(8,128)(2,1)S(1)} %fusion.113.x_ref), channel_id=1, source_target_pairs={{0,1},{1,0},{2,3},{3,2},{4,5},{5,4},{6,7},{7,6},{8,9},{9,8},{10,11... | collective-permute-start | bytes 1671176 | tf_op jit(solution)/shard_map/ppermute | solution.py:29
  3.1 132.7 %collective-permute-start.1 = (bf16[272,1024]{1,0:T(8,128)(2,1)S(1)}, bf16[272,1024]{1,0:T(8,128)(2,1)}, u32[]{:S(2)}, u32[]{:S(2)}) collective-permute-start(bf16[272,1024]{1,0:T(8,128)(2,1)S(1)} %fusion.113.x_ref), channel_id=1, source_target_pairs={{0,2},{1,3},{2,4},{3,5},{4,6},{5,7},{8,10},{9,11},{10,12},{11,13},... | collective-permute-start | bytes 1671176 | tf_op jit(solution)/shard_map/ppermute | solution.py:110
  26.1 31.6 %collective-permute-start.32 = (bf16[256,128]{1,0:T(8,128)(2,1)S(1)}, bf16[256,128]{1,0:T(8,128)(2,1)S(1)}, u32[]{:S(2)}, u32[]{:S(2)}) collective-permute-start(bf16[256,128]{1,0:T(8,128)(2,1)S(1)} %copy-done.48), channel_id=1, source_target_pairs={{0,24},{8,16},{16,8},{24,0},{1,25},{9,17},{17,9},{25,1},{2,26},{10... | collective-permute-start | bytes 196616 | tf_op jit(solution)/shard_map/ppermute | solution.py:29
  28.5 31.6 %collective-permute-start.31 = (bf16[256,128]{1,0:T(8,128)(2,1)S(1)}, bf16[256,128]{1,0:T(8,128)(2,1)S(1)}, u32[]{:S(2)}, u32[]{:S(2)}) collective-permute-start(bf16[256,128]{1,0:T(8,128)(2,1)S(1)} %copy-done.48), channel_id=1, source_target_pairs={{0,16},{8,24},{16,0},{24,8},{1,17},{9,25},{17,1},{25,9},{2,18},{10... | collective-permute-start | bytes 196616 | tf_op jit(solution)/shard_map/ppermute | solution.py:29
  66.3 69.5 %collective-permute-start.2 = (bf16[272,1024]{1,0:T(8,128)(2,1)S(1)}, bf16[272,1024]{1,0:T(8,128)(2,1)}, u32[]{:S(2)}, u32[]{:S(2)}) collective-permute-start(bf16[272,1024]{1,0:T(8,128)(2,1)S(1)} %fusion.113.x_ref), channel_id=1, source_target_pairs={{2,0},{3,1},{4,2},{5,3},{6,4},{7,5},{10,8},{11,9},{12,10},{13,11},... | collective-permute-start | bytes 1671176 | tf_op jit(solution)/shard_map/ppermute | solution.py:111
  67.9 12.8 %collective-permute-start.33 = (bf16[1024,128]{1,0:T(8,128)(2,1)S(1)}, bf16[1024,128]{1,0:T(8,128)(2,1)}, u32[]{:S(2)}, u32[]{:S(2)}) collective-permute-start(bf16[1024,128]{1,0:T(8,128)(2,1)S(1)} %bitcast.463), channel_id=1, source_target_pairs={{0,1},{1,0},{2,3},{3,2},{4,5},{5,4},{6,7},{7,6},{8,9},{9,8},{10,11... | collective-permute-start | bytes 786440 | tf_op jit(solution)/shard_map/ppermute | solution.py:29
  68.2 16.1 %collective-permute-start.34 = (bf16[1024,128]{1,0:T(8,128)(2,1)S(1)}, bf16[1024,128]{1,0:T(8,128)(2,1)}, u32[]{:S(2)}, u32[]{:S(2)}) collective-permute-start(bf16[1024,128]{1,0:T(8,128)(2,1)S(1)} %bitcast.464), channel_id=1, source_target_pairs={{0,2},{1,3},{2,0},{3,1},{4,6},{5,7},{6,4},{7,5},{8,10},{9,11},{10,... | collective-permute-start | bytes 786440 | tf_op jit(solution)/shard_map/ppermute | solution.py:29
  84.3 21.8 %collective-permute-start.36 = (bf16[1024,128]{1,0:T(8,128)(2,1)S(1)}, bf16[1024,128]{1,0:T(8,128)(2,1)S(1)}, u32[]{:S(2)}, u32[]{:S(2)}) collective-permute-start(bf16[1024,128]{1,0:T(8,128)(2,1)S(1)} %bitcast.466), channel_id=1, source_target_pairs={{0,4},{1,5},{2,6},{3,7},{4,0},{5,1},{6,2},{7,3},{8,12},{9,13},{10,... | collective-permute-start | bytes 786440 | tf_op jit(solution)/shard_map/ppermute | solution.py:29
  93.4 17.2 %collective-permute-start.37 = (bf16[1024,128]{1,0:T(8,128)(2,1)S(1)}, bf16[1024,128]{1,0:T(8,128)(2,1)S(1)}, u32[]{:S(2)}, u32[]{:S(2)}) collective-permute-start(bf16[1024,128]{1,0:T(8,128)(2,1)S(1)} %bitcast.467), channel_id=1, source_target_pairs={{0,5},{1,4},{2,7},{3,6},{4,1},{5,0},{6,3},{7,2},{8,13},{9,12},{10,... | collective-permute-start | bytes 786440 | tf_op jit(solution)/shard_map/ppermute | solution.py:29
  136.5 26.7 %collective-permute-start.4 = (bf16[272,1024]{1,0:T(8,128)(2,1)}, bf16[272,1024]{1,0:T(8,128)(2,1)}, u32[]{:S(2)}, u32[]{:S(2)}) collective-permute-start(bf16[272,1024]{1,0:T(8,128)(2,1)} %collective-permute-done.2), channel_id=1, source_target_pairs={{2,0},{3,1},{4,2},{5,3},{10,8},{11,9},{12,10},{13,11},{18,16},{19,... | collective-permute-start | bytes 1671176 | tf_op jit(solution)/shard_map/ppermute | solution.py:111
  163.9 16.8 %collective-permute-start.6 = (bf16[272,1024]{1,0:T(8,128)(2,1)}, bf16[272,1024]{1,0:T(8,128)(2,1)}, u32[]{:S(2)}, u32[]{:S(2)}) collective-permute-start(bf16[272,1024]{1,0:T(8,128)(2,1)} %collective-permute-done.4), channel_id=1, source_target_pairs={{2,0},{3,1},{10,8},{11,9},{18,16},{19,17},{26,24},{27,25}} | collective-permute-start | bytes 1671176 | tf_op jit(solution)/shard_map/ppermute | solution.py:111
  167.3 18.5 %collective-permute-start.8 = (bf16[272,1024]{1,0:T(8,128)(2,1)S(1)}, bf16[272,1024]{1,0:T(8,128)(2,1)}, u32[]{:S(2)}, u32[]{:S(2)}) collective-permute-start(bf16[272,1024]{1,0:T(8,128)(2,1)S(1)} %add.521), channel_id=1, source_target_pairs={{0,1},{1,0},{2,3},{3,2},{4,5},{5,4},{6,7},{7,6},{8,9},{9,8},{10,11... | collective-permute-start | bytes 1671176 | tf_op jit(solution)/shard_map/ppermute | solution.py:29
  278.6 14.1 %collective-permute-start.51 = (bf16[128,1024]{1,0:T(8,128)(2,1)}, bf16[128,1024]{1,0:T(8,128)(2,1)}, u32[]{:S(2)}, u32[]{:S(2)}) collective-permute-start(bf16[128,1024]{1,0:T(8,128)(2,1)} %get-tuple-element.375), channel_id=1, source_target_pairs={{0,16},{8,24},{16,0},{24,8},{1,17},{9,25},{17,1},{25,9},{2,18},{10... | collective-permute-start | bytes 786440 | tf_op jit(solution)/shard_map/ppermute | solution.py:29
  288.5 13.5 %collective-permute-start.55 = (bf16[128,1024]{1,0:T(8,128)(2,1)}, bf16[128,1024]{1,0:T(8,128)(2,1)S(1)}, u32[]{:S(2)}, u32[]{:S(2)}) collective-permute-start(bf16[128,1024]{1,0:T(8,128)(2,1)} %collective-permute-done.54), channel_id=1, source_target_pairs={{0,8},{8,0},{16,24},{24,16},{1,9},{9,1},{17,25},{25,17},{2,10},{10... | collective-permute-start | bytes 786440 | tf_op jit(solution)/shard_map/ppermute | solution.py:29
  431.1 18.7 %collective-permute-start.84 = (bf16[32,1024]{1,0:T(8,128)(2,1)S(1)}, bf16[32,1024]{1,0:T(8,128)(2,1)S(1)}, u32[]{:S(2)}, u32[]{:S(2)}) collective-permute-start(bf16[32,1024]{1,0:T(8,128)(2,1)S(1)} %get-tuple-element.357), channel_id=1, source_target_pairs={{0,4},{1,5},{2,6},{3,7},{4,0},{5,1},{6,2},{7,3},{8,12},{9,13},{10,... | collective-permute-start | bytes 196616 | tf_op jit(solution)/shard_map/ppermute | solution.py:29
  432.9 16.8 %collective-permute-start.85 = (bf16[32,1024]{1,0:T(8,128)(2,1)S(1)}, bf16[32,1024]{1,0:T(8,128)(2,1)S(1)}, u32[]{:S(2)}, u32[]{:S(2)}) collective-permute-start(bf16[32,1024]{1,0:T(8,128)(2,1)S(1)} %get-tuple-element.356), channel_id=1, source_target_pairs={{0,5},{1,4},{2,7},{3,6},{4,1},{5,0},{6,3},{7,2},{8,13},{9,12},{10,... | collective-permute-start | bytes 196616 | tf_op jit(solution)/shard_map/ppermute | solution.py:29
  433.2 16.6 %collective-permute-start.86 = (bf16[32,1024]{1,0:T(8,128)(2,1)S(1)}, bf16[32,1024]{1,0:T(8,128)(2,1)S(1)}, u32[]{:S(2)}, u32[]{:S(2)}) collective-permute-start(bf16[32,1024]{1,0:T(8,128)(2,1)S(1)} %get-tuple-element.355), channel_id=1, source_target_pairs={{0,6},{1,7},{2,4},{3,5},{4,2},{5,3},{6,0},{7,1},{8,14},{9,15},{10,... | collective-permute-start | bytes 196616 | tf_op jit(solution)/shard_map/ppermute | solution.py:29
  536.8 15.5 %collective-permute-start.109 = (bf16[128,1024]{1,0:T(8,128)(2,1)S(1)}, bf16[128,1024]{1,0:T(8,128)(2,1)S(1)}, u32[]{:S(2)}, u32[]{:S(2)}) collective-permute-start(bf16[128,1024]{1,0:T(8,128)(2,1)S(1)} %get-tuple-element.289), channel_id=1, source_target_pairs={{0,16},{8,24},{16,0},{24,8},{1,17},{9,25},{17,1},{25,9},{2,18},{10... | collective-permute-start | bytes 786440 | tf_op jit(solution)/shard_map/ppermute | solution.py:29
  629.8 27.9 %collective-permute-start.155 = (bf16[4,256,128]{2,1,0:T(8,128)(2,1)S(1)}, bf16[4,256,128]{2,1,0:T(8,128)(2,1)S(1)}, u32[]{:S(2)}, u32[]{:S(2)}) collective-permute-start(bf16[4,256,128]{2,1,0:T(8,128)(2,1)S(1)} %bitcast.478), channel_id=1, source_target_pairs={{0,7},{1,6},{2,5},{3,4},{4,3},{5,2},{6,1},{7,0},{8,15},{9,14},{10,... | collective-permute-start | bytes 786440 | tf_op jit(solution)/shard_map/ppermute | solution.py:29
  631.8 28.1 %collective-permute-start.154 = (bf16[4,256,128]{2,1,0:T(8,128)(2,1)S(1)}, bf16[4,256,128]{2,1,0:T(8,128)(2,1)S(1)}, u32[]{:S(2)}, u32[]{:S(2)}) collective-permute-start(bf16[4,256,128]{2,1,0:T(8,128)(2,1)S(1)} %bitcast.477), channel_id=1, source_target_pairs={{0,6},{1,7},{2,4},{3,5},{4,2},{5,3},{6,0},{7,1},{8,14},{9,15},{10,... | collective-permute-start | bytes 786440 | tf_op jit(solution)/shard_map/ppermute | solution.py:29
  633.8 26.1 %collective-permute-start.131 = (bf16[256,1024]{1,0:T(8,128)(2,1)S(1)}, bf16[256,1024]{1,0:T(8,128)(2,1)S(1)}, u32[]{:S(2)}, u32[]{:S(2)}) collective-permute-start(bf16[256,1024]{1,0:T(8,128)(2,1)S(1)} %get-tuple-element.272), channel_id=1, source_target_pairs={{0,1},{1,0},{2,3},{3,2},{4,5},{5,4},{6,7},{7,6},{8,9},{9,8},{10,11... | collective-permute-start | bytes 1572872 | tf_op jit(solution)/shard_map/ppermute | solution.py:29
  634.4 20.6 %collective-permute-start.129 = (bf16[256,1024]{1,0:T(8,128)(2,1)S(1)}, bf16[256,1024]{1,0:T(8,128)(2,1)S(1)}, u32[]{:S(2)}, u32[]{:S(2)}) collective-permute-start(bf16[256,1024]{1,0:T(8,128)(2,1)S(1)} %get-tuple-element.275), channel_id=1, source_target_pairs={{0,2},{1,3},{8,10},{9,11},{16,18},{17,19},{24,26},{25,27}} | collective-permute-start | bytes 1572872 | tf_op jit(solution)/shard_map/ppermute | solution.py:129
  638.0 17.0 %collective-permute-start.130 = (bf16[256,1024]{1,0:T(8,128)(2,1)S(1)}, bf16[256,1024]{1,0:T(8,128)(2,1)S(1)}, u32[]{:S(2)}, u32[]{:S(2)}) collective-permute-start(bf16[256,1024]{1,0:T(8,128)(2,1)S(1)} %get-tuple-element.276), channel_id=1, source_target_pairs={{6,4},{7,5},{14,12},{15,13},{22,20},{23,21},{30,28},{31,29}} | collective-permute-start | bytes 1572872 | tf_op jit(solution)/shard_map/ppermute | solution.py:130
  655.0 20.8 %collective-permute-start.153 = (bf16[4,256,128]{2,1,0:T(8,128)(2,1)S(1)}, bf16[4,256,128]{2,1,0:T(8,128)(2,1)S(1)}, u32[]{:S(2)}, u32[]{:S(2)}) collective-permute-start(bf16[4,256,128]{2,1,0:T(8,128)(2,1)S(1)} %bitcast.476), channel_id=1, source_target_pairs={{0,5},{1,4},{2,7},{3,6},{4,1},{5,0},{6,3},{7,2},{8,13},{9,12},{10,... | collective-permute-start | bytes 786440 | tf_op jit(solution)/shard_map/ppermute | solution.py:29
  655.0 26.5 %collective-permute-start.152 = (bf16[4,256,128]{2,1,0:T(8,128)(2,1)S(1)}, bf16[4,256,128]{2,1,0:T(8,128)(2,1)S(1)}, u32[]{:S(2)}, u32[]{:S(2)}) collective-permute-start(bf16[4,256,128]{2,1,0:T(8,128)(2,1)S(1)} %bitcast.475), channel_id=1, source_target_pairs={{0,4},{1,5},{2,6},{3,7},{4,0},{5,1},{6,2},{7,3},{8,12},{9,13},{10,... | collective-permute-start | bytes 786440 | tf_op jit(solution)/shard_map/ppermute | solution.py:29
  657.8 24.6 %collective-permute-start.151 = (bf16[4,256,128]{2,1,0:T(8,128)(2,1)S(1)}, bf16[4,256,128]{2,1,0:T(8,128)(2,1)S(1)}, u32[]{:S(2)}, u32[]{:S(2)}) collective-permute-start(bf16[4,256,128]{2,1,0:T(8,128)(2,1)S(1)} %bitcast.474), channel_id=1, source_target_pairs={{0,3},{1,2},{2,1},{3,0},{4,7},{5,6},{6,5},{7,4},{8,11},{9,10},{10,... | collective-permute-start | bytes 786440 | tf_op jit(solution)/shard_map/ppermute | solution.py:29
  659.9 22.6 %collective-permute-start.150 = (bf16[4,256,128]{2,1,0:T(8,128)(2,1)S(1)}, bf16[4,256,128]{2,1,0:T(8,128)(2,1)S(1)}, u32[]{:S(2)}, u32[]{:S(2)}) collective-permute-start(bf16[4,256,128]{2,1,0:T(8,128)(2,1)S(1)} %bitcast.473), channel_id=1, source_target_pairs={{0,2},{1,3},{2,0},{3,1},{4,6},{5,7},{6,4},{7,5},{8,10},{9,11},{10,... | collective-permute-start | bytes 786440 | tf_op jit(solution)/shard_map/ppermute | solution.py:29
  659.9 24.0 %collective-permute-start.149 = (bf16[4,256,128]{2,1,0:T(8,128)(2,1)S(1)}, bf16[4,256,128]{2,1,0:T(8,128)(2,1)S(1)}, u32[]{:S(2)}, u32[]{:S(2)}) collective-permute-start(bf16[4,256,128]{2,1,0:T(8,128)(2,1)S(1)} %bitcast.472), channel_id=1, source_target_pairs={{0,1},{1,0},{2,3},{3,2},{4,5},{5,4},{6,7},{7,6},{8,9},{9,8},{10,11... | collective-permute-start | bytes 786440 | tf_op jit(solution)/shard_map/ppermute | solution.py:29
  675.8 13.2 %collective-permute-start.132 = (bf16[256,1024]{1,0:T(8,128)(2,1)S(1)}, bf16[256,1024]{1,0:T(8,128)(2,1)S(1)}, u32[]{:S(2)}, u32[]{:S(2)}) collective-permute-start(bf16[256,1024]{1,0:T(8,128)(2,1)S(1)} %get-tuple-element.143), channel_id=1, source_target_pairs={{0,2},{1,3},{2,4},{3,5},{8,10},{9,11},{10,12},{11,13},{16,18},{17,... | collective-permute-start | bytes 1572872 | tf_op jit(solution)/shard_map/ppermute | solution.py:129
  682.4 32.9 %collective-permute-start.126 = (bf16[256,1024]{1,0:T(8,128)(2,1)S(1)}, bf16[256,1024]{1,0:T(8,128)(2,1)S(1)}, u32[]{:S(2)}, u32[]{:S(2)}) collective-permute-start(bf16[256,1024]{1,0:T(8,128)(2,1)S(1)} %get-tuple-element.271), channel_id=1, source_target_pairs={{0,1},{1,0},{2,3},{3,2},{4,5},{5,4},{6,7},{7,6},{8,9},{9,8},{10,11... | collective-permute-start | bytes 1572872 | tf_op jit(solution)/shard_map/ppermute | solution.py:29
  694.9 16.3 %collective-permute-start.134 = (bf16[256,1024]{1,0:T(8,128)(2,1)S(1)}, bf16[256,1024]{1,0:T(8,128)(2,1)S(1)}, u32[]{:S(2)}, u32[]{:S(2)}) collective-permute-start(bf16[256,1024]{1,0:T(8,128)(2,1)S(1)} %add_convert_fusion.1), channel_id=1, source_target_pairs={{0,2},{1,3},{2,4},{3,5},{4,6},{5,7},{8,10},{9,11},{10,12},{11,13},... | collective-permute-start | bytes 1572872 | tf_op jit(solution)/shard_map/ppermute | solution.py:129
  700.6 14.8 %collective-permute-start.135 = (bf16[256,1024]{1,0:T(8,128)(2,1)S(1)}, bf16[256,1024]{1,0:T(8,128)(2,1)S(1)}, u32[]{:S(2)}, u32[]{:S(2)}) collective-permute-start(bf16[256,1024]{1,0:T(8,128)(2,1)S(1)} %add_convert_fusion), channel_id=1, source_target_pairs={{2,0},{3,1},{4,2},{5,3},{6,4},{7,5},{10,8},{11,9},{12,10},{13,11},... | collective-permute-start | bytes 1572872 | tf_op jit(solution)/shard_map/ppermute | solution.py:130
  (208 other events, 1999.0 us)

commit v2 on v1

v2 whole, which is shorter than its diff:
```python
import functools

import jax
import jax.numpy as jnp
from jax import lax
from jax.experimental import pallas as pl
from jax.experimental.pallas import tpu as pltpu
from jax.sharding import PartitionSpec as P

HEADS = 16
EPS = 1e-05
NEG = -1e30
BF = jnp.bfloat16
F32 = jnp.float32
NT = (((1,), (1,)), ((), ()))
NN = (((1,), (0,)), ((), ()))
LANES = 128


def dot(left, right, dims=NN):
    return lax.dot_general(left, right, dims, preferred_element_type=F32)


def add_low(left, right):
    return (left.astype(F32) + right.astype(F32)).astype(BF)


def send_xor(value, axis, size, mask):
    return lax.ppermute(value, axis, [(i, i ^ mask) for i in range(size)])


def bits_of(size):
    return list(range(size.bit_length() - 1))


def gather_path(value, axis, size, bits):
    held = {0: value}
    for bit in bits:
        held.update({m | (1 << bit): send_xor(v, axis, size, 1 << bit) for m, v in list(held.items())})
    return [held[m] for m in range(size)]


def scatter_path(blocks, axis, size, bits):
    held = dict(enumerate(blocks))
    for bit in bits[:-1]:
        leaving = {m: v for m, v in held.items() if (m >> bit) & 1}
        held = {m: v for m, v in held.items() if not (m >> bit) & 1}
        for m, v in leaving.items():
            keep = m & ~(1 << bit)
            held[keep] = add_low(held[keep], send_xor(v, axis, size, 1 << bit))
    last = 1 << bits[-1]
    return [held[0], send_xor(held[last], axis, size, last)]


def direct_gather(value, axis, size):
    return [value] + [send_xor(value, axis, size, m) for m in range(1, size)]


def direct_exchange(blocks, axis, size):
    return [blocks[0]] + [send_xor(blocks[m], axis, size, m) for m in range(1, size)]


def reorder(stacked, mine, size):
    return jnp.concatenate(
        [lax.dynamic_index_in_dim(stacked, mine ^ j, 0, keepdims=True) for j in range(size)]
    )


def swap_core(value, size):
    return send_xor(value, "col", size, 1)


def right_pairs(first, last, size):
    return [(i, i + 2) for i in range(size) if first <= i // 2 <= last]


def left_pairs(first, last, size):
    return [(i, i - 2) for i in range(size) if first <= i // 2 <= last]


def line_order(mine, size):
    chips = size // 2
    return [
        ((mine // 2 + turn) % chips) * 2 + ((mine % 2) ^ core)
        for turn in range(chips)
        for core in range(2)
    ]


def col_order(mine, size):
    return line_order(mine, size) if size == 8 else [mine ^ m for m in range(size)]


def col_gather(value, size):
    return gather_path(value, "col", size, bits_of(size))


def col_scatter(blocks, size):
    mine, last = scatter_path(blocks, "col", size, bits_of(size))
    return mine.astype(F32) + last.astype(F32)


def layer_stats(stream):
    center = stream - jnp.mean(stream, axis=-1, keepdims=True)
    inv_root = lax.rsqrt(jnp.mean(center * center, axis=-1, keepdims=True) + EPS)
    return (center * inv_root, inv_root)


def norm_back(grad_normed, unit_rows, inv_root, gain_full):
    grad_unit = grad_normed * gain_full
    mean_first = jnp.mean(grad_unit, axis=-1, keepdims=True)
    mean_second = jnp.mean(grad_unit * unit_rows, axis=-1, keepdims=True)
    return inv_root * (grad_unit - mean_first - unit_rows * mean_second)


ANY = pl.BlockSpec(memory_space=pl.ANY)
HBM = pl.BlockSpec(memory_space=pltpu.HBM)
VMEM = pl.BlockSpec(memory_space=pltpu.VMEM)
SMEM = pl.BlockSpec(memory_space=pltpu.SMEM)


def shape(dims, kind):
    return jax.ShapeDtypeStruct(dims, kind)


def params(mib):
    return pltpu.CompilerParams(vmem_limit_bytes=mib * 1024 * 1024)


def copies_of(pairs, sems):
    return [pltpu.make_async_copy(s, d, sems.at[n]) for n, (s, d) in enumerate(pairs)]


def begin(pairs, sems):
    copies = copies_of(pairs, sems)
    for copy in copies:
        copy.start()
    return copies


def finish(copies):
    for copy in copies:
        copy.wait()


def arrange_kernel(count, rows, me_ref, *refs):
    out_ref = refs[count]
    for m in range(count):
        at = pl.ds(pl.multiple_of((me_ref[0] ^ m) * rows, rows), rows)
        out_ref[at, :] = refs[m][:rows, :]


def arrange_rows(pieces, rows, me):
    count = len(pieces)
    cols = pieces[0].shape[1]
    return pl.pallas_call(
        functools.partial(arrange_kernel, count, rows),
        in_specs=[SMEM] + [VMEM] * count,
        out_specs=VMEM,
        out_shape=shape((count * rows, cols), pieces[0].dtype),
        name="arrange_rows",
    )(me, *pieces)


def tile_rows(tiles_ref, block):
    return jnp.concatenate([tiles_ref[block, col] for col in range(tiles_ref.shape[1])], axis=1)


def scalar_lanes(values):
    high = values.astype(BF).astype(F32)
    lane = lax.broadcasted_iota(jnp.int32, (values.shape[0], LANES), 1)
    return jnp.where(lane == 0, high, jnp.where(lane == 1, values - high, 0.0)).astype(BF)


def forward_kernel(tiles_ref, tokens_ref, ctx_ref, cent_ref, onehot_ref, route_ref, residual_ref, gate_ref, moved_ref):
    rows_n, unused, part, unused = tiles_ref.shape
    held = tokens_ref[...].astype(F32)
    for n in range(rows_n):
        held = held + lax.dot_general(
            ctx_ref[n * part : (n + 1) * part, :],
            tile_rows(tiles_ref, n),
            (((0,), (0,)), ((), ())),
            preferred_element_type=F32,
        )
    residual_ref[...] = held
    shared = held.astype(BF)
    cent_rows = dot(onehot_ref[...], cent_ref[...])
    gate = jax.nn.sigmoid(jnp.sum(shared.astype(F32) * cent_rows, axis=1, keepdims=True))
    gate_ref[...] = gate
    sent = jnp.concatenate([shared, scalar_lanes(gate)], axis=1)
    moved_ref[...] = dot(route_ref[...], sent).astype(BF)


def forward_rows(ctx, tiles, tokens, cent, onehot, route):
    tok, width = tokens.shape
    return pl.pallas_call(
        forward_kernel,
        in_specs=[VMEM] * 6,
        out_specs=[VMEM] * 3,
        out_shape=[shape((tok, width), F32), shape((tok, 1), F32), shape((tok, width + LANES), BF)],
        cost_estimate=pl.CostEstimate(
            flops=3 * tok * width * width, bytes_accessed=2 * width * width + 8 * tok * width, transcendentals=0
        ),
        name="forward_rows",
    )(tiles, tokens, ctx, cent, onehot, route)


def enter_kernel(experts_ref, cot_ref, rows_ref, stream_ref, grad_ref, first_ref, second_ref):
    width = stream_ref.shape[1]
    half = first_ref.shape[0]
    stream = rows_ref[:, :width]
    lanes = rows_ref[:, width:]
    gate = jnp.sum(lanes.astype(F32), axis=1, keepdims=True)
    stream_ref[...] = stream
    unit_rows, unused = layer_stats(stream.astype(F32))
    normed = (unit_rows * experts_ref[0:1] + experts_ref[2:3]).astype(BF)
    first_ref[:, :width] = normed[:half]
    first_ref[:, width:] = lanes[:half]
    second_ref[:, :width] = normed[half:]
    second_ref[:, width:] = lanes[half:]
    grad_ref[...] = (cot_ref[...].astype(F32) * gate).astype(BF)


def enter_expert(rows, experts, cot):
    tok, width = cot.shape
    wide = (tok // 2, width + LANES)
    return pl.pallas_call(
        enter_kernel,
        in_specs=[VMEM] * 3,
        out_specs=[VMEM] * 4,
        out_shape=[shape((tok, width), BF)] * 2 + [shape(wide, BF)] * 2,
        cost_estimate=pl.CostEstimate(flops=20 * tok * width, bytes_accessed=10 * tok * width, transcendentals=0),
        name="enter_expert",
    )(experts, cot, rows)


def between_kernel(experts_ref, stream_ref, *refs):
    first_own, first_more, second_own, second_more, out_ref, first_ref, second_ref = refs
    half = first_ref.shape[0]
    for n, (own, more, low) in enumerate(
        ((first_own, first_more, first_ref), (second_own, second_more, second_ref))
    ):
        at = slice(n * half, (n + 1) * half)
        branch = own[...].astype(F32) + more[...].astype(F32)
        stream = stream_ref[at, :].astype(F32) + branch + experts_ref[4:5]
        out_ref[at, :] = stream
        unit_rows, unused = layer_stats(stream)
        low[...] = (unit_rows * experts_ref[1:2] + experts_ref[3:4]).astype(BF)


def between_experts(experts, stream, sums):
    tok, width = stream.shape
    return pl.pallas_call(
        between_kernel,
        in_specs=[VMEM] * 6,
        out_specs=[VMEM] * 3,
        out_shape=[shape((tok, width), F32)] + [shape((tok // 2, width), BF)] * 2,
        cost_estimate=pl.CostEstimate(flops=20 * tok * width, bytes_accessed=12 * tok * width, transcendentals=0),
        name="between_experts",
    )(experts, stream, *sums)


def norm_grads(half, sub, experts_ref, stream_ref, upper_ref, pairs, sums_ref):
    width = stream_ref.shape[1]
    grads = []
    for n, (own, more) in enumerate(pairs):
        at = slice(n * half, (n + 1) * half)
        grad_normed = own[:, :width].astype(F32) + more[:, :width].astype(F32)
        unit_rows, inv_root = layer_stats(stream_ref[at, :].astype(F32))
        upper = upper_ref[at, :].astype(F32)
        for row, values in enumerate((grad_normed * unit_rows, grad_normed, upper)):
            total = jnp.sum(values, axis=0, keepdims=True)
            if n == 0:
                sums_ref[row : row + 1, :] = total
            else:
                sums_ref[row : row + 1, :] += total
        grads.append(upper + norm_back(grad_normed, unit_rows, inv_root, experts_ref[sub : sub + 1]))
    return grads


def middle_back_kernel(experts_ref, stream_ref, upper_ref, *refs):
    first_own, first_more, second_own, second_more, out_ref, first_ref, second_ref, sums_ref = refs
    half = first_ref.shape[0]
    pairs = ((first_own, first_more), (second_own, second_more))
    grads = norm_grads(half, 1, experts_ref, stream_ref, upper_ref, pairs, sums_ref)
    for n, low in enumerate((first_ref, second_ref)):
        out_ref[n * half : (n + 1) * half, :] = grads[n]
        low[...] = grads[n].astype(BF)


def middle_back(experts, stream, upper, sums):
    tok, width = stream.shape
    return pl.pallas_call(
        middle_back_kernel,
        in_specs=[VMEM] * 7,
        out_specs=[VMEM] * 4,
        out_shape=[shape((tok, width), F32)] + [shape((tok // 2, width), BF)] * 2 + [shape((3, width), F32)],
        cost_estimate=pl.CostEstimate(flops=40 * tok * width, bytes_accessed=16 * tok * width, transcendentals=0),
        name="middle_back",
    )(experts, stream, upper, *sums)


def leave_back_kernel(experts_ref, stream_ref, upper_ref, cot_ref, later_ref, first_own, first_more, second_own, second_more, out_ref, sums_ref):
    width = stream_ref.shape[1]
    half = first_own.shape[0]
    pairs = ((first_own, first_more), (second_own, second_more))
    grads = norm_grads(half, 0, experts_ref, stream_ref, upper_ref, pairs, sums_ref)
    for n, (own, more) in enumerate(pairs):
        at = slice(n * half, (n + 1) * half)
        lanes = own[:, width:].astype(F32) + more[:, width:].astype(F32)
        kept = cot_ref[at, :].astype(F32) * (later_ref[at, :] + experts_ref[5:6])
        logit = jnp.sum(lanes, axis=1, keepdims=True) + jnp.sum(kept, axis=1, keepdims=True)
        out_ref[at, :width] = grads[n].astype(BF)
        out_ref[at, width:] = scalar_lanes(logit)


def leave_back(experts, stream, upper, cot, later, sums):
    tok, width = stream.shape
    return pl.pallas_call(
        leave_back_kernel,
        in_specs=[VMEM] * 9,
        out_specs=[VMEM] * 2,
        out_shape=[shape((tok, width + LANES), BF), shape((3, width), F32)],
        cost_estimate=pl.CostEstimate(flops=40 * tok * width, bytes_accessed=20 * tok * width, transcendentals=0),
        name="leave_back",
    )(experts, stream, upper, cot, later, *sums)


def backward_kernel(tiles_ref, unroute_ref, back_ref, cot_ref, cent_ref, onehot_ref, turned_ref, gate_ref, residual_ref, out_ref, low_ref, cent_out, ctx_ref):
    width = cot_ref.shape[1]
    rows_n, unused, part, unused = tiles_ref.shape
    back = dot(unroute_ref[...], back_ref[...])
    gate = gate_ref[...]
    grad_logit = jnp.sum(back[:, width:], axis=1, keepdims=True) * gate * (1.0 - gate)
    cent_rows = dot(onehot_ref[...], cent_ref[...])
    grad = cot_ref[...].astype(F32) + (back[:, :width] + grad_logit * cent_rows)
    out_ref[...] = grad
    low = grad.astype(BF)
    low_ref[...] = low
    for n in range(rows_n):
        ctx_ref[n * part : (n + 1) * part, :] = dot(tile_rows(tiles_ref, n), low, NT).astype(BF)
    cent_out[...] = lax.dot_general(
        turned_ref[...].astype(F32),
        grad_logit * residual_ref[...].astype(BF).astype(F32),
        NN,
        precision=lax.Precision.HIGHEST,
        preferred_element_type=F32,
    )


def backward_rows(back, tiles, unroute, cot, cent, onehot, gate, residual):
    tok, width = cot.shape
    return pl.pallas_call(
        backward_kernel,
        in_specs=[VMEM] * 9,
        out_specs=[VMEM] * 4,
        out_shape=[
            shape((tok, width), F32),
            shape((tok, width), BF),
            shape((LANES, width), F32),
            shape((width, tok), BF),
        ],
        cost_estimate=pl.CostEstimate(
            flops=3 * tok * width * width, bytes_accessed=2 * width * width + 12 * tok * width, transcendentals=0
        ),
        name="backward_rows",
    )(tiles, unroute, back, cot, cent, onehot, onehot.T, gate, residual)


def finish_kernel(stream_ref, branch_ref, experts_ref, out_ref):
    out_ref[...] = (stream_ref[...] + branch_ref[...].astype(F32) + experts_ref[5:6]).astype(BF)


def finish_rows(stream, branch, experts):
    return pl.pallas_call(
        finish_kernel,
        in_specs=[VMEM] * 3,
        out_specs=VMEM,
        out_shape=shape(stream.shape, BF),
        name="finish_rows",
    )(stream, branch, experts)


def project_kernel(scale, sources, rows, lead, gain_ref, shift_ref, w_ref, *refs):
    count = len(sources)
    total = sum(sources)
    blocks, refs = refs[:total], refs[total:]
    outs, refs = refs[:6], refs[6:]
    if lead:
        packets_ref, gain_out, shift_out, refs = *refs[:3], refs[3:]
    x_all, held, sems, out_sems = refs[0], refs[1:7], refs[7], refs[8]
    fw = w_ref.shape[1] // 3
    copies = begin([(b, x_all.at[n]) for n, b in enumerate(blocks)], sems)
    starts = [sum(sources[:n]) for n in range(count)]

    def merged(n, at):
        return sum(x_all[starts[n] + i, at, :].astype(F32) for i in range(sources[n]))

    if lead:
        finish(copies)
        packets = [merged(n, slice(rows, rows + 16)) for n in lead]
        for n, value in enumerate(packets):
            packets_ref[n] = value.astype(BF)
        value = sum(packets)
        gain, shift = value[0:1], value[1:2]
        gain_out[...] = gain
        shift_out[...] = shift
    else:
        gain, shift = gain_ref[...], shift_ref[...]
    leaving = []
    for n in range(count):
        if not lead:
            finish(copies[starts[n] : starts[n] + sources[n]])
        unit_rows, unused = layer_stats(merged(n, slice(0, rows)))
        normed = (unit_rows * gain + shift).astype(BF)
        held[0][n] = normed
        out = dot(normed, w_ref[...])
        keys = out[:, fw : 2 * fw]
        values = out[:, 2 * fw :]
        held[1][n] = (out[:, :fw].astype(BF).astype(F32) * scale).astype(BF)
        held[2][n] = keys.astype(BF)
        held[3][n] = values.astype(BF)
        held[4][n] = keys.T.astype(BF)
        held[5][n] = values.T.astype(BF)
        leaving += begin(
            [(h.at[n], o.at[n]) for h, o in zip(held, outs)], out_sems.at[pl.ds(6 * n, 6)]
        )
    finish(leaving)


def project(blocks, gain, shift, w, rows, scale, lead=()):
    sources = [len(b) for b in blocks]
    flat = [v for b in blocks for v in b]
    count = len(blocks)
    width = flat[0].shape[1]
    fw = w.shape[1] // 3
    kinds = [(count, rows, width)] + [(count, rows, fw)] * 3 + [(count, fw, rows)] * 2
    more = [shape((len(lead), 16, width), BF)] + [shape((1, width), F32)] * 2 if lead else []
    return pl.pallas_call(
        functools.partial(project_kernel, scale, sources, rows, lead),
        in_specs=[VMEM] * 3 + [ANY] * len(flat),
        out_specs=[ANY] * 6 + [VMEM] * len(more),
        out_shape=[shape(k, BF) for k in kinds] + more,
        scratch_shapes=[pltpu.VMEM((len(flat),) + flat[0].shape, BF)]
        + [pltpu.VMEM(k, BF) for k in kinds]
        + [pltpu.SemaphoreType.DMA((len(flat),)), pltpu.SemaphoreType.DMA((6 * count,))],
        cost_estimate=pl.CostEstimate(
            flops=count * (2 * rows * width * fw * 3 + 10 * rows * width),
            bytes_accessed=2 * count * (2 * rows * width + 5 * rows * fw) + 6 * width * fw,
            transcendentals=0,
        ),
        name="project",
    )(gain, shift, w, *flat)


def views(refs):
    return [ref.at[n] for ref in refs for n in range(ref.shape[0])]


def split_lanes(rows, count):
    width = rows.shape[1] // count
    if count == 1:
        return rows
    head_of = lax.broadcasted_iota(jnp.int32, rows.shape, 1) // width
    return jnp.concatenate(
        [jnp.where(head_of == h, rows, jnp.zeros_like(rows)) for h in range(count)], axis=0
    )


def split_rows(cols, count):
    width = cols.shape[0] // count
    if count == 1:
        return cols
    head_of = lax.broadcasted_iota(jnp.int32, cols.shape, 0) // width
    return jnp.concatenate(
        [jnp.where(head_of == h, cols, jnp.zeros_like(cols)) for h in range(count)], axis=1
    )


QB = 2
KB = 2


QB = 2
KB = 2


QB = 2
KB = 2


def attend_kernel(heads, total, groups, qb, kb, lead, order_ref, group_ref, ids_ref, *refs):
    q_in, k_in, vt_in = [views(refs[n * groups : (n + 1) * groups]) for n in range(3)]
    ctx_ref, low_ref, lse_ref, ends_ref, q_all, k_all, vt_all, low_all, count_ref, sems, out_sems = refs[
        3 * groups :
    ]
    rows = low_all.shape[2]
    fw = q_all.shape[2]
    head = fw // heads
    span = qb * rows
    key_rows = kb * rows
    pairs = []
    for n in range(total):
        at = order_ref[n]
        q_at = pl.ds(pl.multiple_of(lax.rem(at, qb) * rows, rows), rows)
        k_at = pl.ds(pl.multiple_of(lax.rem(at, kb) * rows, rows), rows)
        pairs += [
            (q_in[n], q_all.at[lax.div(at, qb), q_at, :]),
            (k_in[n], k_all.at[lax.div(at, kb), k_at, :]),
            (vt_in[n], vt_all.at[lax.div(at, kb), :, k_at]),
        ]
    copies = begin(pairs, sems)

    per = total // ids_ref.shape[0]
    ids = []
    for n in range(total):
        group = ids_ref[group_ref[n]].astype(F32)
        ids.append(group[lead + n % per : lead + n % per + 1, :rows])
    ids = jnp.concatenate(ids, axis=0)
    ends = jnp.zeros((total, rows), F32)
    for n in range(total):
        members = jnp.sum(jnp.where(ids == n, 1.0, 0.0))
        ends = ends + jnp.where(ids >= n, members, 0.0)
    for i in range(total // qb):
        ends_ref[i] = jnp.concatenate([ends[i * qb + b : i * qb + b + 1] for b in range(qb)], axis=1)
        last = jnp.max(ends[i * qb + qb - 1 : i * qb + qb]).astype(jnp.int32)
        count_ref[i] = lax.div(last + (key_rows - 1), key_rows)
    finish(copies)
    spots = lax.broadcasted_iota(jnp.int32, (key_rows, heads * span), 0).astype(F32)

    def block(i, unused):
        queries = split_lanes(q_all[i], heads)
        ends = jnp.concatenate([ends_ref[i]] * heads, axis=1)

        def step(j, state):
            run_max, run_sum, held = state
            scores = dot(k_all[j], queries, NT)
            scores = jnp.where(spots < ends - (j * key_rows).astype(F32), scores, NEG)
            new_max = jnp.maximum(run_max, jnp.max(scores, axis=0, keepdims=True))
            weights = jnp.exp(scores - new_max)
            factor = jnp.exp(run_max - new_max)
            new_sum = run_sum * factor + jnp.sum(weights, axis=0, keepdims=True)
            low = weights.astype(BF)
            values = vt_all[j]
            new_held = tuple(
                held[h] * factor[:, h * span : (h + 1) * span]
                + dot(values[h * head : (h + 1) * head], low[:, h * span : (h + 1) * span])
                for h in range(heads)
            )
            return new_max, new_sum, new_held

        start = (
            jnp.full((1, heads * span), NEG, F32),
            jnp.zeros((1, heads * span), F32),
            tuple(jnp.zeros((head, span), F32) for h in range(heads)),
        )
        run_max, run_sum, held = lax.fori_loop(0, count_ref[i], step, start)
        for h in range(heads):
            result = held[h] / run_sum[:, h * span : (h + 1) * span]
            ctx_ref[i, h * head : (h + 1) * head, :] = result
            for b in range(qb):
                low_all[i * qb + b, h * head : (h + 1) * head, :] = result[
                    :, b * rows : (b + 1) * rows
                ].astype(BF)
        lse_ref[i] = run_max + jnp.log(run_sum)
        return unused

    lax.fori_loop(0, total // qb, block, 0)
    finish(begin([(low_all, low_ref)], out_sems))


def attend(q, k, vt, ids, lead, group, order, heads):
    total = len(order)
    groups = len(q)
    rows, fw = q[0].shape[1:]
    qb, kb = QB, KB
    pairs = total * rows * total * rows * heads
    return pl.pallas_call(
        functools.partial(attend_kernel, heads, total, groups, qb, kb, lead),
        in_specs=[SMEM] * 2 + [VMEM] + [ANY] * (3 * groups),
        out_specs=[VMEM, ANY, VMEM, VMEM],
        out_shape=[
            shape((total // qb, fw, qb * rows), F32),
            shape((total, fw, rows), BF),
            shape((total // qb, 1, heads * qb * rows), F32),
            shape((total // qb, 1, qb * rows), F32),
        ],
        scratch_shapes=[
            pltpu.VMEM((total // qb, qb * rows, fw), BF),
            pltpu.VMEM((total // kb, kb * rows, fw), BF),
            pltpu.VMEM((total // kb, fw, kb * rows), BF),
            pltpu.VMEM((total, fw, rows), BF),
            pltpu.SMEM((total // qb,), jnp.int32),
            pltpu.SemaphoreType.DMA((3 * total,)),
            pltpu.SemaphoreType.DMA((1,)),
        ],
        cost_estimate=pl.CostEstimate(
            flops=2 * pairs * 128, bytes_accessed=10 * total * rows * fw, transcendentals=pairs // 2
        ),
        name="attend",
    )(order, group, ids, *q, *k, *vt)


def attend_back_kernel(heads, scale, total, groups, qb, kb, order_ref, ends_ref, ctx_ref, lse_ref, w_ref, gain_ref, shift_ref, cent_ref, *refs):
    q_in, k_in, v_in, kt_in, normed_in = [views(refs[n * groups : (n + 1) * groups]) for n in range(5)]
    refs = refs[5 * groups :]
    grad_in, refs = refs[0], refs[1:]
    out_refs, refs = refs[:total], refs[total:]
    dq_ref, dk_ref, dv_ref = refs[:3]
    q_raw, k_all, v_all, kt_all, g_raw, q_all, grad_all, delta_all, dq_all, out_all, normed_all, small_all, first_ref = refs[3:16]
    sems, normed_sems, out_sems, small_sems = refs[16:]
    unused, rows, width = out_all.shape
    normed_copies = begin([(normed_in[n], normed_all.at[n]) for n in range(total)], normed_sems)
    fw = q_raw.shape[2]
    head = fw // heads
    span = qb * rows
    pairs = []
    for n in range(total):
        at = order_ref[n]
        q_at = pl.ds(pl.multiple_of(lax.rem(at, qb) * rows, rows), rows)
        k_at = pl.ds(pl.multiple_of(lax.rem(at, kb) * rows, rows), rows)
        pairs += [
            (q_in[n], q_raw.at[lax.div(at, qb), q_at, :]),
            (k_in[n], k_all.at[lax.div(at, kb), k_at, :]),
            (v_in[n], v_all.at[lax.div(at, kb), k_at, :]),
            (kt_in[n], kt_all.at[lax.div(at, kb), :, k_at]),
            (grad_in.at[n], g_raw.at[n // qb, :, pl.ds((n % qb) * rows, rows)]),
        ]
    copies = begin(pairs, sems)
    lasts = [jnp.max(ends_ref[i]).astype(jnp.int32) for i in range(total // qb)]
    for j in range(total // kb):
        first_ref[j] = sum((last <= j * kb * rows).astype(jnp.int32) for last in lasts)
    finish(copies)

    def prepare(i, unused):
        q_all[i] = split_lanes(q_raw[i], heads)
        grad = g_raw[i]
        grad_all[i] = split_rows(grad, heads)
        product = grad.astype(F32) * ctx_ref[i]
        delta_all[i] = jnp.concatenate(
            [
                jnp.sum(product[h * head : (h + 1) * head], axis=0, keepdims=True)
                for h in range(heads)
            ],
            axis=1,
        )
        dq_all[i] = jnp.zeros((fw, span), F32)
        return unused

    lax.fori_loop(0, total // qb, prepare, 0)

    spots = lax.broadcasted_iota(jnp.int32, (kb * rows, span), 0).astype(F32)

    def key_block(j, unused):
        keys = k_all[j]
        values = v_all[j]
        keys_t = kt_all[j]

        def step(i, state):
            dk, dv = state
            ends = ends_ref[i] - (j * (kb * rows)).astype(F32)
            for h in range(heads):
                at = slice(h * span, (h + 1) * span)
                queries = q_all[i, at, :]
                grads = grad_all[i, :, at]
                scores = dot(keys, queries, NT) - lse_ref[i, :, at]
                probs = jnp.exp(jnp.where(spots < ends, scores, NEG))
                grad_probs = dot(values, grads) - delta_all[i, :, at]
                grad_scores = (probs * grad_probs).astype(BF)
                dv = dv + dot(probs.astype(BF), grads, NT)
                dk = dk + dot(grad_scores, queries)
                dq_all[i, h * head : (h + 1) * head, :] += dot(
                    keys_t[h * head : (h + 1) * head], grad_scores
                )
            return dk, dv

        zero = jnp.zeros((kb * rows, fw), F32)
        dk, dv = lax.fori_loop(first_ref[j], total // qb, step, (zero, zero))
        dk_ref[pl.ds(j * kb, kb)] = dk.astype(BF).reshape(kb, rows, fw)
        dv_ref[pl.ds(j * kb, kb)] = dv.astype(BF).reshape(kb, rows, fw)
        return unused

    lax.fori_loop(0, total // kb, key_block, 0)

    def turn(i, unused):
        dq_ref[pl.ds(i * qb, qb)] = (dq_all[i] * scale).T.astype(BF).reshape(qb, rows, fw)
        return unused

    lax.fori_loop(0, total // qb, turn, 0)

    leaving = []
    lifted = jnp.zeros((1, width), F32)
    shifted = jnp.zeros((1, width), F32)
    for n in range(total):
        at = order_ref[n]
        grad = dot(jnp.concatenate([dq_ref[at], dk_ref[at], dv_ref[at]], axis=1), w_ref[...], NT)
        out_all[n] = grad.astype(BF)
        leaving += begin(
            [(out_all.at[n], out_refs[n].at[pl.ds(0, rows), :])], out_sems.at[pl.ds(n, 1)]
        )
        normed_copies[n].wait()
        shifted = shifted + jnp.sum(grad, axis=0, keepdims=True)
        lifted = lifted + jnp.sum(grad * normed_all[n].astype(F32), axis=0, keepdims=True)
    lifted = (lifted - shift_ref[...] * shifted) / gain_ref[...]
    for n in range(total):
        rest = jnp.zeros((small_all.shape[1] - 3, width), F32)
        cent = cent_ref[pl.ds(order_ref[n], 1), :]
        small_all[n] = jnp.concatenate([lifted, shifted, cent, rest], axis=0).astype(BF)
    finish(
        leaving
        + begin(
            [(small_all.at[n], out_refs[n].at[pl.ds(rows, small_all.shape[1]), :]) for n in range(total)],
            small_sems,
        )
    )


def attend_back(q, k, v, kt, normed, grads, ctx, lse, w, gain, shift, cent, ends, order, heads, scale):
    total = len(order)
    groups = len(q)
    rows, fw = q[0].shape[1:]
    width = w.shape[0]
    qb, kb = QB, KB
    pairs = total * rows * total * rows * heads
    out = pl.pallas_call(
        functools.partial(attend_back_kernel, heads, scale, total, groups, qb, kb),
        in_specs=[SMEM] + [VMEM] * 7 + [ANY] * (5 * groups + 1),
        out_specs=[ANY] * total + [VMEM] * 3,
        out_shape=[shape((rows + 16, width), BF)] * total + [shape((total, rows, fw), BF)] * 3,
        scratch_shapes=[
            pltpu.VMEM((total // qb, qb * rows, fw), BF),
            pltpu.VMEM((total // kb, kb * rows, fw), BF),
            pltpu.VMEM((total // kb, kb * rows, fw), BF),
            pltpu.VMEM((total // kb, fw, kb * rows), BF),
            pltpu.VMEM((total // qb, fw, qb * rows), BF),
            pltpu.VMEM((total // qb, heads * qb * rows, fw), BF),
            pltpu.VMEM((total // qb, fw, heads * qb * rows), BF),
            pltpu.VMEM((total // qb, 1, heads * qb * rows), F32),
            pltpu.VMEM((total // qb, fw, qb * rows), F32),
            pltpu.VMEM((total, rows, width), BF),
            pltpu.VMEM((total, rows, width), BF),
            pltpu.VMEM((total, 16, width), BF),
            pltpu.SMEM((total // kb,), jnp.int32),
            pltpu.SemaphoreType.DMA((5 * total,)),
            pltpu.SemaphoreType.DMA((total,)),
            pltpu.SemaphoreType.DMA((total,)),
            pltpu.SemaphoreType.DMA((total,)),
        ],
        cost_estimate=pl.CostEstimate(
            flops=5 * pairs * 128, bytes_accessed=20 * total * rows * fw, transcendentals=pairs // 2
        ),
        name="attend_back",
    )(order, ends, ctx, lse, w, gain, shift, cent, *q, *k, *v, *kt, *normed, grads)
    return out[:total], out[total], out[total + 1], out[total + 2]


def project_grads_kernel(total, groups, parts, order_ref, dq_ref, dk_ref, dv_ref, *refs):
    normed_in, (out_ref, normed_all, sems) = views(refs[:groups]), refs[groups:]
    rows = dq_ref.shape[1]
    copies = begin(
        [
            (normed_in[n], normed_all.at[pl.ds(pl.multiple_of(order_ref[n] * rows, rows), rows)])
            for n in range(total)
        ],
        sems,
    )
    grads = jnp.concatenate(
        [ref[...].reshape(total * rows, ref.shape[2]) for ref in (dq_ref, dk_ref, dv_ref)], axis=1
    )
    finish(copies)
    step = out_ref.shape[0] // parts
    for n in range(parts):
        out_ref[n * step : (n + 1) * step, :] = lax.dot_general(
            normed_all[:, n * step : (n + 1) * step],
            grads,
            (((0,), (0,)), ((), ())),
            preferred_element_type=F32,
        ).astype(BF)


def project_grads(dq, dk, dv, normed, order, parts):
    total, rows, fw = dq.shape
    width = normed[0].shape[2]
    return pl.pallas_call(
        functools.partial(project_grads_kernel, total, len(normed), parts),
        in_specs=[SMEM] + [VMEM] * 3 + [ANY] * len(normed),
        out_specs=VMEM,
        out_shape=shape((width, 3 * fw), BF),
        scratch_shapes=[pltpu.VMEM((total * rows, width), BF), pltpu.SemaphoreType.DMA((total,))],
        cost_estimate=pl.CostEstimate(
            flops=2 * total * rows * width * 3 * fw,
            bytes_accessed=2 * total * rows * (width + 3 * fw) + 2 * width * 3 * fw,
            transcendentals=0,
        ),
        name="project_grads",
    )(order, dq, dk, dv, *normed)


def output_grads_kernel(ctx_ref, grad_ref, out_ref):
    cols_n, rows_n, part, fw = out_ref.shape
    for n in range(rows_n):
        result = dot(ctx_ref[n * part : (n + 1) * part, :], grad_ref[...]).astype(BF)
        for col in range(cols_n):
            out_ref[col, n] = result[:, col * fw : (col + 1) * fw]


def output_grads(ctx, grad, rows_n, cols_n):
    tok, width = grad.shape
    return pl.pallas_call(
        output_grads_kernel,
        in_specs=[VMEM] * 2,
        out_specs=VMEM,
        out_shape=shape((cols_n, rows_n, width // rows_n, width // cols_n), BF),
        cost_estimate=pl.CostEstimate(
            flops=2 * tok * width * width, bytes_accessed=2 * width * width, transcendentals=0
        ),
        name="output_grads",
    )(ctx, grad)


CHUNK = 512


def gelu_pair(pre_act):
    below = 0.5 * (1.0 + lax.erf(pre_act * 0.7071067811865476))
    bell = jnp.exp(-0.5 * pre_act * pre_act) * 0.3989422804014327
    return pre_act * below, below + pre_act * bell


def weight_copies(sub, w_in, w_back, first, second, sems):
    count, unused, chunk = first.shape

    def copy(n, which):
        at = pl.ds(pl.multiple_of(n * chunk, chunk), chunk)
        if which == 0:
            return pltpu.make_async_copy(w_in.at[0, sub, :, at], first.at[n], sems.at[2 * n])
        return pltpu.make_async_copy(w_back.at[0, sub, at, :], second.at[n], sems.at[2 * n + 1])

    for n in range(count):
        copy(n, 0).start()
        copy(n, 1).start()
    return copy


def add_to(total, n, more):
    @pl.when(n == 0)
    def begin_sum():
        total[...] = more

    @pl.when(n > 0)
    def add_sum():
        total[...] += more


def piece_pairs(pieces, held, first_lane=0):
    rows = held.shape[0] // len(pieces)
    lanes = pl.ds(first_lane, held.shape[1])
    return [(piece.at[:, lanes], held.at[pl.ds(m * rows, rows), :]) for m, piece in enumerate(pieces)]


def back_pairs(pieces, held):
    rows = held.shape[0] // len(pieces)
    return [(held.at[pl.ds(m * rows, rows), :], piece) for m, piece in enumerate(pieces)]


def spread_pairs(me_ref, whole, held, count):
    rows = held.shape[0] // count
    size = count // 2
    pairs = []
    for m in range(count):
        at = ((me_ref[0] ^ (m % size)) * 2 + m // size) * rows
        pairs.append((whole.at[pl.ds(pl.multiple_of(at, rows), rows), :], held.at[pl.ds(m * rows, rows), :]))
    return pairs


def expert_first_kernel(sub, count, bias_ref, w_in, w_back, *refs):
    pieces, refs = refs[:count], refs[count:]
    outs, refs = refs[:count], refs[count:]
    all_ref, hidden_ref, slope_ref = refs[:3]
    held, first, second, hidden, slope, total, low, sem_w, sem_x, sem_o, sem_r = refs[3:]
    chunks, unused, chunk = first.shape
    weights = weight_copies(sub, w_in, w_back, first, second, sem_w)
    finish(begin(piece_pairs(pieces, held), sem_x))
    leaving = begin([(held, all_ref)], sem_r.at[pl.ds(0, 1)])
    kept = [(hidden, hidden_ref), (slope, slope_ref)]

    def step(n, unused):
        weights(n, 0).wait()
        value, rise = gelu_pair(dot(held[...], first[n]) + bias_ref[n].astype(F32))
        hidden[n] = value.astype(BF)
        slope[n] = rise
        begin([(h.at[n], o.at[n]) for h, o in kept], sem_r.at[pl.ds(2 * n + 1, 2)])
        weights(n, 1).wait()
        add_to(total, n, dot(hidden[n], second[n]))
        return unused

    lax.fori_loop(0, chunks, step, 0)
    low[...] = total[...].astype(BF)
    leaving += begin(back_pairs(outs, low), sem_o)
    finish(leaving)
    for n in range(chunks):
        finish(copies_of([(h.at[n], o.at[n]) for h, o in kept], sem_r.at[pl.ds(2 * n + 1, 2)]))


def expert_first(pieces, sub, w_in, w_back, bias):
    count = len(pieces)
    rows, width = pieces[0].shape[0] * count, w_in.shape[2]
    ff = w_in.shape[3]
    chunk = min(CHUNK, ff)
    chunks = ff // chunk
    out = pl.pallas_call(
        functools.partial(expert_first_kernel, sub, count),
        in_specs=[VMEM, ANY, ANY] + [ANY] * count,
        out_specs=[ANY] * (count + 3),
        out_shape=[shape((rows // count, width), BF)] * count
        + [
            shape((rows, width), BF),
            shape((chunks, rows, chunk), BF),
            shape((chunks, rows, chunk), F32),
        ],
        scratch_shapes=[
            pltpu.VMEM((rows, width), BF),
            pltpu.VMEM((chunks, width, chunk), BF),
            pltpu.VMEM((chunks, chunk, width), BF),
            pltpu.VMEM((chunks, rows, chunk), BF),
            pltpu.VMEM((chunks, rows, chunk), F32),
            pltpu.VMEM((rows, width), F32),
            pltpu.VMEM((rows, width), BF),
            pltpu.SemaphoreType.DMA((2 * chunks,)),
            pltpu.SemaphoreType.DMA((count,)),
            pltpu.SemaphoreType.DMA((count,)),
            pltpu.SemaphoreType.DMA((2 * chunks + 1,)),
        ],
        cost_estimate=pl.CostEstimate(
            flops=4 * rows * width * ff, bytes_accessed=8 * rows * width, transcendentals=2 * rows * ff
        ),
        name="expert_first",
    )(bias.reshape(chunks, 1, chunk), w_in, w_back, *pieces)
    return out[:count], out[count], out[count + 1], out[count + 2]


def expert_second_kernel(sub, count, me_ref, bias_ref, w_in, w_back, *refs):
    cot_in, refs = refs[: count // 2], refs[count // 2 :]
    pieces, refs = refs[:count], refs[count:]
    gates, refs = refs[:count], refs[count:]
    grad_outs, refs = refs[:count], refs[count:]
    out_ref, all_ref, grad_all_ref, hidden_ref, pre_ref, bias_out, logit_ref = refs[:7]
    held, cot, gate, held_grad, first, second, hidden, grad_pre, total, low, low_grad = refs[7:18]
    sem_w, sem_x, sem_c, sem_g, sem_o, sem_p, sem_r = refs[18:]
    chunks, unused, chunk = first.shape
    weights = weight_copies(sub, w_in, w_back, first, second, sem_w)
    arriving = begin(piece_pairs(pieces, held), sem_x)
    width = held.shape[1]
    size, rows = count // 2, cot.shape[0] // count
    early = begin(
        [
            (cot_in[m % size].at[pl.ds(m // size * rows, rows), :], cot.at[pl.ds(m * rows, rows), :])
            for m in range(count)
        ],
        sem_c,
    )
    early += begin(piece_pairs(gates, gate, width), sem_g)
    finish(early)
    held_grad[...] = (
        cot[...].astype(F32) * jnp.sum(gate[...].astype(F32), axis=1, keepdims=True)
    ).astype(BF)
    finish(arriving)
    leaving = begin([(held, all_ref), (held_grad, grad_all_ref)], sem_r.at[pl.ds(0, 2)])
    kept = [(hidden, hidden_ref), (grad_pre, pre_ref)]

    def step(n, unused):
        weights(n, 0).wait()
        pre_act = dot(held[...], first[n]) + bias_ref[n].astype(F32)
        weights(n, 1).wait()
        grad_hidden = dot(held_grad[...], second[n], NT)
        value, rise = gelu_pair(pre_act)
        hidden[n] = value.astype(BF)
        back = (grad_hidden * rise).astype(BF)
        grad_pre[n] = back
        bias_out[n] = jnp.sum(back.astype(F32), axis=0, keepdims=True)
        begin([(h.at[n], o.at[n]) for h, o in kept], sem_r.at[pl.ds(2 * n + 2, 2)])
        add_to(total, n, dot(grad_pre[n], first[n], NT))
        return unused

    lax.fori_loop(0, chunks, step, 0)
    low_grad[...] = total[...].astype(BF)
    leaving += begin(back_pairs(grad_outs, low_grad), sem_p)

    def forward(n, unused):
        add_to(total, n, dot(hidden[n], second[n]))
        return unused

    lax.fori_loop(0, chunks, forward, 0)
    low[...] = total[...].astype(BF)
    logit_ref[...] = scalar_lanes(
        jnp.sum(cot[...].astype(F32) * total[...], axis=1, keepdims=True)
    )
    outs = [(h, w) for w, h in spread_pairs(me_ref, out_ref, low, count)]
    finish(leaving + begin(outs, sem_o))
    for n in range(chunks):
        finish(copies_of([(h.at[n], o.at[n]) for h, o in kept], sem_r.at[pl.ds(2 * n + 2, 2)]))


def expert_second(pieces, gates, cot, sub, w_in, w_back, bias, me):
    count = len(pieces)
    rows, width = pieces[0].shape
    rows = rows * count
    ff = w_in.shape[3]
    chunk = min(CHUNK, ff)
    chunks = ff // chunk
    out = pl.pallas_call(
        functools.partial(expert_second_kernel, sub, count),
        in_specs=[SMEM, VMEM] + [ANY] * (2 + 2 * count + count // 2),
        out_specs=[ANY] * (count + 5) + [VMEM] * 2,
        out_shape=[shape((rows // count, width), BF)] * count
        + [shape((rows, width), BF)] * 3
        + [shape((chunks, rows, chunk), BF)] * 2
        + [shape((chunks, 1, chunk), F32), shape((rows, LANES), BF)],
        scratch_shapes=[
            pltpu.VMEM((rows, width), BF),
            pltpu.VMEM((rows, width), BF),
            pltpu.VMEM((rows, LANES), BF),
            pltpu.VMEM((rows, width), BF),
            pltpu.VMEM((chunks, width, chunk), BF),
            pltpu.VMEM((chunks, chunk, width), BF),
            pltpu.VMEM((chunks, rows, chunk), BF),
            pltpu.VMEM((chunks, rows, chunk), BF),
            pltpu.VMEM((rows, width), F32),
            pltpu.VMEM((rows, width), BF),
            pltpu.VMEM((rows, width), BF),
            pltpu.SemaphoreType.DMA((2 * chunks,)),
            pltpu.SemaphoreType.DMA((count,)),
            pltpu.SemaphoreType.DMA((count,)),
            pltpu.SemaphoreType.DMA((count,)),
            pltpu.SemaphoreType.DMA((count,)),
            pltpu.SemaphoreType.DMA((count,)),
            pltpu.SemaphoreType.DMA((2 * chunks + 2,)),
        ],
        cost_estimate=pl.CostEstimate(
            flops=8 * rows * width * ff, bytes_accessed=12 * rows * width, transcendentals=2 * rows * ff
        ),
        name="expert_second",
    )(me, bias.reshape(chunks, 1, chunk), w_in, w_back, *cot, *pieces, *gates)
    return out[:count], *out[count:]


def expert_back_kernel(sub, count, logit_ref, w_in, w_back, slope_in, *refs):
    grads, refs = refs[:count], refs[count:]
    grad_outs, refs = refs[:count], refs[count:]
    grad_all_ref, pre_ref, bias_out = refs[:3]
    held_grad, first, second, slope, grad_pre, total, low_grad = refs[3:10]
    sem_w, sem_s, sem_g, sem_p, sem_r = refs[10:]
    chunks, unused, chunk = first.shape
    weights = weight_copies(sub, w_in, w_back, first, second, sem_w)
    arriving_grad = begin(piece_pairs(grads, held_grad), sem_g)
    begin([(slope_in.at[n], slope.at[n]) for n in range(chunks)], sem_s)
    low_grad[:, held_grad.shape[1] :] = logit_ref[...]
    finish(arriving_grad)
    leaving = begin([(held_grad, grad_all_ref)], sem_r.at[pl.ds(0, 1)])

    def step(n, unused):
        weights(n, 1).wait()
        grad_hidden = dot(held_grad[...], second[n], NT)
        pltpu.make_async_copy(slope_in.at[n], slope.at[n], sem_s.at[n]).wait()
        back = (grad_hidden * slope[n]).astype(BF)
        grad_pre[n] = back
        bias_out[n] = jnp.sum(back.astype(F32), axis=0, keepdims=True)
        begin([(grad_pre.at[n], pre_ref.at[n])], sem_r.at[pl.ds(n + 1, 1)])
        weights(n, 0).wait()
        add_to(total, n, dot(grad_pre[n], first[n], NT))
        return unused

    lax.fori_loop(0, chunks, step, 0)
    low_grad[:, : total.shape[1]] = total[...].astype(BF)
    finish(leaving + begin(back_pairs(grad_outs, low_grad), sem_p))
    for n in range(chunks):
        finish(copies_of([(grad_pre.at[n], pre_ref.at[n])], sem_r.at[pl.ds(n + 1, 1)]))


def expert_back(grads, slope, logit, sub, w_in, w_back):
    count = len(grads)
    rows, width = grads[0].shape
    rows = rows * count
    ff = w_in.shape[3]
    chunk = min(CHUNK, ff)
    chunks = ff // chunk
    out = pl.pallas_call(
        functools.partial(expert_back_kernel, sub, count),
        in_specs=[VMEM] + [ANY] * (3 + count),
        out_specs=[ANY] * (count + 2) + [VMEM],
        out_shape=[shape((rows // count, width + LANES), BF)] * count
        + [shape((rows, width), BF), shape((chunks, rows, chunk), BF), shape((chunks, 1, chunk), F32)],
        scratch_shapes=[
            pltpu.VMEM((rows, width), BF),
            pltpu.VMEM((chunks, width, chunk), BF),
            pltpu.VMEM((chunks, chunk, width), BF),
            pltpu.VMEM((chunks, rows, chunk), F32),
            pltpu.VMEM((chunks, rows, chunk), BF),
            pltpu.VMEM((rows, width), F32),
            pltpu.VMEM((rows, width + LANES), BF),
            pltpu.SemaphoreType.DMA((2 * chunks,)),
            pltpu.SemaphoreType.DMA((chunks,)),
            pltpu.SemaphoreType.DMA((count,)),
            pltpu.SemaphoreType.DMA((count,)),
            pltpu.SemaphoreType.DMA((chunks + 1,)),
        ],
        cost_estimate=pl.CostEstimate(
            flops=4 * rows * width * ff, bytes_accessed=10 * rows * width, transcendentals=0
        ),
        name="expert_back",
    )(logit, w_in, w_back, slope, *grads)
    return out[:count], *out[count:]


def weight_grads_kernel(chunked_left, left_ref, right_ref, *refs):
    out_ref = refs[-1]
    if chunked_left:
        left, right = left_ref[0], right_ref[...]
    else:
        left, right = left_ref[...], right_ref[0]
    out_ref[0, 0] = lax.dot_general(left, right, (((0,), (0,)), ((), ())), preferred_element_type=F32)


def weight_grads(left, right, sub, held, chunked_left):
    chunked, plain = (left, right) if chunked_left else (right, left)
    chunks, rows, chunk = chunked.shape
    width = plain.shape[1]
    pieces = pl.BlockSpec((1, rows, chunk), lambda n: (n, 0, 0))
    whole = pl.BlockSpec((rows, width), lambda n: (0, 0))
    if chunked_left:
        in_specs = [pieces, whole]
        out_spec = pl.BlockSpec((1, 1, chunk, width), lambda n: (0, sub, n, 0))
        dims = (1, 2, chunks * chunk, width)
    else:
        in_specs = [whole, pieces]
        out_spec = pl.BlockSpec((1, 1, width, chunk), lambda n: (0, sub, 0, n))
        dims = (1, 2, width, chunks * chunk)
    more = [] if held is None else [held]
    return pl.pallas_call(
        functools.partial(weight_grads_kernel, chunked_left),
        grid=(chunks,),
        in_specs=in_specs + [ANY] * len(more),
        out_specs=out_spec,
        out_shape=shape(dims, F32),
        input_output_aliases={2: 0} if more else {},
        cost_estimate=pl.CostEstimate(
            flops=2 * rows * width * chunks * chunk,
            bytes_accessed=4 * width * chunks * chunk + 2 * rows * (width + chunks * chunk),
            transcendentals=0,
        ),
        name="weight_grads",
    )(left, right, *more)


def stack_gather(value, axis, size):
    for bit in bits_of(size):
        value = jnp.concatenate([value, send_xor(value, axis, size, 1 << bit)])
    return value


def stack_scatter(value, axis, size):
    for bit in bits_of(size)[::-1]:
        half = value.shape[0] // 2
        value = value[:half] + send_xor(value[half:], axis, size, 1 << bit)
    return value


def together(*values):
    return lax.optimization_barrier(values)


def after(value, *earlier):
    return lax.optimization_barrier((value, *earlier))[0]


def gather_pieces(first, second, axis, size):
    bits = bits_of(size)
    return gather_path(first, axis, size, bits) + gather_path(second, axis, size, bits[::-1])


def scatter_pieces(pieces, axis, size):
    bits = bits_of(size)
    return scatter_path(pieces[:size], axis, size, bits) + scatter_path(
        pieces[size:], axis, size, bits[::-1]
    )


def shards(
    tokens,
    block_ids,
    expert_ids,
    cotangent,
    norm_gain,
    norm_shift,
    w_query,
    w_key,
    w_value,
    w_output,
    centroids,
    expert_gain,
    expert_shift,
    w_in,
    b_in,
    w_back,
    b_back,
):
    rows_n = lax.axis_size("row")
    cols_n = lax.axis_size("col")
    r = lax.axis_index("row")
    c = lax.axis_index("col")
    me = jnp.stack([r, c]).astype(jnp.int32)
    tok, width = tokens.shape
    fw = width // cols_n
    heads = HEADS // cols_n
    scale = float(width // HEADS) ** (-0.5)
    part = width // rows_n
    own = norm_gain.shape[0]
    slot = tok // cols_n

    count = 2 * own + part
    w_cat = jnp.concatenate([w_query, w_key, w_value], axis=1)
    order = jnp.stack(col_order(c, cols_n)).astype(jnp.int32)

    def gather_tiles(value):
        return lax.all_gather(value, ("row", "col"), axis=0, tiled=True).reshape(
            rows_n, cols_n, part, fw
        )

    def matrix_sums(part_qkv, part_output):
        parts = jnp.concatenate([part_qkv, part_output], axis=1).reshape(rows_n, part, 4 * fw)
        parts = reorder(parts, r, rows_n)
        return direct_exchange([parts[m] for m in range(rows_n)], "row", rows_n)

    def exchange(rows):
        return lax.all_to_all(
            rows.reshape(cols_n, -1, rows.shape[-1]), "col", split_axis=0, concat_axis=0, tiled=True
        ).reshape(rows.shape)

    onehot = expert_ids[:, None] == jnp.arange(LANES, dtype=jnp.int32)[None, :]
    onehot_low = onehot.astype(BF)
    below = (jnp.arange(tok)[:, None] > jnp.arange(tok)[None, :]).astype(BF)
    before = dot(below, onehot_low)
    rank = jnp.sum(jnp.where(onehot, before, 0.0), axis=1).astype(jnp.int32)
    place = expert_ids * slot + rank
    route = (jnp.arange(tok, dtype=jnp.int32)[:, None] == place[None, :]).astype(BF)
    unroute = (place[:, None] == jnp.arange(tok, dtype=jnp.int32)[None, :]).astype(BF)
    moved_cot = dot(route, cotangent).astype(BF)
    small_experts = jnp.concatenate([expert_gain[0], expert_shift[0], b_back[0]])

    if cols_n == 8:
        chips = cols_n // 2
        z, core = c // 2, c % 2
        lane = jnp.arange(width, dtype=jnp.int32)
        mine = lane // own == r * cols_n + c
        cent_row = jnp.where(lane // part == r, jnp.tile(centroids[0], rows_n), 0)
        ids_row = jnp.pad(block_ids[0].astype(BF), (0, width - tok))
        packet = jnp.stack(
            [
                jnp.where(mine, jnp.tile(norm_gain, width // own), 0),
                jnp.where(mine, jnp.tile(norm_shift, width // own), 0),
                jnp.where(core == 0, cent_row, 0),
                jnp.where(core == 1, cent_row, 0),
                jnp.where(core == 0, ids_row, 0),
                jnp.where(core == 1, ids_row, 0),
                jnp.zeros_like(ids_row),
                jnp.zeros_like(ids_row),
            ]
        )
        packet = packet + swap_core(packet, cols_n)
        top = direct_gather(packet[:4], "row", rows_n)
        block = jnp.concatenate(
            [tokens, sum(top[1:], top[0]), packet[4:], jnp.zeros((8, width), BF)]
        )
        move_right = lambda v, s: lax.ppermute(v, "col", right_pairs(s - 1, chips - 2, cols_n))
        move_left = lambda v, s: lax.ppermute(v, "col", left_pairs(1, chips - s, cols_n))
        swap = lambda v: swap_core(v, cols_n)
        right_1, left_1 = move_right(block, 1), move_left(block, 1)
        w_pieces = direct_gather(after(w_cat, block), "row", rows_n)
        small_experts = direct_gather(after(small_experts, block), "row", rows_n)
        cot_own = exchange(moved_cot)
        right_1, left_1, cot_own, *rest = together(
            right_1, left_1, cot_own, *w_pieces, *small_experts
        )
        w_pieces, small_experts = rest[:rows_n], rest[rows_n:]
        right_2, left_2 = move_right(right_1, 2), move_left(left_1, 2)
        swapped, right_1s, left_1s = swap(block), swap(right_1), swap(left_1)
        w_cat = arrange_rows(w_pieces, part, me)
        right_2, left_2, swapped, right_1s, left_1s, w_cat = together(
            right_2, left_2, swapped, right_1s, left_1s, w_cat
        )
        right_3, left_3 = move_right(right_2, 3), move_left(left_2, 3)
        right_2s, left_2s = swap(right_2), swap(left_2)
        cot_pieces = direct_gather(after(cot_own, right_1), "row", rows_n)
        right_3, left_3, right_2s, left_2s, *cot_pieces = together(
            right_3, left_3, right_2s, left_2s, *cot_pieces
        )
        right_3s, left_3s = swap(right_3), swap(left_3)
        tiles = gather_tiles(after(w_output, right_3))
        nothing = jnp.zeros((1, width), F32)
        *early, packets, gain_attn, shift_attn = project(
            [
                (block,),
                (swapped,),
                (left_1, right_3),
                (left_2, right_2),
                (left_2s, right_2s),
                (left_3, right_1),
            ],
            nothing, nothing, w_cat, tok, scale, (0, 2, 3, 5),
        )
        late = project(
            [(left_1s, right_3s), (left_3s, right_1s)], gain_attn, shift_attn, w_cat, tok, scale
        )
        places = (0, 1, 2, 4, 5, 6, 3, 7)
        order = order[jnp.array(places)]
        projected = list(zip(early, late))
        ids, lead = packets, 4
        group = (jnp.arange(cols_n, dtype=jnp.int32) // 2 - z) % chips
        cents = packets[:, 2:4]
        turned = (jnp.arange(chips) - z) % chips
        centroids_of = lambda held: jnp.take(held, turned, axis=0).reshape(cols_n, width)
    else:
        w_pieces = direct_gather(w_cat, "row", rows_n)
        small_experts = direct_gather(small_experts, "row", rows_n)
        cot_own = exchange(moved_cot)
        cot_pieces = direct_gather(cot_own, "row", rows_n)
        w_cat = arrange_rows(w_pieces, part, me)
        gain_attn, shift_attn = [
            lax.all_gather(v, ("row", "col"), axis=0, tiled=True).reshape(1, width).astype(F32)
            for v in (norm_gain, norm_shift)
        ]
        cents = lax.all_gather(
            lax.all_gather(centroids, "row", axis=1, tiled=True), "col", axis=0, tiled=True
        )
        centroids_of = lambda held: held
        tiles = gather_tiles(w_output)
        blocks = [(v,) for v in col_gather(tokens, cols_n)]
        projected = [(p,) for p in project(blocks, gain_attn, shift_attn, w_cat, tok, scale)]
        ids = lax.all_gather(block_ids[0].astype(BF), "col", axis=0, tiled=True)
        ids, lead = ids.reshape(cols_n, 1, tok).astype(F32), 0
        group = jnp.arange(cols_n, dtype=jnp.int32)
    normed, q, k, v, kt, vt = projected

    ctx, ctx_low, lse, ends = attend(q, k, vt, ids, lead, group, order, heads)
    small_experts, cents, ctx_low = together(jnp.stack(small_experts), cents, ctx_low)
    ctx_low = exchange(ctx_low.reshape(width, tok))
    experts = reorder(small_experts, r, rows_n).transpose(1, 0, 2).reshape(6, width).astype(F32)
    full_centroids = jnp.pad(centroids_of(cents), ((0, LANES - cols_n), (0, 0)))
    residual, gate, moved = forward_rows(ctx_low, tiles, tokens, full_centroids, onehot_low, route)

    stream_0, grad_2, half_1, half_2 = enter_expert(exchange(moved), experts, cot_own)
    wide_pieces = gather_pieces(half_1, half_2, "row", rows_n)
    partial, normed_all_0, hidden_0, slope_0 = expert_first(wide_pieces, 0, w_in, w_back, b_in[0, 0])
    stream_1, half_1, half_2 = between_experts(
        experts, stream_0, scatter_pieces(partial, "row", rows_n)
    )
    pieces = gather_pieces(half_1, half_2, "row", rows_n)
    partial, branch, normed_all_1, grad_all_1, hidden_1, grad_pre_1, bias_1, logit = expert_second(
        pieces, wide_pieces, cot_pieces, 1, w_in, w_back, b_in[0, 1], me
    )
    sums = scatter_pieces(partial, "row", rows_n)
    w_in_grad = weight_grads(normed_all_1, grad_pre_1, 1, None, False)
    w_in_grad, *sums = together(w_in_grad, *sums)
    grad_1, half_1, half_2, sums_1 = middle_back(experts, stream_1, grad_2, sums)
    pieces = gather_pieces(half_1, half_2, "row", rows_n)
    w_back_grad = weight_grads(hidden_1, after(grad_all_1, grad_1), 1, None, True)
    w_back_grad, *pieces = together(w_back_grad, *pieces)
    partial, grad_all_0, grad_pre_0, bias_0 = expert_back(pieces, slope_0, logit, 0, w_in, w_back)
    sums = together(*scatter_pieces(partial, "row", rows_n))
    branch = lax.psum_scatter(after(branch, sums[0]), "row", scatter_dimension=0, tiled=True)
    leaving, sums_0 = leave_back(experts, stream_0, grad_1, cot_own, stream_1, sums)
    returned = exchange(leaving)
    w_in_grad = weight_grads(normed_all_0, after(grad_pre_0, sums_0), 0, w_in_grad, False)
    w_in_grad, returned = together(w_in_grad, returned)
    grad_residual, grad_attended, part_cent, grad_ctx = backward_rows(
        returned, tiles, unroute, cotangent, full_centroids, onehot_low, gate, residual
    )

    grad_ctx = exchange(grad_ctx)
    part_output = output_grads(ctx_low, grad_attended, rows_n, cols_n)
    w_back_grad = weight_grads(hidden_0, after(grad_all_0, grad_attended), 0, w_back_grad, True)
    expert_low = finish_rows(stream_1, branch, experts)
    part_output, w_back_grad, expert_low, grad_ctx = together(
        part_output, w_back_grad, expert_low, grad_ctx
    )
    expert_low = exchange(expert_low)
    part_output = lax.psum_scatter(
        part_output.reshape(cols_n * width, fw), "col", scatter_dimension=0, tiled=True
    )
    partial, dq, dk, dv = attend_back(
        q, k, v, kt, normed, grad_ctx.reshape(cols_n, fw, tok), ctx, lse, w_cat, gain_attn, shift_attn,
        part_cent, ends, order, heads, scale,
    )
    dq, expert_low, *partial = together(dq, expert_low, *partial)
    if cols_n == 8:
        partial = [partial[places.index(n)] for n in range(cols_n)]
        halves = [
            add_low(partial[2 * turn], swap(partial[2 * turn + 1])) for turn in range(chips)
        ]
        into_right = lambda v, s: lax.ppermute(
            v, "col", right_pairs(0, min(s - 1, chips - 2), cols_n)
        )
        into_left = lambda v, s: lax.ppermute(
            v, "col", left_pairs(max(chips - s, 1), chips - 1, cols_n)
        )
        from_left, from_right = into_right(halves[3], 1), into_left(halves[1], 1)
        part_qkv = project_grads(after(dq, halves[3]), dk, dv, normed, order, rows_n)
        from_left, from_right, part_qkv, part_output = together(
            from_left, from_right, part_qkv, part_output
        )
        from_left = into_right(add_low(from_left, halves[2]), 2)
        from_right = into_left(add_low(from_right, halves[2]), 2)
        output = (residual + gate * dot(unroute, expert_low)).astype(BF)
        grad_sums = matrix_sums(part_qkv, part_output)
        from_left, from_right, output, *grad_sums = together(from_left, from_right, output, *grad_sums)
        from_left = into_right(add_low(from_left, halves[1]), 3)
        from_right = into_left(add_low(from_right, halves[3]), 3)
        summed = halves[0].astype(F32) + from_left.astype(F32) + from_right.astype(F32)
    else:
        part_qkv = project_grads(dq, dk, dv, normed, order, rows_n)
        output = (residual + gate * dot(unroute, expert_low)).astype(BF)
        grad_sums = matrix_sums(part_qkv, part_output)
        summed = col_scatter(partial, cols_n)
    grad_matrices = sum(v.astype(F32) for v in grad_sums)
    grad_qkv, grad_output = grad_matrices[:, : 3 * fw], grad_matrices[:, 3 * fw :]
    grad_normed_attn = summed[:tok]

    norm_rows = summed[tok : tok + 2].reshape(2, rows_n, cols_n, own)
    norm_rows = lax.dynamic_index_in_dim(norm_rows, c, 2, keepdims=False).transpose(1, 0, 2)
    expert_rows = jnp.concatenate([sums_0, sums_1]).reshape(6, rows_n, part).transpose(1, 0, 2)
    packed = jnp.concatenate(
        [
            norm_rows.reshape(rows_n, 2 * own),
            summed[tok + 2].reshape(rows_n, part),
            expert_rows.reshape(rows_n, 6 * part),
        ],
        axis=1,
    )[:, None]
    packed = reorder(packed, r, rows_n)
    packed = sum(direct_exchange([packed[m] for m in range(rows_n)], "row", rows_n))[0]
    expert_sums = packed[count:].reshape(2, 3, part).transpose(1, 0, 2)

    inputs = tokens.astype(F32)
    unit_attn, inv_attn = layer_stats(inputs)
    tokens_grad = grad_residual + norm_back(grad_normed_attn, unit_attn, inv_attn, gain_attn)
    return (
        output,
        tokens_grad,
        packed[:own],
        packed[own : 2 * own],
        grad_qkv[:, :fw],
        grad_qkv[:, fw : 2 * fw],
        grad_qkv[:, 2 * fw :],
        grad_output,
        packed[None, 2 * own : count],
        expert_sums[None, 0],
        expert_sums[None, 1],
        w_in_grad,
        jnp.stack([bias_0.reshape(-1), bias_1.reshape(-1)])[None],
        w_back_grad,
        expert_sums[None, 2],
    )


def solution(mesh):
    placed = (
        P(("row", "col"), None),
        P("row", "col"),
        P(("row", "col")),
        P(("row", "col"), None),
        P(("row", "col")),
        P(("row", "col")),
        P("row", "col"),
        P("row", "col"),
        P("row", "col"),
        P("row", "col"),
        P("col", "row"),
        P("col", None, "row"),
        P("col", None, "row"),
        P("col", None, None, "row"),
        P("col", None, "row"),
        P("col", None, "row", None),
        P("col", None, "row"),
    )
    return jax.shard_map(
        shards,
        mesh=mesh,
        in_specs=placed,
        out_specs=(
            P(("row", "col"), None),
            P(("row", "col"), None),
            P(("row", "col")),
            P(("row", "col")),
            P("row", "col"),
            P("row", "col"),
            P("row", "col"),
            P("row", "col"),
            P("col", "row"),
            P("col", None, "row"),
            P("col", None, "row"),
            P("col", None, None, "row"),
            P("col", None, "row"),
            P("col", None, "row", None),
            P("col", None, "row"),
        ),
        check_vma=False,
    )
```

time: 744 us -> 532 us (0.72)
  waiting for transfers between devices: 291 us -> 160 us
  Pallas kernels: 55.6 us -> 173 us
  matrix products: 66.6 us -> 4.37 us
  starting transfers between devices: 186 us -> 127 us
  local copies, waits for them, and re-layouts: 75.6 us -> 21.2 us
  other arithmetic: 57.5 us -> 22 us
  between operations: 3.6 us -> 15.4 us
    ppermute x147 -> x66, waiting for transfers between devices: 232 us -> 88.8 us  [send_xor(): return lax.ppermute(value, axis, [(i, i ^ mask) for i in range(size)])]
    pallas_call x3 -> x21, Pallas kernels: 55.6 us -> 173 us  [the longest x1 33.6 us: attend_back(): pl.pallas_call(functools.partial(attend_back_kernel, heads, scale, total,...]
    ppermute x147 -> x66, starting transfers between devices: 162 us -> 67.2 us  [send_xor(): return lax.ppermute(value, axis, [(i, i ^ mask) for i in range(size)])]
    all_to_all x0 -> x6, waiting for transfers between devices: none -> 47.9 us  [exchange(): lax.all_to_all(rows.reshape(cols_n, -1, rows.shape[-1]), 'col', split_axi...]
    dot_general x16 -> x3, matrix products: 50.8 us -> 4.37 us  [dot(): return lax.dot_general(left, right, dims, preferred_element_type=F32)]
    ppermute x12, waiting for transfers between devices: 59.1 us -> 23.1 us  [the longest x3 12.3 us: shards(): lax.ppermute(v, 'col', left_pairs(1, chips - s, cols_n))]
    unnamed x330 -> x158, local copies, waits for them, and re-layouts: 44.5 us -> 12.2 us
    all_to_all x0 -> x6, starting transfers between devices: none -> 30.6 us  [exchange(): lax.all_to_all(rows.reshape(cols_n, -1, rows.shape[-1]), 'col', split_axi...]
  transfers between devices with their start and end apart: 159 -> 87, of which waited for: 73 -> 36; matrix products, arithmetic and copies ran while one was open for 13% -> 6% of each run, Pallas kernels for 0% -> 22%
where the time goes in v2:
time: 532 us; the launch traced here: 522 us
  Pallas kernels  173 us (33%)
  waiting for transfers between devices  160 us (30%)
  starting transfers between devices  127 us (24%)
  other arithmetic  22 us (4%)
  local copies, waits for them, and re-layouts  21.2 us (4%)
  between operations  15.4 us (3%)
    ppermute x66, waiting for transfers between devices, send_xor(): return lax.ppermute(value, axis, [(i, i ^ mask) for i in range(size)])  88.8 us
    ppermute x66, starting transfers between devices, send_xor(): return lax.ppermute(value, axis, [(i, i ^ mask) for i in range(size)])  67.2 us
    all_to_all x6, waiting for transfers between devices, exchange(): lax.all_to_all(rows.reshape(cols_n, -1, rows.shape[-1]), 'col', split_axi...  47.9 us
    pallas_call x1, Pallas kernels, attend_back(): pl.pallas_call(functools.partial(attend_back_kernel, heads, scale, total,...  33.6 us
    all_to_all x6, starting transfers between devices, exchange(): lax.all_to_all(rows.reshape(cols_n, -1, rows.shape[-1]), 'col', split_axi...  30.6 us
    pallas_call x4, Pallas kernels, weight_grads(): pl.pallas_call(functools.partial(weight_grads_kernel, chunked_left), grid...  23.4 us
    pallas_call x1, Pallas kernels, expert_second(): pl.pallas_call(functools.partial(expert_second_kernel, sub, count), in_sp...  20.6 us
    pallas_call x1, Pallas kernels, attend(): pl.pallas_call(functools.partial(attend_kernel, heads, total, groups, qb,...  18.5 us
  transfers between devices with their start and end apart: 87, of which 36 were waited for; matrix products, arithmetic and copies ran while one was open for 6% of the time, Pallas kernels for 22%

profile of v2, /device:TPU:0, one launch (start us, length us, event | category | flops | bytes accessed | tf_op | source)
XLA Modules:
  0.0 522.1 jit_solution(692759038639756786)
XLA Ops:
  18.3 5.4 %all-to-all-start = ((bf16[8,32,1024]{2,1,0:T(8,128)(2,1)}), bf16[8,32,1024]{2,1,0:T(8,128)(2,1)S(1)}, u32[]{:S(2)}, u32[]{:S(2)}) async-start(bf16[8,32,1024]{2,1,0:T(8,128)(2,1)} %bitcast.8), calls=%async_computation | async-start | bytes 1048576 | tf_op jit(solution)/shard_map/all_to_all | solution.py:1235
  43.5 5.3 %collective-permute-done.7.refs_2_ = bf16[256,384]{1,0:T(8,128)(2,1)S(1)} collective-permute-done((bf16[256,384]{1,0:T(8,128)(2,1)S(1)}, bf16[256,384]{1,0:T(8,128)(2,1)S(1)}, u32[]{:S(2)}, u32[]{:S(2)}) %collective-permute-start.7) | collective-permute-done | bytes 196640 | tf_op jit(solution)/shard_map/ppermute | solution.py:29
  56.7 11.9 %collective-permute-done.13.refs_4_ = bf16[272,1024]{1,0:T(8,128)(2,1)} collective-permute-done((bf16[272,1024]{1,0:T(8,128)(2,1)S(1)}, bf16[272,1024]{1,0:T(8,128)(2,1)}, u32[]{:S(2)}, u32[]{:S(2)}) %collective-permute-start.13) | collective-permute-done | bytes 557088 | tf_op jit(solution)/shard_map/ppermute | solution.py:1275
  73.7 12.4 %collective-permute-done.23.refs_3_ = bf16[256,1024]{1,0:T(8,128)(2,1)S(1)} collective-permute-done((bf16[256,1024]{1,0:T(8,128)(2,1)S(1)}, bf16[256,1024]{1,0:T(8,128)(2,1)S(1)}, u32[]{:S(2)}, u32[]{:S(2)}) %collective-permute-start.23) | collective-permute-done | bytes 524320 | tf_op jit(solution)/shard_map/ppermute | solution.py:29
  91.1 9.5 %project.2 = (bf16[6,256,1024]{2,1,0:T(8,128)(2,1)}, bf16[6,256,128]{2,1,0:T(8,128)(2,1)}, bf16[6,256,128]{2,1,0:T(8,128)(2,1)}, bf16[6,256,128]{2,1,0:T(8,128)(...) custom-call(f32[1,1024]{1,0:T(1,128)} %broadcast_in_dim.58.gain_ref., ...), custom_call_target="tpu_custom_call" | custom-call | flops 1223688192 | bytes 9043968 | tf_op jit(solution)/shard_map/project/pallas_call | solution.py:439
  101.6 4.7 project.3
  106.3 18.5 %attend.1 = (f32[4,128,512]{2,1,0:T(8,128)}, bf16[8,128,256]{2,1,0:T(8,128)(2,1)}, f32[4,1,1024]{2,1,0:T(1,128)}, f32[4,1,512]{2,1,0:T(1,128)}) custom-call(s32[8]{0:T(128)} %gather_fusion, s32[8]{0:T(128)} %and_select_fusion.4.group_ref, bf16[4,16,1024]{2,1,0:T(8,128)(2,1)} %get-tuple-element.202.ids_ref, bf16[6,256,128]{2,1,0:T(8,128)(2,1)} %get-tuple-element.203.refs_0_, ...), custom_call_target="tpu_custom_call" | custom-call | flops 2147483648 | bytes 2621440 | tf_op jit(solution)/shard_map/attend/pallas_call | solution.py:578
  124.8 9.8 %all-to-all-start.1 = ((bf16[8,128,256]{2,1,0:T(8,128)(2,1)}), bf16[8,128,256]{2,1,0:T(8,128)(2,1)S(1)}, u32[]{:S(2)}, u32[]{:S(2)}) async-start(bf16[8,128,256]{2,1,0:T(8,128)(2,1)} %get-tuple-element.223), calls=%async_computation.1 | async-start | bytes 1048576 | tf_op jit(solution)/shard_map/all_to_all | solution.py:1235
  137.7 17.9 %all-to-all-done.1 = bf16[8,128,256]{2,1,0:T(8,128)(2,1)S(1)} async-done(((bf16[8,128,256]{2,1,0:T(8,128)(2,1)}), bf16[8,128,256]{2,1,0:T(8,128)(2,1)S(1)}, u32[]{:S(2)}, u32[]{:S(2)}) %all-to-all-start.1) | async-done | bytes 524320 | tf_op jit(solution)/shard_map/all_to_all | solution.py:1235
  164.8 16.0 %all-to-all-done.2 = bf16[8,32,1152]{2,1,0:T(8,128)(2,1)S(1)} async-done(((bf16[8,32,1152]{2,1,0:T(8,128)(2,1)}), bf16[8,32,1152]{2,1,0:T(8,128)(2,1)S(1)}, u32[]{:S(2)}, u32[]{:S(2)}) %all-to-all-start.2) | async-done | bytes 589856 | tf_op jit(solution)/shard_map/all_to_all | solution.py:1235
  188.4 6.1 %collective-permute-done.26.refs_1_.refs_13_ = bf16[128,1152]{1,0:T(8,128)(2,1)S(1)} collective-permute-done((bf16[128,1152]{1,0:T(8,128)(2,1)}, bf16[128,1152]{1,0:T(8,128)(2,1)S(1)}, u32[]{:S(2)}, u32[]{:S(2)}) %collective-permute-start.26) | collective-permute-done | bytes 294944 | tf_op jit(solution)/shard_map/ppermute | solution.py:29
  202.1 4.6 collective-permute-done.28.refs_3_.refs_15_
  207.5 12.1 %expert_first.1 = (bf16[128,1024]{1,0:T(8,128)(2,1)}, bf16[128,1024]{1,0:T(8,128)(2,1)}, bf16[128,1024]{1,0:T(8,128)(2,1)}, bf16[128,1024]{1,0:T(8,128)(2,1)}, b...) custom-call(bf16[2,1,512]{2,1,0:T(2,128)(2,1)} %bitcast.107, ...), custom_call_target="tpu_custom_call" | custom-call | flops 4294967296 | bytes 8388608 | tf_op jit(solution)/shard_map/expert_first/pallas_call | solution.py:911
  223.8 5.4 %collective-permute-done.33 = bf16[128,1024]{1,0:T(8,128)(2,1)S(1)} collective-permute-done((bf16[128,1024]{1,0:T(8,128)(2,1)}, bf16[128,1024]{1,0:T(8,128)(2,1)S(1)}, u32[]{:S(2)}, u32[]{:S(2)}) %collective-permute-start.33) | collective-permute-done | bytes 262176 | tf_op jit(solution)/shard_map/ppermute | solution.py:29
  247.1 5.0 collective-permute-done.38.refs_5_
  260.8 20.6 %expert_second.1 = (bf16[128,1024]{1,0:T(8,128)(2,1)}, bf16[128,1024]{1,0:T(8,128)(2,1)}, bf16[128,1024]{1,0:T(8,128)(2,1)}, bf16[128,1024]{1,0:T(8,128)(2,1)}, ...) custom-call(s32[2]{0:T(128)} %pad_add_fusion.me_ref, ...), custom_call_target="tpu_custom_call" | custom-call | flops 8589934592 | bytes 12582912 | tf_op jit(solution)/shard_map/expert_second/pallas_call | solution.py:1011
  285.5 5.9 %weight_grads.4.refs_0_ = f32[1,2,1024,1024]{3,2,1,0:T(8,128)} custom-call(bf16[1024,1024]{1,0:T(8,128)(2,1)} %get-tuple-element.250.left_ref, bf16[2,1024,512]{2,1,0:T(8,128)(2,1)} %get-tuple-element.251.right_ref), custom_call_target="tpu_custom_call" | custom-call | flops 2147483648 | bytes 8388608 | tf_op jit(solution)/shard_map/weight_grads/pallas_call | solution.py:1139
  316.3 5.8 %weight_grads.5.refs_0_ = f32[1,2,1024,1024]{3,2,1,0:T(8,128)} custom-call(bf16[2,1024,512]{2,1,0:T(8,128)(2,1)} %get-tuple-element.246.left_ref, bf16[1024,1024]{1,0:T(8,128)(2,1)} %get-tuple-element.265.right_ref), custom_call_target="tpu_custom_call" | custom-call | flops 2147483648 | bytes 8388608 | tf_op jit(solution)/shard_map/weight_grads/pallas_call | solution.py:1139
  323.1 13.2 %expert_back.1 = (bf16[128,1152]{1,0:T(8,128)(2,1)}, bf16[128,1152]{1,0:T(8,128)(2,1)}, bf16[128,1152]{1,0:T(8,128)(2,1)}, bf16[128,1152]{1,0:T(8,128)(2,1)}, bf...) custom-call(bf16[1024,128]{1,0:T(8,128)(2,1)} %get-tuple-element.244, ...), custom_call_target="tpu_custom_call" | custom-call | flops 4294967296 | bytes 10485760 | tf_op jit(solution)/shard_map/expert_back/pallas_call | solution.py:1087
  340.4 4.8 collective-permute-done.57
  361.3 4.7 all-to-all-start.3
  366.7 6.0 %weight_grads.6 = f32[1,2,1024,1024]{3,2,1,0:T(8,128)} custom-call(bf16[1024,1024]{1,0:T(8,128)(2,1)} %get-tuple-element.228.left_ref, bf16[2,1024,512]{2,1,0:T(8,128)(2,1)} %get-tuple-element.290.right_ref, f32[1,2,1024,1024]{3,2,1,0:T(8,128)} %weight_grads.4.refs_0_), custom_call_target="tpu_custom_call", output_to_operand_aliasing={{}: (2, {})} | custom-call | flops 2147483648 | bytes 8388608 | tf_op jit(solution)/shard_map/weight_grads/pallas_call | solution.py:1139
  372.7 10.1 %all-to-all-done.3 = bf16[8,32,1152]{2,1,0:T(8,128)(2,1)S(1)} async-done(((bf16[8,32,1152]{2,1,0:T(8,128)(2,1)}), bf16[8,32,1152]{2,1,0:T(8,128)(2,1)S(1)}, u32[]{:S(2)}, u32[]{:S(2)}) %all-to-all-start.3) | async-done | bytes 589856 | tf_op jit(solution)/shard_map/all_to_all | solution.py:1235
  383.6 4.9 backward_rows.1
  395.3 5.8 %weight_grads.7 = f32[1,2,1024,1024]{3,2,1,0:T(8,128)} custom-call(bf16[2,1024,512]{2,1,0:T(8,128)(2,1)} %get-tuple-element.304.left_ref, bf16[1024,1024]{1,0:T(8,128)(2,1)} %get-tuple-element.306.right_ref, f32[1,2,1024,1024]{3,2,1,0:T(8,128)} %weight_grads.5.refs_0_), custom_call_target="tpu_custom_call", output_to_operand_aliasing={{}: (2, {})} | custom-call | flops 2147483648 | bytes 8388608 | tf_op jit(solution)/shard_map/weight_grads/pallas_call | solution.py:1139
  411.6 33.6 %attend_back.1 = (bf16[272,1024]{1,0:T(8,128)(2,1)}, bf16[272,1024]{1,0:T(8,128)(2,1)}, bf16[272,1024]{1,0:T(8,128)(2,1)}, bf16[272,1024]{1,0:T(8,128)(2,1)}, bf...) custom-call(s32[8]{0:T(128)} %gather_fusion, ...), custom_call_target="tpu_custom_call" | custom-call | flops 5368709120 | bytes 5242880 | tf_op jit(solution)/shard_map/attend_back/pallas_call | solution.py:725
  448.9 4.7 collective-permute-start.63
  456.0 7.0 %project_grads.1 = bf16[1024,384]{1,0:T(8,128)(2,1)} custom-call(s32[8]{0:T(128)} %gather_fusion, bf16[8,256,128]{2,1,0:T(8,128)(2,1)} %get-tuple-element.327.dq_ref, bf16[8,256,128]{2,1,0:T(8,128)(2,1)} %get-tuple-element.328.dk_ref, bf16[8,256,128]{2,1,0:T(8,128)(2,1)} %get-tuple-element.329.dv_ref, ...), custom_call_target="tpu_custom_call" | custom-call | flops 1610612736 | bytes 6553600 | tf_op jit(solution)/shard_map/project_grads/pallas_call | solution.py:784
  466.8 4.5 collective-permute-start.67
  477.6 4.6 collective-permute-done.69
  488.4 6.3 %collective-permute-start.73 = (bf16[272,1024]{1,0:T(8,128)(2,1)S(1)}, bf16[272,1024]{1,0:T(8,128)(2,1)S(1)}, u32[]{:S(2)}, u32[]{:S(2)}) collective-permute-start(bf16[272,1024]{1,0:T(8,128)(2,1)S(1)} %add_convert_fusion.1), channel_id=1, source_target_pairs={{0,2},{1,3},{2,4},{3,5},{4,6},{5,7},{8,10},{9,11},{10,12},{11,13},... | collective-permute-start | bytes 1671176 | tf_op jit(solution)/shard_map/ppermute | solution.py:1400
  495.7 7.4 %collective-permute-done.74 = bf16[272,1024]{1,0:T(8,128)(2,1)S(1)} collective-permute-done((bf16[272,1024]{1,0:T(8,128)(2,1)S(1)}, bf16[272,1024]{1,0:T(8,128)(2,1)S(1)}, u32[]{:S(2)}, u32[]{:S(2)}) %collective-permute-start.74) | collective-permute-done | bytes 557088 | tf_op jit(solution)/shard_map/ppermute | solution.py:1403
  (421 shorter events, 212.1 us)
Async XLA Ops:
  18.3 30.5 %all-to-all-start = ((bf16[8,32,1024]{2,1,0:T(8,128)(2,1)}), bf16[8,32,1024]{2,1,0:T(8,128)(2,1)S(1)}, u32[]{:S(2)}, u32[]{:S(2)}) async-start(bf16[8,32,1024]{2,1,0:T(8,128)(2,1)} %bitcast.8), calls=%async_computation | async-start | bytes 1048576 | tf_op jit(solution)/shard_map/all_to_all | solution.py:1235
  23.7 131.9 %all-gather.2.cloned.1.call-start = ((), (), s32[]{:S(2)}) async-start(), calls=%async_computation.8 | async-start | bytes 2162688 | tf_op jit(solution)/shard_map/all_gather | solution.py:1225
  24.1 24.7 %collective-permute-start.4 = (bf16[272,1024]{1,0:T(8,128)(2,1)S(1)}, bf16[272,1024]{1,0:T(8,128)(2,1)S(1)}, u32[]{:S(2)}, u32[]{:S(2)}) collective-permute-start(bf16[272,1024]{1,0:T(8,128)(2,1)S(1)} %maximum_maximum_fusion.refs_0_), channel_id=1, source_target_pairs={{0,2},{1,3},{2,4},{3,5},{4,6},{5,7},{8,10},{9,11},{10,12},{11,13},... | collective-permute-start | bytes 1671176 | tf_op jit(solution)/shard_map/ppermute | solution.py:1274
  28.1 20.6 %collective-permute-start.5 = (bf16[272,1024]{1,0:T(8,128)(2,1)S(1)}, bf16[272,1024]{1,0:T(8,128)(2,1)S(1)}, u32[]{:S(2)}, u32[]{:S(2)}) collective-permute-start(bf16[272,1024]{1,0:T(8,128)(2,1)S(1)} %maximum_maximum_fusion.refs_0_), channel_id=1, source_target_pairs={{2,0},{3,1},{4,2},{5,3},{6,4},{7,5},{10,8},{11,9},{12,10},{13,11},... | collective-permute-start | bytes 1671176 | tf_op jit(solution)/shard_map/ppermute | solution.py:1275
  29.5 13.9 %collective-permute-start.6 = (bf16[256,384]{1,0:T(8,128)(2,1)S(1)}, bf16[256,384]{1,0:T(8,128)(2,1)}, u32[]{:S(2)}, u32[]{:S(2)}) collective-permute-start(bf16[256,384]{1,0:T(8,128)(2,1)S(1)} %pad_maximum_fusion.1.refs_0_), channel_id=1, source_target_pairs={{0,8},{8,0},{16,24},{24,16},{1,9},{9,1},{17,25},{25,17},{2,10},{10... | collective-permute-start | bytes 589832 | tf_op jit(solution)/shard_map/ppermute | solution.py:29
  50.2 18.3 %collective-permute-start.13 = (bf16[272,1024]{1,0:T(8,128)(2,1)S(1)}, bf16[272,1024]{1,0:T(8,128)(2,1)}, u32[]{:S(2)}, u32[]{:S(2)}) collective-permute-start(bf16[272,1024]{1,0:T(8,128)(2,1)S(1)} %collective-permute-done.5.refs_2_), channel_id=1, source_target_pairs={{2,0},{3,1},{4,2},{5,3},{10,8},{11,9},{12,10},{13,11},{18,16},{19,... | collective-permute-start | bytes 1671176 | tf_op jit(solution)/shard_map/ppermute | solution.py:1275
  51.5 17.0 %collective-permute-start.15 = (bf16[272,1024]{1,0:T(8,128)(2,1)S(1)}, bf16[272,1024]{1,0:T(8,128)(2,1)}, u32[]{:S(2)}, u32[]{:S(2)}) collective-permute-start(bf16[272,1024]{1,0:T(8,128)(2,1)S(1)} %collective-permute-done.4.refs_9_), channel_id=1, source_target_pairs={{0,1},{1,0},{2,3},{3,2},{4,5},{5,4},{6,7},{7,6},{8,9},{9,8},{10,11... | collective-permute-start | bytes 1671176 | tf_op jit(solution)/shard_map/ppermute | solution.py:29
  51.6 17.0 %collective-permute-start.16 = (bf16[272,1024]{1,0:T(8,128)(2,1)S(1)}, bf16[272,1024]{1,0:T(8,128)(2,1)}, u32[]{:S(2)}, u32[]{:S(2)}) collective-permute-start(bf16[272,1024]{1,0:T(8,128)(2,1)S(1)} %collective-permute-done.5.refs_2_), channel_id=1, source_target_pairs={{0,1},{1,0},{2,3},{3,2},{4,5},{5,4},{6,7},{7,6},{8,9},{9,8},{10,11... | collective-permute-start | bytes 1671176 | tf_op jit(solution)/shard_map/ppermute | solution.py:29
  52.1 18.5 %collective-permute-start.21 = (bf16[256,1024]{1,0:T(8,128)(2,1)S(1)}, bf16[256,1024]{1,0:T(8,128)(2,1)}, u32[]{:S(2)}, u32[]{:S(2)}) collective-permute-start(bf16[256,1024]{1,0:T(8,128)(2,1)S(1)} %bitcast.76), channel_id=1, source_target_pairs={{0,8},{8,0},{16,24},{24,16},{1,9},{9,1},{17,25},{25,17},{2,10},{10... | collective-permute-start | bytes 1572872 | tf_op jit(solution)/shard_map/ppermute | solution.py:29
  52.6 18.6 %collective-permute-start.22 = (bf16[256,1024]{1,0:T(8,128)(2,1)S(1)}, bf16[256,1024]{1,0:T(8,128)(2,1)}, u32[]{:S(2)}, u32[]{:S(2)}) collective-permute-start(bf16[256,1024]{1,0:T(8,128)(2,1)S(1)} %bitcast.77), channel_id=1, source_target_pairs={{0,16},{8,24},{16,0},{24,8},{1,17},{9,25},{17,1},{25,9},{2,18},{10... | collective-permute-start | bytes 1572872 | tf_op jit(solution)/shard_map/ppermute | solution.py:29
  68.6 17.5 %collective-permute-start.17 = (bf16[272,1024]{1,0:T(8,128)(2,1)S(1)}, bf16[272,1024]{1,0:T(8,128)(2,1)S(1)}, u32[]{:S(2)}, u32[]{:S(2)}) collective-permute-start(bf16[272,1024]{1,0:T(8,128)(2,1)S(1)} %collective-permute-done.12.refs_5_), channel_id=1, source_target_pairs={{4,6},{5,7},{12,14},{13,15},{20,22},{21,23},{28,30},{29,31}} | collective-permute-start | bytes 1671176 | tf_op jit(solution)/shard_map/ppermute | solution.py:1274
  69.3 17.2 %collective-permute-start.19 = (bf16[272,1024]{1,0:T(8,128)(2,1)S(1)}, bf16[272,1024]{1,0:T(8,128)(2,1)S(1)}, u32[]{:S(2)}, u32[]{:S(2)}) collective-permute-start(bf16[272,1024]{1,0:T(8,128)(2,1)S(1)} %collective-permute-done.12.refs_5_), channel_id=1, source_target_pairs={{0,1},{1,0},{2,3},{3,2},{4,5},{5,4},{6,7},{7,6},{8,9},{9,8},{10,11... | collective-permute-start | bytes 1671176 | tf_op jit(solution)/shard_map/ppermute | solution.py:29
  69.3 17.1 %collective-permute-start.18 = (bf16[272,1024]{1,0:T(8,128)(2,1)}, bf16[272,1024]{1,0:T(8,128)(2,1)S(1)}, u32[]{:S(2)}, u32[]{:S(2)}) collective-permute-start(bf16[272,1024]{1,0:T(8,128)(2,1)} %collective-permute-done.13.refs_4_), channel_id=1, source_target_pairs={{2,0},{3,1},{10,8},{11,9},{18,16},{19,17},{26,24},{27,25}} | collective-permute-start | bytes 1671176 | tf_op jit(solution)/shard_map/ppermute | solution.py:1275
  70.7 17.5 %collective-permute-start.20 = (bf16[272,1024]{1,0:T(8,128)(2,1)}, bf16[272,1024]{1,0:T(8,128)(2,1)}, u32[]{:S(2)}, u32[]{:S(2)}) collective-permute-start(bf16[272,1024]{1,0:T(8,128)(2,1)} %collective-permute-done.13.refs_4_), channel_id=1, source_target_pairs={{0,1},{1,0},{2,3},{3,2},{4,5},{5,4},{6,7},{7,6},{8,9},{9,8},{10,11... | collective-permute-start | bytes 1671176 | tf_op jit(solution)/shard_map/ppermute | solution.py:29
  71.2 14.8 %collective-permute-start.23 = (bf16[256,1024]{1,0:T(8,128)(2,1)S(1)}, bf16[256,1024]{1,0:T(8,128)(2,1)S(1)}, u32[]{:S(2)}, u32[]{:S(2)}) collective-permute-start(bf16[256,1024]{1,0:T(8,128)(2,1)S(1)} %bitcast.78), channel_id=1, source_target_pairs={{0,24},{8,16},{16,8},{24,0},{1,25},{9,17},{17,9},{25,1},{2,26},{10... | collective-permute-start | bytes 1572872 | tf_op jit(solution)/shard_map/ppermute | solution.py:29
  124.8 30.8 %all-to-all-start.1 = ((bf16[8,128,256]{2,1,0:T(8,128)(2,1)}), bf16[8,128,256]{2,1,0:T(8,128)(2,1)S(1)}, u32[]{:S(2)}, u32[]{:S(2)}) async-start(bf16[8,128,256]{2,1,0:T(8,128)(2,1)} %get-tuple-element.223), calls=%async_computation.1 | async-start | bytes 1048576 | tf_op jit(solution)/shard_map/all_to_all | solution.py:1235
  160.4 20.4 %all-to-all-start.2 = ((bf16[8,32,1152]{2,1,0:T(8,128)(2,1)}), bf16[8,32,1152]{2,1,0:T(8,128)(2,1)S(1)}, u32[]{:S(2)}, u32[]{:S(2)}) async-start(bf16[8,32,1152]{2,1,0:T(8,128)(2,1)} %bitcast.93), calls=%async_computation.2 | async-start | bytes 1179648 | tf_op jit(solution)/shard_map/all_to_all | solution.py:1235
  164.1 237.0 %reduce-scatter.3.cloned.1.call-start = ((), (), s32[]{:S(2)}) async-start(), calls=%async_computation.9 | async-start | bytes 2621440 | tf_op jit(solution)/shard_map/reduce_scatter | solution.py:1370
  187.2 14.9 %collective-permute-start.27 = (bf16[128,1152]{1,0:T(8,128)(2,1)}, bf16[128,1152]{1,0:T(8,128)(2,1)S(1)}, u32[]{:S(2)}, u32[]{:S(2)}) collective-permute-start(bf16[128,1152]{1,0:T(8,128)(2,1)} %get-tuple-element.226.refs_0_.refs_12_), channel_id=1, source_target_pairs={{0,16},{8,24},{16,0},{24,8},{1,17},{9,25},{17,1},{25,9},{2,18},{10... | collective-permute-start | bytes 884744 | tf_op jit(solution)/shard_map/ppermute | solution.py:29
  187.6 14.5 %collective-permute-start.29 = (bf16[128,1152]{1,0:T(8,128)(2,1)}, bf16[128,1152]{1,0:T(8,128)(2,1)S(1)}, u32[]{:S(2)}, u32[]{:S(2)}) collective-permute-start(bf16[128,1152]{1,0:T(8,128)(2,1)} %get-tuple-element.227.refs_4_.refs_16_), channel_id=1, source_target_pairs={{0,8},{8,0},{16,24},{24,16},{1,9},{9,1},{17,25},{25,17},{2,10},{10... | collective-permute-start | bytes 884744 | tf_op jit(solution)/shard_map/ppermute | solution.py:29
  282.3 14.7 %collective-permute-start.44 = (bf16[128,1024]{1,0:T(8,128)(2,1)}, bf16[128,1024]{1,0:T(8,128)(2,1)S(1)}, u32[]{:S(2)}, u32[]{:S(2)}) collective-permute-start(bf16[128,1024]{1,0:T(8,128)(2,1)} %get-tuple-element.253), channel_id=1, source_target_pairs={{0,8},{8,0},{16,24},{24,16},{1,9},{9,1},{17,25},{25,17},{2,10},{10... | collective-permute-start | bytes 786440 | tf_op jit(solution)/shard_map/ppermute | solution.py:29
  283.5 14.3 %collective-permute-start.47 = (bf16[128,1024]{1,0:T(8,128)(2,1)}, bf16[128,1024]{1,0:T(8,128)(2,1)S(1)}, u32[]{:S(2)}, u32[]{:S(2)}) collective-permute-start(bf16[128,1024]{1,0:T(8,128)(2,1)} %get-tuple-element.257), channel_id=1, source_target_pairs={{0,16},{8,24},{16,0},{24,8},{1,17},{9,25},{17,1},{25,9},{2,18},{10... | collective-permute-start | bytes 786440 | tf_op jit(solution)/shard_map/ppermute | solution.py:29
  361.3 21.5 %all-to-all-start.3 = ((bf16[8,32,1152]{2,1,0:T(8,128)(2,1)}), bf16[8,32,1152]{2,1,0:T(8,128)(2,1)S(1)}, u32[]{:S(2)}, u32[]{:S(2)}) async-start(bf16[8,32,1152]{2,1,0:T(8,128)(2,1)} %bitcast.94), calls=%async_computation.3 | async-start | bytes 1179648 | tf_op jit(solution)/shard_map/all_to_all | solution.py:1235
  388.5 18.8 %all-to-all-start.4 = ((bf16[8,128,256]{2,1,0:T(8,128)(2,1)}), bf16[8,128,256]{2,1,0:T(8,128)(2,1)S(1)}, u32[]{:S(2)}, u32[]{:S(2)}) async-start(bf16[8,128,256]{2,1,0:T(8,128)(2,1)} %bitcast.95), calls=%async_computation.5 | async-start | bytes 1048576 | tf_op jit(solution)/shard_map/all_to_all | solution.py:1235
  392.0 72.9 %reduce-scatter.5.cloned.1.call-start = ((), (), s32[]{:S(2)}) async-start(), calls=%async_computation.10 | async-start | bytes 2359296 | tf_op jit(solution)/shard_map/reduce_scatter | solution.py:1387
  408.1 37.2 %all-to-all-start.5 = ((bf16[8,32,1024]{2,1,0:T(8,128)(2,1)}), bf16[8,32,1024]{2,1,0:T(8,128)(2,1)S(1)}, u32[]{:S(2)}, u32[]{:S(2)}) async-start(bf16[8,32,1024]{2,1,0:T(8,128)(2,1)} %bitcast.34), calls=%async_computation.6 | async-start | bytes 1048576 | tf_op jit(solution)/shard_map/all_to_all | solution.py:1235
  446.0 18.9 %collective-permute-start.66 = (bf16[272,1024]{1,0:T(8,128)(2,1)}, bf16[272,1024]{1,0:T(8,128)(2,1)}, u32[]{:S(2)}, u32[]{:S(2)}) collective-permute-start(bf16[272,1024]{1,0:T(8,128)(2,1)} %get-tuple-element.333), channel_id=1, source_target_pairs={{0,1},{1,0},{2,3},{3,2},{4,5},{5,4},{6,7},{7,6},{8,9},{9,8},{10,11... | collective-permute-start | bytes 1671176 | tf_op jit(solution)/shard_map/ppermute | solution.py:29
  448.9 16.1 %collective-permute-start.63 = (bf16[272,1024]{1,0:T(8,128)(2,1)S(1)}, bf16[272,1024]{1,0:T(8,128)(2,1)}, u32[]{:S(2)}, u32[]{:S(2)}) collective-permute-start(bf16[272,1024]{1,0:T(8,128)(2,1)S(1)} %add_convert_fusion.5), channel_id=1, source_target_pairs={{0,2},{1,3},{8,10},{9,11},{16,18},{17,19},{24,26},{25,27}} | collective-permute-start | bytes 1671176 | tf_op jit(solution)/shard_map/ppermute | solution.py:1400
  466.8 19.7 %collective-permute-start.67 = (bf16[272,1024]{1,0:T(8,128)(2,1)S(1)}, bf16[272,1024]{1,0:T(8,128)(2,1)S(1)}, u32[]{:S(2)}, u32[]{:S(2)}) collective-permute-start(bf16[272,1024]{1,0:T(8,128)(2,1)S(1)} %get-tuple-element.388), channel_id=1, source_target_pairs={{0,2},{1,3},{2,4},{3,5},{8,10},{9,11},{10,12},{11,13},{16,18},{17,... | collective-permute-start | bytes 1671176 | tf_op jit(solution)/shard_map/ppermute | solution.py:1400
  471.4 15.2 %collective-permute-start.68 = (bf16[272,1024]{1,0:T(8,128)(2,1)S(1)}, bf16[272,1024]{1,0:T(8,128)(2,1)S(1)}, u32[]{:S(2)}, u32[]{:S(2)}) collective-permute-start(bf16[272,1024]{1,0:T(8,128)(2,1)S(1)} %get-tuple-element.387), channel_id=1, source_target_pairs={{4,2},{5,3},{6,4},{7,5},{12,10},{13,11},{14,12},{15,13},{20,18},{2... | collective-permute-start | bytes 1671176 | tf_op jit(solution)/shard_map/ppermute | solution.py:1403
  486.8 16.4 %collective-permute-start.74 = (bf16[272,1024]{1,0:T(8,128)(2,1)S(1)}, bf16[272,1024]{1,0:T(8,128)(2,1)S(1)}, u32[]{:S(2)}, u32[]{:S(2)}) collective-permute-start(bf16[272,1024]{1,0:T(8,128)(2,1)S(1)} %add_convert_fusion), channel_id=1, source_target_pairs={{2,0},{3,1},{4,2},{5,3},{6,4},{7,5},{10,8},{11,9},{12,10},{13,11},... | collective-permute-start | bytes 1671176 | tf_op jit(solution)/shard_map/ppermute | solution.py:1403
  488.4 16.1 %collective-permute-start.73 = (bf16[272,1024]{1,0:T(8,128)(2,1)S(1)}, bf16[272,1024]{1,0:T(8,128)(2,1)S(1)}, u32[]{:S(2)}, u32[]{:S(2)}) collective-permute-start(bf16[272,1024]{1,0:T(8,128)(2,1)S(1)} %add_convert_fusion.1), channel_id=1, source_target_pairs={{0,2},{1,3},{2,4},{3,5},{4,6},{5,7},{8,10},{9,11},{10,12},{11,13},... | collective-permute-start | bytes 1671176 | tf_op jit(solution)/shard_map/ppermute | solution.py:1400
  (131 other events, 1313.2 us)
Sparse Core Ops, SparseCore 0:
  88.3 64.8 all-gather.1
  356.6 35.0 reduce-scatter.2
  407.5 38.4 reduce-scatter.4

commit v3 on v2

--- a/solution.py
+++ b/solution.py
@@ -33,23 +33,24 @@
     return list(range(size.bit_length() - 1))
 
 
-def gather_path(value, axis, size, bits):
-    held = {0: value}
+def gather_path(values, axis, size, bits, done=()):
+    if not done:
+        values = [values]
+    held = dict(zip([0] + [1 << bit for bit in done], values))
     for bit in bits:
         held.update({m | (1 << bit): send_xor(v, axis, size, 1 << bit) for m, v in list(held.items())})
-    return [held[m] for m in range(size)]
+    return [held[m] for m in sorted(held)]
 
 
 def scatter_path(blocks, axis, size, bits):
-    held = dict(enumerate(blocks))
-    for bit in bits[:-1]:
+    held = {m: [v] for m, v in enumerate(blocks)}
+    for bit in bits:
         leaving = {m: v for m, v in held.items() if (m >> bit) & 1}
         held = {m: v for m, v in held.items() if not (m >> bit) & 1}
         for m, v in leaving.items():
-            keep = m & ~(1 << bit)
-            held[keep] = add_low(held[keep], send_xor(v, axis, size, 1 << bit))
-    last = 1 << bits[-1]
-    return [held[0], send_xor(held[last], axis, size, last)]
+            total = v[0] if len(v) == 1 else sum(n.astype(F32) for n in v).astype(BF)
+            held[m & ~(1 << bit)].append(send_xor(total, axis, size, 1 << bit))
+    return held[0]
 
 
 def direct_gather(value, axis, size):
@@ -96,8 +97,7 @@
 
 
 def col_scatter(blocks, size):
-    mine, last = scatter_path(blocks, "col", size, bits_of(size))
-    return mine.astype(F32) + last.astype(F32)
+    return sum(v.astype(F32) for v in scatter_path(blocks, "col", size, bits_of(size)))
 
 
 def layer_stats(stream):
@@ -143,27 +143,34 @@
         copy.wait()
 
 
-def arrange_kernel(count, rows, me_ref, *refs):
-    out_ref = refs[count]
+def arrange_kernel(count, me_ref, *refs):
+    outs, rest = refs[count:-1], refs[-1]
+    rows = outs[0].shape[0] // count
     for m in range(count):
-        at = pl.ds(pl.multiple_of((me_ref[0] ^ m) * rows, rows), rows)
-        out_ref[at, :] = refs[m][:rows, :]
-
-
-def arrange_rows(pieces, rows, me):
+        owner = me_ref[0] ^ m
+        at = pl.ds(pl.multiple_of(owner * rows, rows), rows)
+        done = 0
+        for out in outs:
+            out[at, :] = refs[m][:rows, done : done + out.shape[1]]
+            done += out.shape[1]
+        rest[owner] = refs[m][rows:, :]
+
+
+def arrange_rows(pieces, rows, widths, me):
     count = len(pieces)
-    cols = pieces[0].shape[1]
+    kind = pieces[0].dtype
     return pl.pallas_call(
-        functools.partial(arrange_kernel, count, rows),
+        functools.partial(arrange_kernel, count),
         in_specs=[SMEM] + [VMEM] * count,
-        out_specs=VMEM,
-        out_shape=shape((count * rows, cols), pieces[0].dtype),
+        out_specs=[VMEM] * (len(widths) + 1),
+        out_shape=[shape((count * rows, w), kind) for w in widths]
+        + [shape((count, pieces[0].shape[0] - rows, pieces[0].shape[1]), kind)],
         name="arrange_rows",
     )(me, *pieces)
 
 
 def tile_rows(tiles_ref, block):
-    return jnp.concatenate([tiles_ref[block, col] for col in range(tiles_ref.shape[1])], axis=1)
+    return jnp.concatenate([tiles_ref[col, block] for col in range(tiles_ref.shape[0])], axis=1)
 
 
 def scalar_lanes(values):
@@ -172,8 +179,11 @@
     return jnp.where(lane == 0, high, jnp.where(lane == 1, values - high, 0.0)).astype(BF)
 
 
-def forward_kernel(tiles_ref, tokens_ref, ctx_ref, cent_ref, onehot_ref, route_ref, residual_ref, gate_ref, moved_ref):
-    rows_n, unused, part, unused = tiles_ref.shape
+def forward_kernel(total, me_ref, tiles_ref, tokens_ref, cent_ref, onehot_ref, route_ref, *refs):
+    pieces, refs = refs[:total], refs[total:]
+    moved, (ctx_ref, residual_ref, gate_ref, sent) = refs[:total], refs[total:]
+    unused, rows_n, part, unused = tiles_ref.shape
+    place_pieces(pieces, me_ref, ctx_ref)
     held = tokens_ref[...].astype(F32)
     for n in range(rows_n):
         held = held + lax.dot_general(
@@ -187,27 +197,36 @@
     cent_rows = dot(onehot_ref[...], cent_ref[...])
     gate = jax.nn.sigmoid(jnp.sum(shared.astype(F32) * cent_rows, axis=1, keepdims=True))
     gate_ref[...] = gate
-    sent = jnp.concatenate([shared, scalar_lanes(gate)], axis=1)
-    moved_ref[...] = dot(route_ref[...], sent).astype(BF)
-
-
-def forward_rows(ctx, tiles, tokens, cent, onehot, route):
+    leaving = jnp.concatenate([shared, scalar_lanes(gate)], axis=1)
+    sent[...] = dot(route_ref[...], leaving).astype(BF)
+    slot = moved[0].shape[0]
+    for m in range(total):
+        moved[m][...] = sent[pl.ds(pl.multiple_of((me_ref[1] ^ m) * slot, slot), slot), :]
+
+
+def forward_rows(pieces, tiles, tokens, cent, onehot, route, me):
+    total = len(pieces)
     tok, width = tokens.shape
-    return pl.pallas_call(
-        forward_kernel,
-        in_specs=[VMEM] * 6,
-        out_specs=[VMEM] * 3,
-        out_shape=[shape((tok, width), F32), shape((tok, 1), F32), shape((tok, width + LANES), BF)],
+    out = pl.pallas_call(
+        functools.partial(forward_kernel, total),
+        in_specs=[SMEM] + [VMEM] * (5 + total),
+        out_specs=[VMEM] * (total + 3),
+        out_shape=[shape((tok // total, width + LANES), BF)] * total
+        + [shape((width, tok), BF), shape((tok, width), F32), shape((tok, 1), F32)],
+        scratch_shapes=[pltpu.VMEM((tok, width + LANES), BF)],
         cost_estimate=pl.CostEstimate(
             flops=3 * tok * width * width, bytes_accessed=2 * width * width + 8 * tok * width, transcendentals=0
         ),
         name="forward_rows",
-    )(tiles, tokens, ctx, cent, onehot, route)
-
-
-def enter_kernel(experts_ref, cot_ref, rows_ref, stream_ref, grad_ref, first_ref, second_ref):
+    )(me, tiles, tokens, cent, onehot, route, *pieces)
+    return out[:total], *out[total:]
+
+
+def enter_kernel(total, me_ref, experts_ref, cot_ref, *refs):
+    pieces, (stream_ref, grad_ref, first_ref, second_ref, rows_ref) = refs[:total], refs[total:]
     width = stream_ref.shape[1]
     half = first_ref.shape[0]
+    place_pieces(pieces, me_ref, rows_ref)
     stream = rows_ref[:, :width]
     lanes = rows_ref[:, width:]
     gate = jnp.sum(lanes.astype(F32), axis=1, keepdims=True)
@@ -221,28 +240,35 @@
     grad_ref[...] = (cot_ref[...].astype(F32) * gate).astype(BF)
 
 
-def enter_expert(rows, experts, cot):
+def enter_expert(pieces, experts, cot, me):
+    total = len(pieces)
     tok, width = cot.shape
     wide = (tok // 2, width + LANES)
     return pl.pallas_call(
-        enter_kernel,
-        in_specs=[VMEM] * 3,
+        functools.partial(enter_kernel, total),
+        in_specs=[SMEM] + [VMEM] * (2 + total),
         out_specs=[VMEM] * 4,
         out_shape=[shape((tok, width), BF)] * 2 + [shape(wide, BF)] * 2,
+        scratch_shapes=[pltpu.VMEM((tok, width + LANES), BF)],
         cost_estimate=pl.CostEstimate(flops=20 * tok * width, bytes_accessed=10 * tok * width, transcendentals=0),
         name="enter_expert",
-    )(experts, cot, rows)
+    )(me, experts, cot, *pieces)
+
+
+def add_up(refs, lanes):
+    return sum(ref[:, lanes].astype(F32) for ref in refs)
+
+
+def halves_of(refs):
+    return refs[: len(refs) // 2], refs[len(refs) // 2 :]
 
 
 def between_kernel(experts_ref, stream_ref, *refs):
-    first_own, first_more, second_own, second_more, out_ref, first_ref, second_ref = refs
+    sums, (out_ref, first_ref, second_ref) = refs[:-3], refs[-3:]
     half = first_ref.shape[0]
-    for n, (own, more, low) in enumerate(
-        ((first_own, first_more, first_ref), (second_own, second_more, second_ref))
-    ):
+    for n, (parts, low) in enumerate(zip(halves_of(sums), (first_ref, second_ref))):
         at = slice(n * half, (n + 1) * half)
-        branch = own[...].astype(F32) + more[...].astype(F32)
-        stream = stream_ref[at, :].astype(F32) + branch + experts_ref[4:5]
+        stream = stream_ref[at, :].astype(F32) + add_up(parts, slice(None)) + experts_ref[4:5]
         out_ref[at, :] = stream
         unit_rows, unused = layer_stats(stream)
         low[...] = (unit_rows * experts_ref[1:2] + experts_ref[3:4]).astype(BF)
@@ -252,7 +278,7 @@
     tok, width = stream.shape
     return pl.pallas_call(
         between_kernel,
-        in_specs=[VMEM] * 6,
+        in_specs=[VMEM] * (2 + len(sums)),
         out_specs=[VMEM] * 3,
         out_shape=[shape((tok, width), F32)] + [shape((tok // 2, width), BF)] * 2,
         cost_estimate=pl.CostEstimate(flops=20 * tok * width, bytes_accessed=12 * tok * width, transcendentals=0),
@@ -260,12 +286,12 @@
     )(experts, stream, *sums)
 
 
-def norm_grads(half, sub, experts_ref, stream_ref, upper_ref, pairs, sums_ref):
+def norm_grads(half, sub, experts_ref, stream_ref, upper_ref, sums, sums_ref):
     width = stream_ref.shape[1]
     grads = []
-    for n, (own, more) in enumerate(pairs):
+    for n, parts in enumerate(halves_of(sums)):
         at = slice(n * half, (n + 1) * half)
-        grad_normed = own[:, :width].astype(F32) + more[:, :width].astype(F32)
+        grad_normed = add_up(parts, slice(0, width))
         unit_rows, inv_root = layer_stats(stream_ref[at, :].astype(F32))
         upper = upper_ref[at, :].astype(F32)
         for row, values in enumerate((grad_normed * unit_rows, grad_normed, upper)):
@@ -279,10 +305,9 @@
 
 
 def middle_back_kernel(experts_ref, stream_ref, upper_ref, *refs):
-    first_own, first_more, second_own, second_more, out_ref, first_ref, second_ref, sums_ref = refs
+    sums, (out_ref, first_ref, second_ref, sums_ref) = refs[:-4], refs[-4:]
     half = first_ref.shape[0]
-    pairs = ((first_own, first_more), (second_own, second_more))
-    grads = norm_grads(half, 1, experts_ref, stream_ref, upper_ref, pairs, sums_ref)
+    grads = norm_grads(half, 1, experts_ref, stream_ref, upper_ref, sums, sums_ref)
     for n, low in enumerate((first_ref, second_ref)):
         out_ref[n * half : (n + 1) * half, :] = grads[n]
         low[...] = grads[n].astype(BF)
@@ -292,7 +317,7 @@
     tok, width = stream.shape
     return pl.pallas_call(
         middle_back_kernel,
-        in_specs=[VMEM] * 7,
+        in_specs=[VMEM] * (3 + len(sums)),
         out_specs=[VMEM] * 4,
         out_shape=[shape((tok, width), F32)] + [shape((tok // 2, width), BF)] * 2 + [shape((3, width), F32)],
         cost_estimate=pl.CostEstimate(flops=40 * tok * width, bytes_accessed=16 * tok * width, transcendentals=0),
@@ -300,35 +325,48 @@
     )(experts, stream, upper, *sums)
 
 
-def leave_back_kernel(experts_ref, stream_ref, upper_ref, cot_ref, later_ref, first_own, first_more, second_own, second_more, out_ref, sums_ref):
+def leave_back_kernel(total, me_ref, experts_ref, stream_ref, upper_ref, cot_ref, later_ref, *refs):
+    sums, refs = refs[: -total - 2], refs[-total - 2 :]
+    outs, sums_ref, held = refs[:total], refs[total], refs[total + 1]
     width = stream_ref.shape[1]
-    half = first_own.shape[0]
-    pairs = ((first_own, first_more), (second_own, second_more))
-    grads = norm_grads(half, 0, experts_ref, stream_ref, upper_ref, pairs, sums_ref)
-    for n, (own, more) in enumerate(pairs):
+    slot = outs[0].shape[0]
+    half = stream_ref.shape[0] // 2
+    grads = norm_grads(half, 0, experts_ref, stream_ref, upper_ref, sums, sums_ref)
+    for n, parts in enumerate(halves_of(sums)):
         at = slice(n * half, (n + 1) * half)
-        lanes = own[:, width:].astype(F32) + more[:, width:].astype(F32)
         kept = cot_ref[at, :].astype(F32) * (later_ref[at, :] + experts_ref[5:6])
-        logit = jnp.sum(lanes, axis=1, keepdims=True) + jnp.sum(kept, axis=1, keepdims=True)
-        out_ref[at, :width] = grads[n].astype(BF)
-        out_ref[at, width:] = scalar_lanes(logit)
-
-
-def leave_back(experts, stream, upper, cot, later, sums):
+        logit = jnp.sum(add_up(parts, slice(width, None)), axis=1, keepdims=True)
+        logit = logit + jnp.sum(kept, axis=1, keepdims=True)
+        held[at, :width] = grads[n].astype(BF)
+        held[at, width:] = scalar_lanes(logit)
+    for m in range(total):
+        outs[m][...] = held[pl.ds(pl.multiple_of((me_ref[1] ^ m) * slot, slot), slot), :]
+
+
+def leave_back(experts, stream, upper, cot, later, sums, me, total):
     tok, width = stream.shape
     return pl.pallas_call(
-        leave_back_kernel,
-        in_specs=[VMEM] * 9,
-        out_specs=[VMEM] * 2,
-        out_shape=[shape((tok, width + LANES), BF), shape((3, width), F32)],
+        functools.partial(leave_back_kernel, total),
+        in_specs=[SMEM] + [VMEM] * (5 + len(sums)),
+        out_specs=[VMEM] * (total + 1),
+        out_shape=[shape((tok // total, width + LANES), BF)] * total + [shape((3, width), F32)],
+        scratch_shapes=[pltpu.VMEM((tok, width + LANES), BF)],
         cost_estimate=pl.CostEstimate(flops=40 * tok * width, bytes_accessed=20 * tok * width, transcendentals=0),
         name="leave_back",
-    )(experts, stream, upper, cot, later, *sums)
-
-
-def backward_kernel(tiles_ref, unroute_ref, back_ref, cot_ref, cent_ref, onehot_ref, turned_ref, gate_ref, residual_ref, out_ref, low_ref, cent_out, ctx_ref):
+    )(me, experts, stream, upper, cot, later, *sums)
+
+
+def place_pieces(pieces, me_ref, held):
+    rows = pieces[0].shape[0]
+    for m, piece in enumerate(pieces):
+        held[pl.ds(pl.multiple_of((me_ref[1] ^ m) * rows, rows), rows), :] = piece[...]
+
+
+def backward_kernel(total, me_ref, tiles_ref, unroute_ref, cot_ref, cent_ref, onehot_ref, turned_ref, gate_ref, residual_ref, *refs):
+    pieces, (out_ref, low_ref, cent_out, ctx_ref, back_ref) = refs[:total], refs[total:]
+    place_pieces(pieces, me_ref, back_ref)
     width = cot_ref.shape[1]
-    rows_n, unused, part, unused = tiles_ref.shape
+    unused, rows_n, part, unused = tiles_ref.shape
     back = dot(unroute_ref[...], back_ref[...])
     gate = gate_ref[...]
     grad_logit = jnp.sum(back[:, width:], axis=1, keepdims=True) * gate * (1.0 - gate)
@@ -348,11 +386,12 @@
     )
 
 
-def backward_rows(back, tiles, unroute, cot, cent, onehot, gate, residual):
+def backward_rows(pieces, tiles, unroute, cot, cent, onehot, gate, residual, me):
     tok, width = cot.shape
+    total = len(pieces)
     return pl.pallas_call(
-        backward_kernel,
-        in_specs=[VMEM] * 9,
+        functools.partial(backward_kernel, total),
+        in_specs=[SMEM] + [VMEM] * (8 + total),
         out_specs=[VMEM] * 4,
         out_shape=[
             shape((tok, width), F32),
@@ -360,11 +399,12 @@
             shape((LANES, width), F32),
             shape((width, tok), BF),
         ],
+        scratch_shapes=[pltpu.VMEM((tok, width + LANES), BF)],
         cost_estimate=pl.CostEstimate(
             flops=3 * tok * width * width, bytes_accessed=2 * width * width + 12 * tok * width, transcendentals=0
         ),
         name="backward_rows",
-    )(tiles, unroute, back, cot, cent, onehot, onehot.T, gate, residual)
+    )(me, tiles, unroute, cot, cent, onehot, onehot.T, gate, residual, *pieces)
 
 
 def finish_kernel(stream_ref, branch_ref, experts_ref, out_ref):
@@ -381,38 +421,16 @@
     )(stream, branch, experts)
 
 
-def project_kernel(scale, sources, rows, lead, gain_ref, shift_ref, w_ref, *refs):
-    count = len(sources)
-    total = sum(sources)
-    blocks, refs = refs[:total], refs[total:]
-    outs, refs = refs[:6], refs[6:]
-    if lead:
-        packets_ref, gain_out, shift_out, refs = *refs[:3], refs[3:]
+def project_kernel(scale, count, gain_ref, shift_ref, w_ref, *refs):
+    blocks, outs, refs = refs[:count], refs[count : count + 6], refs[count + 6 :]
     x_all, held, sems, out_sems = refs[0], refs[1:7], refs[7], refs[8]
     fw = w_ref.shape[1] // 3
     copies = begin([(b, x_all.at[n]) for n, b in enumerate(blocks)], sems)
-    starts = [sum(sources[:n]) for n in range(count)]
-
-    def merged(n, at):
-        return sum(x_all[starts[n] + i, at, :].astype(F32) for i in range(sources[n]))
-
-    if lead:
-        finish(copies)
-        packets = [merged(n, slice(rows, rows + 16)) for n in lead]
-        for n, value in enumerate(packets):
-            packets_ref[n] = value.astype(BF)
-        value = sum(packets)
-        gain, shift = value[0:1], value[1:2]
-        gain_out[...] = gain
-        shift_out[...] = shift
-    else:
-        gain, shift = gain_ref[...], shift_ref[...]
     leaving = []
     for n in range(count):
-        if not lead:
-            finish(copies[starts[n] : starts[n] + sources[n]])
-        unit_rows, unused = layer_stats(merged(n, slice(0, rows)))
-        normed = (unit_rows * gain + shift).astype(BF)
+        copies[n].wait()
+        unit_rows, unused = layer_stats(x_all[n].astype(F32))
+        normed = (unit_rows * gain_ref[...] + shift_ref[...]).astype(BF)
         held[0][n] = normed
         out = dot(normed, w_ref[...])
         keys = out[:, fw : 2 * fw]
@@ -428,29 +446,26 @@
     finish(leaving)
 
 
-def project(blocks, gain, shift, w, rows, scale, lead=()):
-    sources = [len(b) for b in blocks]
-    flat = [v for b in blocks for v in b]
+def project(blocks, gain, shift, w, scale):
     count = len(blocks)
-    width = flat[0].shape[1]
+    rows, width = blocks[0].shape
     fw = w.shape[1] // 3
     kinds = [(count, rows, width)] + [(count, rows, fw)] * 3 + [(count, fw, rows)] * 2
-    more = [shape((len(lead), 16, width), BF)] + [shape((1, width), F32)] * 2 if lead else []
     return pl.pallas_call(
-        functools.partial(project_kernel, scale, sources, rows, lead),
-        in_specs=[VMEM] * 3 + [ANY] * len(flat),
-        out_specs=[ANY] * 6 + [VMEM] * len(more),
-        out_shape=[shape(k, BF) for k in kinds] + more,
-        scratch_shapes=[pltpu.VMEM((len(flat),) + flat[0].shape, BF)]
+        functools.partial(project_kernel, scale, count),
+        in_specs=[VMEM] * 3 + [ANY] * count,
+        out_specs=[ANY] * 6,
+        out_shape=[shape(k, BF) for k in kinds],
+        scratch_shapes=[pltpu.VMEM((count, rows, width), BF)]
         + [pltpu.VMEM(k, BF) for k in kinds]
-        + [pltpu.SemaphoreType.DMA((len(flat),)), pltpu.SemaphoreType.DMA((6 * count,))],
+        + [pltpu.SemaphoreType.DMA((count,)), pltpu.SemaphoreType.DMA((6 * count,))],
         cost_estimate=pl.CostEstimate(
             flops=count * (2 * rows * width * fw * 3 + 10 * rows * width),
             bytes_accessed=2 * count * (2 * rows * width + 5 * rows * fw) + 6 * width * fw,
             transcendentals=0,
         ),
         name="project",
-    )(gain, shift, w, *flat)
+    )(gain, shift, w, *blocks)
 
 
 def views(refs):
@@ -489,11 +504,11 @@
 KB = 2
 
 
-def attend_kernel(heads, total, groups, qb, kb, lead, order_ref, group_ref, ids_ref, *refs):
+def attend_kernel(heads, total, groups, qb, kb, me_ref, order_ref, ids_ref, *refs):
     q_in, k_in, vt_in = [views(refs[n * groups : (n + 1) * groups]) for n in range(3)]
-    ctx_ref, low_ref, lse_ref, ends_ref, q_all, k_all, vt_all, low_all, count_ref, sems, out_sems = refs[
-        3 * groups :
-    ]
+    refs = refs[3 * groups :]
+    low_refs, refs = refs[:total], refs[total:]
+    ctx_ref, lse_ref, ends_ref, q_all, k_all, vt_all, low_all, count_ref, sems, out_sems = refs
     rows = low_all.shape[2]
     fw = q_all.shape[2]
     head = fw // heads
@@ -511,12 +526,7 @@
         ]
     copies = begin(pairs, sems)
 
-    per = total // ids_ref.shape[0]
-    ids = []
-    for n in range(total):
-        group = ids_ref[group_ref[n]].astype(F32)
-        ids.append(group[lead + n % per : lead + n % per + 1, :rows])
-    ids = jnp.concatenate(ids, axis=0)
+    ids = ids_ref[...]
     ends = jnp.zeros((total, rows), F32)
     for n in range(total):
         members = jnp.sum(jnp.where(ids == n, 1.0, 0.0))
@@ -566,22 +576,22 @@
         return unused
 
     lax.fori_loop(0, total // qb, block, 0)
-    finish(begin([(low_all, low_ref)], out_sems))
-
-
-def attend(q, k, vt, ids, lead, group, order, heads):
+    finish(begin([(low_all.at[me_ref[1] ^ m], low_refs[m]) for m in range(total)], out_sems))
+
+
+def attend(q, k, vt, ids, order, heads, me):
     total = len(order)
     groups = len(q)
     rows, fw = q[0].shape[1:]
     qb, kb = QB, KB
     pairs = total * rows * total * rows * heads
-    return pl.pallas_call(
-        functools.partial(attend_kernel, heads, total, groups, qb, kb, lead),
+    out = pl.pallas_call(
+        functools.partial(attend_kernel, heads, total, groups, qb, kb),
         in_specs=[SMEM] * 2 + [VMEM] + [ANY] * (3 * groups),
-        out_specs=[VMEM, ANY, VMEM, VMEM],
-        out_shape=[
+        out_specs=[ANY] * total + [VMEM] * 3,
+        out_shape=[shape((fw, rows), BF)] * total
+        + [
             shape((total // qb, fw, qb * rows), F32),
-            shape((total, fw, rows), BF),
             shape((total // qb, 1, heads * qb * rows), F32),
             shape((total // qb, 1, qb * rows), F32),
         ],
@@ -592,16 +602,17 @@
             pltpu.VMEM((total, fw, rows), BF),
             pltpu.SMEM((total // qb,), jnp.int32),
             pltpu.SemaphoreType.DMA((3 * total,)),
-            pltpu.SemaphoreType.DMA((1,)),
+            pltpu.SemaphoreType.DMA((total,)),
         ],
         cost_estimate=pl.CostEstimate(
             flops=2 * pairs * 128, bytes_accessed=10 * total * rows * fw, transcendentals=pairs // 2
         ),
         name="attend",
-    )(order, group, ids, *q, *k, *vt)
-
-
-def attend_back_kernel(heads, scale, total, groups, qb, kb, order_ref, ends_ref, ctx_ref, lse_ref, w_ref, gain_ref, shift_ref, cent_ref, *refs):
+    )(me, order, ids, *q, *k, *vt)
+    return out[:total], *out[total:]
+
+
+def attend_back_kernel(heads, scale, total, groups, qb, kb, order_ref, out_order_ref, ends_ref, ctx_ref, lse_ref, w_ref, gain_ref, shift_ref, cent_ref, *refs):
     q_in, k_in, v_in, kt_in, normed_in = [views(refs[n * groups : (n + 1) * groups]) for n in range(5)]
     refs = refs[5 * groups :]
     grad_in, refs = refs[0], refs[1:]
@@ -610,7 +621,7 @@
     q_raw, k_all, v_all, kt_all, g_raw, q_all, grad_all, delta_all, dq_all, out_all, normed_all, small_all, first_ref = refs[3:16]
     sems, normed_sems, out_sems, small_sems = refs[16:]
     unused, rows, width = out_all.shape
-    normed_copies = begin([(normed_in[n], normed_all.at[n]) for n in range(total)], normed_sems)
+    normed_copies = begin([(normed_in[n], normed_all.at[order_ref[n]]) for n in range(total)], normed_sems)
     fw = q_raw.shape[2]
     head = fw // heads
     span = qb * rows
@@ -691,20 +702,20 @@
     leaving = []
     lifted = jnp.zeros((1, width), F32)
     shifted = jnp.zeros((1, width), F32)
+    finish(normed_copies)
     for n in range(total):
-        at = order_ref[n]
+        at = out_order_ref[n]
         grad = dot(jnp.concatenate([dq_ref[at], dk_ref[at], dv_ref[at]], axis=1), w_ref[...], NT)
         out_all[n] = grad.astype(BF)
         leaving += begin(
             [(out_all.at[n], out_refs[n].at[pl.ds(0, rows), :])], out_sems.at[pl.ds(n, 1)]
         )
-        normed_copies[n].wait()
         shifted = shifted + jnp.sum(grad, axis=0, keepdims=True)
-        lifted = lifted + jnp.sum(grad * normed_all[n].astype(F32), axis=0, keepdims=True)
+        lifted = lifted + jnp.sum(grad * normed_all[at].astype(F32), axis=0, keepdims=True)
     lifted = (lifted - shift_ref[...] * shifted) / gain_ref[...]
     for n in range(total):
         rest = jnp.zeros((small_all.shape[1] - 3, width), F32)
-        cent = cent_ref[pl.ds(order_ref[n], 1), :]
+        cent = cent_ref[pl.ds(out_order_ref[n], 1), :]
         small_all[n] = jnp.concatenate([lifted, shifted, cent, rest], axis=0).astype(BF)
     finish(
         leaving
@@ -715,7 +726,7 @@
     )
 
 
-def attend_back(q, k, v, kt, normed, grads, ctx, lse, w, gain, shift, cent, ends, order, heads, scale):
+def attend_back(q, k, v, kt, normed, grads, ctx, lse, w, gain, shift, cent, ends, order, out_order, heads, scale):
     total = len(order)
     groups = len(q)
     rows, fw = q[0].shape[1:]
@@ -724,7 +735,7 @@
     pairs = total * rows * total * rows * heads
     out = pl.pallas_call(
         functools.partial(attend_back_kernel, heads, scale, total, groups, qb, kb),
-        in_specs=[SMEM] + [VMEM] * 7 + [ANY] * (5 * groups + 1),
+        in_specs=[SMEM] * 2 + [VMEM] * 7 + [ANY] * (5 * groups + 1),
         out_specs=[ANY] * total + [VMEM] * 3,
         out_shape=[shape((rows + 16, width), BF)] * total + [shape((total, rows, fw), BF)] * 3,
         scratch_shapes=[
@@ -750,7 +761,7 @@
             flops=5 * pairs * 128, bytes_accessed=20 * total * rows * fw, transcendentals=pairs // 2
         ),
         name="attend_back",
-    )(order, ends, ctx, lse, w, gain, shift, cent, *q, *k, *v, *kt, *normed, grads)
+    )(order, out_order, ends, ctx, lse, w, gain, shift, cent, *q, *k, *v, *kt, *normed, grads)
     return out[:total], out[total], out[total + 1], out[total + 2]
 
 
@@ -879,8 +890,9 @@
     all_ref, hidden_ref, slope_ref = refs[:3]
     held, first, second, hidden, slope, total, low, sem_w, sem_x, sem_o, sem_r = refs[3:]
     chunks, unused, chunk = first.shape
+    arriving = begin(piece_pairs(pieces, held), sem_x)
     weights = weight_copies(sub, w_in, w_back, first, second, sem_w)
-    finish(begin(piece_pairs(pieces, held), sem_x))
+    finish(arriving)
     leaving = begin([(held, all_ref)], sem_r.at[pl.ds(0, 1)])
     kept = [(hidden, hidden_ref), (slope, slope_ref)]
 
@@ -939,26 +951,19 @@
     return out[:count], out[count], out[count + 1], out[count + 2]
 
 
-def expert_second_kernel(sub, count, me_ref, bias_ref, w_in, w_back, *refs):
-    cot_in, refs = refs[: count // 2], refs[count // 2 :]
+def expert_second_kernel(sub, count, bias_ref, w_in, w_back, *refs):
+    cot_in, refs = refs[:count], refs[count:]
     pieces, refs = refs[:count], refs[count:]
     gates, refs = refs[:count], refs[count:]
     grad_outs, refs = refs[:count], refs[count:]
-    out_ref, all_ref, grad_all_ref, hidden_ref, pre_ref, bias_out, logit_ref = refs[:7]
-    held, cot, gate, held_grad, first, second, hidden, grad_pre, total, low, low_grad = refs[7:18]
-    sem_w, sem_x, sem_c, sem_g, sem_o, sem_p, sem_r = refs[18:]
+    all_ref, grad_all_ref, hidden_ref, pre_ref, bias_out = refs[:5]
+    held, cot, gate, held_grad, first, second, hidden, grad_pre, total, low_grad = refs[5:15]
+    sem_w, sem_x, sem_c, sem_g, sem_p, sem_r = refs[15:]
     chunks, unused, chunk = first.shape
     weights = weight_copies(sub, w_in, w_back, first, second, sem_w)
     arriving = begin(piece_pairs(pieces, held), sem_x)
     width = held.shape[1]
-    size, rows = count // 2, cot.shape[0] // count
-    early = begin(
-        [
-            (cot_in[m % size].at[pl.ds(m // size * rows, rows), :], cot.at[pl.ds(m * rows, rows), :])
-            for m in range(count)
-        ],
-        sem_c,
-    )
+    early = begin(piece_pairs(cot_in, cot), sem_c)
     early += begin(piece_pairs(gates, gate, width), sem_g)
     finish(early)
     held_grad[...] = (
@@ -986,22 +991,73 @@
     low_grad[...] = total[...].astype(BF)
     leaving += begin(back_pairs(grad_outs, low_grad), sem_p)
 
-    def forward(n, unused):
+    finish(leaving)
+    for n in range(chunks):
+        finish(copies_of([(h.at[n], o.at[n]) for h, o in kept], sem_r.at[pl.ds(2 * n + 2, 2)]))
+
+
+def expert_branch_kernel(sub, count, me_ref, hidden_in, w_back, *refs):
+    cot_in, (out_ref, logit_ref, hidden, second, cot, total, low, sem_h, sem_w, sem_c, sem_o) = (
+        refs[:count],
+        refs[count:],
+    )
+    chunks, unused, chunk = hidden.shape
+
+    def copy(n, which):
+        at = pl.ds(pl.multiple_of(n * chunk, chunk), chunk)
+        if which == 0:
+            return pltpu.make_async_copy(hidden_in.at[n], hidden.at[n], sem_h.at[n])
+        return pltpu.make_async_copy(w_back.at[0, sub, at, :], second.at[n], sem_w.at[n])
+
+    for n in range(chunks):
+        copy(n, 0).start()
+        copy(n, 1).start()
+    early = begin(piece_pairs(cot_in, cot), sem_c)
+
+    def step(n, unused):
+        copy(n, 0).wait()
+        copy(n, 1).wait()
         add_to(total, n, dot(hidden[n], second[n]))
         return unused
 
-    lax.fori_loop(0, chunks, forward, 0)
+    lax.fori_loop(0, chunks, step, 0)
     low[...] = total[...].astype(BF)
+    leaving = begin([(h, w) for w, h in spread_pairs(me_ref, out_ref, low, count)], sem_o)
+    finish(early)
     logit_ref[...] = scalar_lanes(
         jnp.sum(cot[...].astype(F32) * total[...], axis=1, keepdims=True)
     )
-    outs = [(h, w) for w, h in spread_pairs(me_ref, out_ref, low, count)]
-    finish(leaving + begin(outs, sem_o))
-    for n in range(chunks):
-        finish(copies_of([(h.at[n], o.at[n]) for h, o in kept], sem_r.at[pl.ds(2 * n + 2, 2)]))
-
-
-def expert_second(pieces, gates, cot, sub, w_in, w_back, bias, me):
+    finish(leaving)
+
+
+def expert_branch(hidden, cot, sub, w_back, me):
+    count = len(cot)
+    chunks, rows, chunk = hidden.shape
+    width = cot[0].shape[1]
+    return pl.pallas_call(
+        functools.partial(expert_branch_kernel, sub, count),
+        in_specs=[SMEM] + [ANY] * (2 + count),
+        out_specs=[ANY, VMEM],
+        out_shape=[shape((rows, width), BF), shape((rows, LANES), BF)],
+        scratch_shapes=[
+            pltpu.VMEM((chunks, rows, chunk), BF),
+            pltpu.VMEM((chunks, chunk, width), BF),
+            pltpu.VMEM((rows, width), BF),
+            pltpu.VMEM((rows, width), F32),
+            pltpu.VMEM((rows, width), BF),
+            pltpu.SemaphoreType.DMA((chunks,)),
+            pltpu.SemaphoreType.DMA((chunks,)),
+            pltpu.SemaphoreType.DMA((count,)),
+            pltpu.SemaphoreType.DMA((count,)),
+        ],
+        cost_estimate=pl.CostEstimate(
+            flops=2 * rows * width * chunks * chunk, bytes_accessed=8 * rows * width, transcendentals=0
+        ),
+        name="expert_branch",
+    )(me, hidden, w_back, *cot)
+
+
+def expert_second(pieces, gates, cot, sub, w_in, w_back, bias):
     count = len(pieces)
     rows, width = pieces[0].shape
     rows = rows * count
@@ -1010,12 +1066,12 @@
     chunks = ff // chunk
     out = pl.pallas_call(
         functools.partial(expert_second_kernel, sub, count),
-        in_specs=[SMEM, VMEM] + [ANY] * (2 + 2 * count + count // 2),
-        out_specs=[ANY] * (count + 5) + [VMEM] * 2,
+        in_specs=[VMEM] + [ANY] * (2 + 3 * count),
+        out_specs=[ANY] * (count + 4) + [VMEM],
         out_shape=[shape((rows // count, width), BF)] * count
-        + [shape((rows, width), BF)] * 3
+        + [shape((rows, width), BF)] * 2
         + [shape((chunks, rows, chunk), BF)] * 2
-        + [shape((chunks, 1, chunk), F32), shape((rows, LANES), BF)],
+        + [shape((chunks, 1, chunk), F32)],
         scratch_shapes=[
             pltpu.VMEM((rows, width), BF),
             pltpu.VMEM((rows, width), BF),
@@ -1027,9 +1083,7 @@
             pltpu.VMEM((chunks, rows, chunk), BF),
             pltpu.VMEM((rows, width), F32),
             pltpu.VMEM((rows, width), BF),
-            pltpu.VMEM((rows, width), BF),
             pltpu.SemaphoreType.DMA((2 * chunks,)),
-            pltpu.SemaphoreType.DMA((count,)),
             pltpu.SemaphoreType.DMA((count,)),
             pltpu.SemaphoreType.DMA((count,)),
             pltpu.SemaphoreType.DMA((count,)),
@@ -1037,10 +1091,10 @@
             pltpu.SemaphoreType.DMA((2 * chunks + 2,)),
         ],
         cost_estimate=pl.CostEstimate(
-            flops=8 * rows * width * ff, bytes_accessed=12 * rows * width, transcendentals=2 * rows * ff
+            flops=6 * rows * width * ff, bytes_accessed=12 * rows * width, transcendentals=2 * rows * ff
         ),
         name="expert_second",
-    )(me, bias.reshape(chunks, 1, chunk), w_in, w_back, *cot, *pieces, *gates)
+    )(bias.reshape(chunks, 1, chunk), w_in, w_back, *cot, *pieces, *gates)
     return out[:count], *out[count:]
 
 
@@ -1051,8 +1105,8 @@
     held_grad, first, second, slope, grad_pre, total, low_grad = refs[3:10]
     sem_w, sem_s, sem_g, sem_p, sem_r = refs[10:]
     chunks, unused, chunk = first.shape
+    arriving_grad = begin(piece_pairs(grads, held_grad), sem_g)
     weights = weight_copies(sub, w_in, w_back, first, second, sem_w)
-    arriving_grad = begin(piece_pairs(grads, held_grad), sem_g)
     begin([(slope_in.at[n], slope.at[n]) for n in range(chunks)], sem_s)
     low_grad[:, held_grad.shape[1] :] = logit_ref[...]
     finish(arriving_grad)
@@ -1218,13 +1272,19 @@
     slot = tok // cols_n
 
     count = 2 * own + part
-    w_cat = jnp.concatenate([w_query, w_key, w_value], axis=1)
-    order = jnp.stack(col_order(c, cols_n)).astype(jnp.int32)
+    small_experts = jnp.concatenate([expert_gain[0], expert_shift[0], b_back[0]]).reshape(-1)
+    more = 16 * -(-small_experts.shape[0] // (64 * fw))
+    small_experts = jnp.pad(small_experts, (0, more * 4 * fw - small_experts.shape[0]))
+    w_cat = jnp.concatenate(
+        [
+            jnp.concatenate([w_query, w_key, w_value, w_output], axis=1),
+            small_experts.reshape(more, 4 * fw),
+        ]
+    )
+    out_order = jnp.stack(col_order(c, cols_n)).astype(jnp.int32)
 
     def gather_tiles(value):
-        return lax.all_gather(value, ("row", "col"), axis=0, tiled=True).reshape(
-            rows_n, cols_n, part, fw
-        )
+        return lax.all_gather(value, "col", axis=0, tiled=True).reshape(cols_n, rows_n, part, fw)
 
     def matrix_sums(part_qkv, part_output):
         parts = jnp.concatenate([part_qkv, part_output], axis=1).reshape(rows_n, part, 4 * fw)
@@ -1245,122 +1305,112 @@
     route = (jnp.arange(tok, dtype=jnp.int32)[:, None] == place[None, :]).astype(BF)
     unroute = (place[:, None] == jnp.arange(tok, dtype=jnp.int32)[None, :]).astype(BF)
     moved_cot = dot(route, cotangent).astype(BF)
-    small_experts = jnp.concatenate([expert_gain[0], expert_shift[0], b_back[0]])
+
+    small = jnp.concatenate([norm_gain, norm_shift, centroids[0], block_ids[0].astype(BF)])[None]
+
+    def small_params(small):
+        small = small.reshape(cols_n, rows_n, count + tok)
+        small = reorder(small.transpose(1, 0, 2), r, rows_n).transpose(1, 0, 2)
+        gain, shift = [
+            small[:, :, n * own : (n + 1) * own].transpose(1, 0, 2).reshape(1, width).astype(F32)
+            for n in range(2)
+        ]
+        cents = small[:, :, 2 * own : count].reshape(cols_n, width)
+        ids = lax.dynamic_index_in_dim(small[:, :, count:], r, 1, keepdims=False)
+        return gain, shift, jnp.pad(cents, ((0, LANES - cols_n), (0, 0))), ids.astype(F32)
 
     if cols_n == 8:
         chips = cols_n // 2
         z, core = c // 2, c % 2
-        lane = jnp.arange(width, dtype=jnp.int32)
-        mine = lane // own == r * cols_n + c
-        cent_row = jnp.where(lane // part == r, jnp.tile(centroids[0], rows_n), 0)
-        ids_row = jnp.pad(block_ids[0].astype(BF), (0, width - tok))
-        packet = jnp.stack(
-            [
-                jnp.where(mine, jnp.tile(norm_gain, width // own), 0),
-                jnp.where(mine, jnp.tile(norm_shift, width // own), 0),
-                jnp.where(core == 0, cent_row, 0),
-                jnp.where(core == 1, cent_row, 0),
-                jnp.where(core == 0, ids_row, 0),
-                jnp.where(core == 1, ids_row, 0),
-                jnp.zeros_like(ids_row),
-                jnp.zeros_like(ids_row),
-            ]
-        )
-        packet = packet + swap_core(packet, cols_n)
-        top = direct_gather(packet[:4], "row", rows_n)
-        block = jnp.concatenate(
-            [tokens, sum(top[1:], top[0]), packet[4:], jnp.zeros((8, width), BF)]
-        )
         move_right = lambda v, s: lax.ppermute(v, "col", right_pairs(s - 1, chips - 2, cols_n))
         move_left = lambda v, s: lax.ppermute(v, "col", left_pairs(1, chips - s, cols_n))
         swap = lambda v: swap_core(v, cols_n)
-        right_1, left_1 = move_right(block, 1), move_left(block, 1)
-        w_pieces = direct_gather(after(w_cat, block), "row", rows_n)
-        small_experts = direct_gather(after(small_experts, block), "row", rows_n)
+        right_1, left_1 = move_right(tokens, 1), move_left(tokens, 1)
+        tokens_s, small_s = swap(tokens), swap(small)
+        right_1, left_1, tokens_s, small_s = together(right_1, left_1, tokens_s, small_s)
+        right_2, left_2 = move_right(right_1, 2), move_left(left_1, 2)
+        near = jnp.where(z < 2, left_1, right_1)
+        near_s = swap(near)
+        small = jnp.concatenate(direct_gather(jnp.stack([small, small_s]), "row", rows_n), axis=1)
+        right_2, left_2, near, near_s, small = together(right_2, left_2, near, near_s, small)
+        right_3, left_3 = move_right(right_2, 3), move_left(left_2, 3)
+        middle = jnp.where(
+            z < 2, jnp.where(z == 0, left_2, right_1), jnp.where(z == 2, left_1, right_2)
+        )
+        middle_s = swap(middle)
+        small = [small] + [send_xor(small, "col", cols_n, 2 * m) for m in range(1, chips)]
+        w_pieces = direct_gather(after(w_cat, right_2), "row", rows_n)
+        joined = together(
+            right_3, left_3, middle, middle_s, onehot_low, route, unroute, moved_cot, *small, *w_pieces
+        )
+        right_3, left_3, middle, middle_s, onehot_low, route, unroute, moved_cot = joined[:8]
+        small, w_pieces = joined[8 : 8 + chips], joined[8 + chips :]
+        far = jnp.where(z < 2, jnp.where(z == 0, left_3, left_2), jnp.where(z == 2, right_2, right_3))
+        far_s = swap(far)
+        w_cat, tile_rows_own, small_experts = arrange_rows(w_pieces, part, (3 * fw, fw), me)
+        small = reorder(reorder(jnp.stack(small), z, chips).transpose(1, 0, 2, 3), core, 2)
+        gain_attn, shift_attn, full_centroids, ids = small_params(small.transpose(1, 0, 2, 3))
+        tiles = gather_tiles(after(tile_rows_own, far))
+        early = project(
+            [tokens, tokens_s, near, near_s, middle, middle_s], gain_attn, shift_attn, w_cat, scale
+        )
+        cot_own = exchange(after(moved_cot, early[1]))
+        late = project([far, far_s], gain_attn, shift_attn, w_cat, scale)
+        from_z = [
+            z,
+            jnp.where(z % 2 == 0, 1, 2),
+            jnp.where(z < 2, jnp.where(z == 0, 2, 0), jnp.where(z == 2, 3, 1)),
+            jnp.where(z < 2, 3, 0),
+        ]
+        order = jnp.stack([at * 2 + (core ^ n) for at in from_z for n in range(2)]).astype(jnp.int32)
+        projected = list(zip(early, late))
+    else:
+        small = jnp.concatenate(direct_gather(small, "row", rows_n))
+        small = lax.all_gather(small, "col", axis=0, tiled=True)
+        gain_attn, shift_attn, full_centroids, ids = small_params(small)
+        w_pieces = direct_gather(w_cat, "row", rows_n)
         cot_own = exchange(moved_cot)
-        right_1, left_1, cot_own, *rest = together(
-            right_1, left_1, cot_own, *w_pieces, *small_experts
-        )
-        w_pieces, small_experts = rest[:rows_n], rest[rows_n:]
-        right_2, left_2 = move_right(right_1, 2), move_left(left_1, 2)
-        swapped, right_1s, left_1s = swap(block), swap(right_1), swap(left_1)
-        w_cat = arrange_rows(w_pieces, part, me)
-        right_2, left_2, swapped, right_1s, left_1s, w_cat = together(
-            right_2, left_2, swapped, right_1s, left_1s, w_cat
-        )
-        right_3, left_3 = move_right(right_2, 3), move_left(left_2, 3)
-        right_2s, left_2s = swap(right_2), swap(left_2)
-        cot_pieces = direct_gather(after(cot_own, right_1), "row", rows_n)
-        right_3, left_3, right_2s, left_2s, *cot_pieces = together(
-            right_3, left_3, right_2s, left_2s, *cot_pieces
-        )
-        right_3s, left_3s = swap(right_3), swap(left_3)
-        tiles = gather_tiles(after(w_output, right_3))
-        nothing = jnp.zeros((1, width), F32)
-        *early, packets, gain_attn, shift_attn = project(
-            [
-                (block,),
-                (swapped,),
-                (left_1, right_3),
-                (left_2, right_2),
-                (left_2s, right_2s),
-                (left_3, right_1),
-            ],
-            nothing, nothing, w_cat, tok, scale, (0, 2, 3, 5),
-        )
-        late = project(
-            [(left_1s, right_3s), (left_3s, right_1s)], gain_attn, shift_attn, w_cat, tok, scale
-        )
-        places = (0, 1, 2, 4, 5, 6, 3, 7)
-        order = order[jnp.array(places)]
-        projected = list(zip(early, late))
-        ids, lead = packets, 4
-        group = (jnp.arange(cols_n, dtype=jnp.int32) // 2 - z) % chips
-        cents = packets[:, 2:4]
-        turned = (jnp.arange(chips) - z) % chips
-        centroids_of = lambda held: jnp.take(held, turned, axis=0).reshape(cols_n, width)
-    else:
-        w_pieces = direct_gather(w_cat, "row", rows_n)
-        small_experts = direct_gather(small_experts, "row", rows_n)
-        cot_own = exchange(moved_cot)
-        cot_pieces = direct_gather(cot_own, "row", rows_n)
-        w_cat = arrange_rows(w_pieces, part, me)
-        gain_attn, shift_attn = [
-            lax.all_gather(v, ("row", "col"), axis=0, tiled=True).reshape(1, width).astype(F32)
-            for v in (norm_gain, norm_shift)
-        ]
-        cents = lax.all_gather(
-            lax.all_gather(centroids, "row", axis=1, tiled=True), "col", axis=0, tiled=True
-        )
-        centroids_of = lambda held: held
-        tiles = gather_tiles(w_output)
-        blocks = [(v,) for v in col_gather(tokens, cols_n)]
-        projected = [(p,) for p in project(blocks, gain_attn, shift_attn, w_cat, tok, scale)]
-        ids = lax.all_gather(block_ids[0].astype(BF), "col", axis=0, tiled=True)
-        ids, lead = ids.reshape(cols_n, 1, tok).astype(F32), 0
-        group = jnp.arange(cols_n, dtype=jnp.int32)
+        w_cat, tile_rows_own, small_experts = arrange_rows(w_pieces, part, (3 * fw, fw), me)
+        tiles = gather_tiles(tile_rows_own)
+        order = out_order
+        blocks = col_gather(tokens, cols_n)
+        projected = [(p,) for p in project(blocks, gain_attn, shift_attn, w_cat, scale)]
     normed, q, k, v, kt, vt = projected
 
-    ctx, ctx_low, lse, ends = attend(q, k, vt, ids, lead, group, order, heads)
-    small_experts, cents, ctx_low = together(jnp.stack(small_experts), cents, ctx_low)
-    ctx_low = exchange(ctx_low.reshape(width, tok))
-    experts = reorder(small_experts, r, rows_n).transpose(1, 0, 2).reshape(6, width).astype(F32)
-    full_centroids = jnp.pad(centroids_of(cents), ((0, LANES - cols_n), (0, 0)))
-    residual, gate, moved = forward_rows(ctx_low, tiles, tokens, full_centroids, onehot_low, route)
-
-    stream_0, grad_2, half_1, half_2 = enter_expert(exchange(moved), experts, cot_own)
+    ctx_low, ctx, lse, ends = attend(q, k, vt, ids, order, heads, me)
+    cot_own, small_experts, *ctx_low = together(cot_own, small_experts, *ctx_low)
+    bits = bits_of(rows_n)
+    near_cot = {
+        half: gather_path(cot_own[half * tok // 2 : (half + 1) * tok // 2], "row", rows_n, [bit])
+        for half, bit in ((0, bits[0]), (1, bits[-1]))
+    }
+    ctx_low = direct_exchange(ctx_low, "col", cols_n)
+    rest = together(*ctx_low, *near_cot[0], *near_cot[1])
+    ctx_low, near_cot = rest[:cols_n], {0: rest[cols_n : cols_n + 2], 1: rest[cols_n + 2 :]}
+    cot_pieces = gather_path(near_cot[0], "row", rows_n, bits[1:], [bits[0]]) + gather_path(
+        near_cot[1], "row", rows_n, bits[::-1][1:], [bits[-1]]
+    )
+    experts = small_experts.reshape(rows_n, -1)[:, : 6 * part].reshape(rows_n, 6, part)
+    experts = experts.transpose(1, 0, 2).reshape(6, width).astype(F32)
+    moved, ctx_low, residual, gate = forward_rows(
+        ctx_low, tiles, tokens, full_centroids, onehot_low, route, me
+    )
+
+    rest = together(*direct_exchange(moved, "col", cols_n), *cot_pieces)
+    arrived, cot_pieces = rest[:cols_n], rest[cols_n:]
+    stream_0, grad_2, half_1, half_2 = enter_expert(arrived, experts, cot_own, me)
     wide_pieces = gather_pieces(half_1, half_2, "row", rows_n)
     partial, normed_all_0, hidden_0, slope_0 = expert_first(wide_pieces, 0, w_in, w_back, b_in[0, 0])
     stream_1, half_1, half_2 = between_experts(
         experts, stream_0, scatter_pieces(partial, "row", rows_n)
     )
     pieces = gather_pieces(half_1, half_2, "row", rows_n)
-    partial, branch, normed_all_1, grad_all_1, hidden_1, grad_pre_1, bias_1, logit = expert_second(
-        pieces, wide_pieces, cot_pieces, 1, w_in, w_back, b_in[0, 1], me
+    partial, normed_all_1, grad_all_1, hidden_1, grad_pre_1, bias_1 = expert_second(
+        pieces, wide_pieces, cot_pieces, 1, w_in, w_back, b_in[0, 1]
     )
     sums = scatter_pieces(partial, "row", rows_n)
-    w_in_grad = weight_grads(normed_all_1, grad_pre_1, 1, None, False)
-    w_in_grad, *sums = together(w_in_grad, *sums)
+    branch, logit = expert_branch(hidden_1, cot_pieces, 1, w_back, me)
+    branch, logit, *sums = together(branch, logit, *sums)
     grad_1, half_1, half_2, sums_1 = middle_back(experts, stream_1, grad_2, sums)
     pieces = gather_pieces(half_1, half_2, "row", rows_n)
     w_back_grad = weight_grads(hidden_1, after(grad_all_1, grad_1), 1, None, True)
@@ -1368,12 +1418,12 @@
     partial, grad_all_0, grad_pre_0, bias_0 = expert_back(pieces, slope_0, logit, 0, w_in, w_back)
     sums = together(*scatter_pieces(partial, "row", rows_n))
     branch = lax.psum_scatter(after(branch, sums[0]), "row", scatter_dimension=0, tiled=True)
-    leaving, sums_0 = leave_back(experts, stream_0, grad_1, cot_own, stream_1, sums)
-    returned = exchange(leaving)
-    w_in_grad = weight_grads(normed_all_0, after(grad_pre_0, sums_0), 0, w_in_grad, False)
-    w_in_grad, returned = together(w_in_grad, returned)
+    *leaving, sums_0 = leave_back(experts, stream_0, grad_1, cot_own, stream_1, sums, me, cols_n)
+    returned = direct_exchange(leaving, "col", cols_n)
+    w_in_grad = weight_grads(normed_all_0, after(grad_pre_0, sums_0), 0, None, False)
+    w_in_grad, *returned = together(w_in_grad, *returned)
     grad_residual, grad_attended, part_cent, grad_ctx = backward_rows(
-        returned, tiles, unroute, cotangent, full_centroids, onehot_low, gate, residual
+        returned, tiles, unroute, cotangent, full_centroids, onehot_low, gate, residual, me
     )
 
     grad_ctx = exchange(grad_ctx)
@@ -1389,11 +1439,10 @@
     )
     partial, dq, dk, dv = attend_back(
         q, k, v, kt, normed, grad_ctx.reshape(cols_n, fw, tok), ctx, lse, w_cat, gain_attn, shift_attn,
-        part_cent, ends, order, heads, scale,
+        part_cent, ends, order, out_order, heads, scale,
     )
     dq, expert_low, *partial = together(dq, expert_low, *partial)
     if cols_n == 8:
-        partial = [partial[places.index(n)] for n in range(cols_n)]
         halves = [
             add_low(partial[2 * turn], swap(partial[2 * turn + 1])) for turn in range(chips)
         ]
@@ -1413,13 +1462,17 @@
         output = (residual + gate * dot(unroute, expert_low)).astype(BF)
         grad_sums = matrix_sums(part_qkv, part_output)
         from_left, from_right, output, *grad_sums = together(from_left, from_right, output, *grad_sums)
+        normed_all_1, from_left, from_right = together(normed_all_1, from_left, from_right)
         from_left = into_right(add_low(from_left, halves[1]), 3)
         from_right = into_left(add_low(from_right, halves[3]), 3)
+        w_in_grad = weight_grads(normed_all_1, grad_pre_1, 1, w_in_grad, False)
+        from_left, from_right, w_in_grad = together(from_left, from_right, w_in_grad)
         summed = halves[0].astype(F32) + from_left.astype(F32) + from_right.astype(F32)
     else:
         part_qkv = project_grads(dq, dk, dv, normed, order, rows_n)
         output = (residual + gate * dot(unroute, expert_low)).astype(BF)
         grad_sums = matrix_sums(part_qkv, part_output)
+        w_in_grad = weight_grads(normed_all_1, grad_pre_1, 1, w_in_grad, False)
         summed = col_scatter(partial, cols_n)
     grad_matrices = sum(v.astype(F32) for v in grad_sums)
     grad_qkv, grad_output = grad_matrices[:, : 3 * fw], grad_matrices[:, 3 * fw :]

time: 532 us -> 501 us (0.942)
  waiting for transfers between devices: 160 us -> 121 us
  starting transfers between devices: 127 us -> 142 us
    all_to_all x6 -> x3, waiting for transfers between devices: 47.9 us -> 4.06 us  [exchange(): lax.all_to_all(rows.reshape(cols_n, -1, rows.shape[-1]), 'col', split_axi...]
    ppermute x66 -> x87, starting transfers between devices: 67.2 us -> 99.7 us  [send_xor(): return lax.ppermute(value, axis, [(i, i ^ mask) for i in range(size)])]
    all_to_all x6 -> x3, starting transfers between devices: 30.6 us -> 12.5 us  [exchange(): lax.all_to_all(rows.reshape(cols_n, -1, rows.shape[-1]), 'col', split_axi...]
    convert_element_type x17 -> x5, other arithmetic: 12.7 us -> 4.29 us  [add_low(): return (left.astype(F32) + right.astype(F32)).astype(BF)]
    pallas_call x9 -> x10, Pallas kernels: 38.8 us -> 46.3 us  [the longest x2 12.2 us: project(): pl.pallas_call(functools.partial(project_kernel, scale, count), in_specs=...]
    ppermute x66 -> x87, waiting for transfers between devices: 88.8 us -> 95.4 us  [send_xor(): return lax.ppermute(value, axis, [(i, i ^ mask) for i in range(size)])]
    convert_element_type x3 -> x10, other arithmetic: 2.06 us -> 8.4 us  [the longest x6 6.17 us: scatter_path(): total = v[0] if len(v) == 1 else sum((n.astype(F32) for n in v)).astype(BF)]
    unnamed x158 -> x212, local copies, waits for them, and re-layouts: 12.2 us -> 11 us
  transfers between devices with their start and end apart: 87 -> 105, of which waited for: 36 -> 50; matrix products, arithmetic and copies ran while one was open for 6% -> 6% of each run, Pallas kernels for 22% -> 24%
where the time goes in v3:
time: 501 us; the launch traced here: 493 us
  Pallas kernels  170 us (34%)
  starting transfers between devices  142 us (28%)
  waiting for transfers between devices  121 us (24%)
  other arithmetic  21.2 us (4%)
  local copies, waits for them, and re-layouts  18.7 us (4%)
  between operations  15.9 us (3%)
    ppermute x87, starting transfers between devices, send_xor(): return lax.ppermute(value, axis, [(i, i ^ mask) for i in range(size)])  99.7 us
    ppermute x87, waiting for transfers between devices, send_xor(): return lax.ppermute(value, axis, [(i, i ^ mask) for i in range(size)])  95.4 us
    pallas_call x1, Pallas kernels, attend_back(): pl.pallas_call(functools.partial(attend_back_kernel, heads, scale, total,...  29.4 us
    pallas_call x4, Pallas kernels, weight_grads(): pl.pallas_call(functools.partial(weight_grads_kernel, chunked_left), grid...  23.7 us
    pallas_call x1, Pallas kernels, attend(): pl.pallas_call(functools.partial(attend_kernel, heads, total, groups, qb,...  17.6 us
    pallas_call x1, Pallas kernels, expert_second(): pl.pallas_call(functools.partial(expert_second_kernel, sub, count), in_sp...  16.4 us
    ppermute x3, starting transfers between devices, shards(): lax.ppermute(v, 'col', right_pairs(0, min(s - 1, chips - 2), cols_n))  16.2 us
    ppermute x3, waiting for transfers between devices, shards(): lax.ppermute(v, 'col', left_pairs(1, chips - s, cols_n))  15.3 us
  transfers between devices with their start and end apart: 105, of which 50 were waited for; matrix products, arithmetic and copies ran while one was open for 6% of the time, Pallas kernels for 24%

profile of v3, /device:TPU:0, one launch (start us, length us, event | category | flops | bytes accessed | tf_op | source)
XLA Modules:
  0.0 492.8 jit_solution(11509869095431303042)
XLA Ops:
  9.1 5.2 %collective-permute-start = (bf16[256,1024]{1,0:T(8,128)(2,1)}, bf16[256,1024]{1,0:T(8,128)(2,1)S(1)}, u32[]{:S(2)}, u32[]{:S(2)}) collective-permute-start(bf16[256,1024]{1,0:T(8,128)(2,1)} %tokens_ref.1), channel_id=1, source_target_pairs={{0,2},{1,3},{2,4},{3,5},{4,6},{5,7},{8,10},{9,11},{10,12},{11,13},... | collective-permute-start | bytes 1572872 | tf_op jit(solution)/shard_map/ppermute | solution.py:1325
  18.4 6.6 %collective-permute-done.1 = bf16[256,1024]{1,0:T(8,128)(2,1)S(1)} collective-permute-done((bf16[256,1024]{1,0:T(8,128)(2,1)}, bf16[256,1024]{1,0:T(8,128)(2,1)S(1)}, u32[]{:S(2)}, u32[]{:S(2)}) %collective-permute-start.1) | collective-permute-done | bytes 524320 | tf_op jit(solution)/shard_map/ppermute | solution.py:1326
  37.6 7.9 %collective-permute-done.5 = bf16[256,1024]{1,0:T(8,128)(2,1)S(1)} collective-permute-done((bf16[256,1024]{1,0:T(8,128)(2,1)S(1)}, bf16[256,1024]{1,0:T(8,128)(2,1)S(1)}, u32[]{:S(2)}, u32[]{:S(2)}) %collective-permute-start.5) | collective-permute-done | bytes 524320 | tf_op jit(solution)/shard_map/ppermute | solution.py:1326
  71.1 7.8 %project.2 = (bf16[6,256,1024]{2,1,0:T(8,128)(2,1)}, bf16[6,256,128]{2,1,0:T(8,128)(2,1)}, bf16[6,256,128]{2,1,0:T(8,128)(2,1)}, bf16[6,256,128]{2,1,0:T(8,128)(...) custom-call(f32[1,1024]{1,0:T(1,128)} %reshape.196.gain_ref, f32[1,1024]{1,0:T(1,128)} %reshape.197.shift_ref, ...), custom_call_target="tpu_custom_call" | custom-call | flops 1223688192 | bytes 9043968 | tf_op jit(solution)/shard_map/project/pallas_call | solution.py:454
  85.3 4.5 project.3
  89.7 17.6 %attend.1 = (bf16[128,256]{1,0:T(8,128)(2,1)}, bf16[128,256]{1,0:T(8,128)(2,1)}, bf16[128,256]{1,0:T(8,128)(2,1)}, bf16[128,256]{1,0:T(8,128)(2,1)}, bf16[128,25...) custom-call(s32[2]{0:T(128)} %pad_add_fusion.me_ref, ...), custom_call_target="tpu_custom_call" | custom-call | flops 2147483648 | bytes 2621440 | tf_op jit(solution)/shard_map/attend/pallas_call | solution.py:588
  131.4 4.2 forward_rows.1
  149.7 4.8 collective-permute-done.32.refs_4_
  164.1 6.1 %collective-permute-done.40.refs_1_.refs_17_ = bf16[128,1152]{1,0:T(8,128)(2,1)S(1)} collective-permute-done((bf16[128,1152]{1,0:T(8,128)(2,1)}, bf16[128,1152]{1,0:T(8,128)(2,1)S(1)}, u32[]{:S(2)}, u32[]{:S(2)}) %collective-permute-start.40) | collective-permute-done | bytes 294944 | tf_op jit(solution)/shard_map/ppermute | solution.py:29
  172.9 5.1 %collective-permute-done.41.refs_2_.refs_18_ = bf16[128,1152]{1,0:T(8,128)(2,1)S(1)} collective-permute-done((bf16[128,1152]{1,0:T(8,128)(2,1)}, bf16[128,1152]{1,0:T(8,128)(2,1)S(1)}, u32[]{:S(2)}, u32[]{:S(2)}) %collective-permute-start.41) | collective-permute-done | bytes 294944 | tf_op jit(solution)/shard_map/ppermute | solution.py:29
  178.0 4.6 collective-permute-done.42.refs_3_.refs_19_
  183.4 11.1 %expert_first.1 = (bf16[128,1024]{1,0:T(8,128)(2,1)}, bf16[128,1024]{1,0:T(8,128)(2,1)}, bf16[128,1024]{1,0:T(8,128)(2,1)}, bf16[128,1024]{1,0:T(8,128)(2,1)}, b...) custom-call(bf16[2,1,512]{2,1,0:T(2,128)(2,1)} %bitcast.137, ...), custom_call_target="tpu_custom_call" | custom-call | flops 4294967296 | bytes 8388608 | tf_op jit(solution)/shard_map/expert_first/pallas_call | solution.py:923
  198.7 5.4 %collective-permute-done.47 = bf16[128,1024]{1,0:T(8,128)(2,1)S(1)} collective-permute-done((bf16[128,1024]{1,0:T(8,128)(2,1)}, bf16[128,1024]{1,0:T(8,128)(2,1)S(1)}, u32[]{:S(2)}, u32[]{:S(2)}) %collective-permute-start.47) | collective-permute-done | bytes 262176 | tf_op jit(solution)/shard_map/ppermute | solution.py:29
  221.4 5.4 %collective-permute-done.52.refs_9_ = bf16[128,1024]{1,0:T(8,128)(2,1)S(1)} collective-permute-done((bf16[128,1024]{1,0:T(8,128)(2,1)}, bf16[128,1024]{1,0:T(8,128)(2,1)S(1)}, u32[]{:S(2)}, u32[]{:S(2)}) %collective-permute-start.52) | collective-permute-done | bytes 262176 | tf_op jit(solution)/shard_map/ppermute | solution.py:29
  235.8 16.4 %expert_second.1 = (bf16[128,1024]{1,0:T(8,128)(2,1)}, bf16[128,1024]{1,0:T(8,128)(2,1)}, bf16[128,1024]{1,0:T(8,128)(2,1)}, bf16[128,1024]{1,0:T(8,128)(2,1)}, ...) custom-call(bf16[2,1,512]{2,1,0:T(2,128)(2,1)} %bitcast.136, ...), custom_call_target="tpu_custom_call" | custom-call | flops 6442450944 | bytes 12582912 | tf_op jit(solution)/shard_map/expert_second/pallas_call | solution.py:1067
  265.1 8.2 %expert_branch.1 = (bf16[1024,1024]{1,0:T(8,128)(2,1)}, bf16[1024,128]{1,0:T(8,128)(2,1)}) custom-call(s32[2]{0:T(128)} %pad_add_fusion.me_ref, bf16[2,1024,512]{2,1,0:T(8,128)(2,1)} %get-tuple-element.368.hidden_in.left_ref, bf16[1,2,1024,1024]{3,2,1,0:T(8,128)(2,1)} %w_back.7, bf16[128,1024]{1,0:T(8,128)(2,1)} %copy-done.10, bf16[128,1024]{1,0:T(8,128)(2,1)} %copy-done.27, ...), custom_call_target="tpu_custom_call" | custom-call | flops 2147483648 | bytes 8388608 | tf_op jit(solution)/shard_map/expert_branch/pallas_call | solution.py:1037
  274.3 3.9 middle_back.1
  288.1 5.8 %weight_grads.4.refs_0_ = f32[1,2,1024,1024]{3,2,1,0:T(8,128)} custom-call(bf16[2,1024,512]{2,1,0:T(8,128)(2,1)} %get-tuple-element.368.hidden_in.left_ref, bf16[1024,1024]{1,0:T(8,128)(2,1)} %get-tuple-element.391.right_ref), custom_call_target="tpu_custom_call" | custom-call | flops 2147483648 | bytes 8388608 | tf_op jit(solution)/shard_map/weight_grads/pallas_call | solution.py:1193
  294.9 12.8 %expert_back.1 = (bf16[128,1152]{1,0:T(8,128)(2,1)}, bf16[128,1152]{1,0:T(8,128)(2,1)}, bf16[128,1152]{1,0:T(8,128)(2,1)}, bf16[128,1152]{1,0:T(8,128)(2,1)}, bf...) custom-call(bf16[1024,128]{1,0:T(8,128)(2,1)} %get-tuple-element.379, ...), custom_call_target="tpu_custom_call" | custom-call | flops 4294967296 | bytes 10485760 | tf_op jit(solution)/shard_map/expert_back/pallas_call | solution.py:1141
  311.9 5.4 %collective-permute-done.71 = bf16[128,1152]{1,0:T(8,128)(2,1)S(1)} collective-permute-done((bf16[128,1152]{1,0:T(8,128)(2,1)}, bf16[128,1152]{1,0:T(8,128)(2,1)S(1)}, u32[]{:S(2)}, u32[]{:S(2)}) %collective-permute-start.71) | collective-permute-done | bytes 294944 | tf_op jit(solution)/shard_map/ppermute | solution.py:29
  328.5 4.3 leave_back.1
  343.1 6.0 %weight_grads.5.refs_0_ = f32[1,2,1024,1024]{3,2,1,0:T(8,128)} custom-call(bf16[1024,1024]{1,0:T(8,128)(2,1)} %get-tuple-element.348.left_ref, bf16[2,1024,512]{2,1,0:T(8,128)(2,1)} %get-tuple-element.418.right_ref), custom_call_target="tpu_custom_call" | custom-call | flops 2147483648 | bytes 8388608 | tf_op jit(solution)/shard_map/weight_grads/pallas_call | solution.py:1193
  352.2 5.0 %backward_rows.1 = (f32[256,1024]{1,0:T(8,128)}, bf16[256,1024]{1,0:T(8,128)(2,1)}, f32[128,1024]{1,0:T(8,128)}, bf16[1024,256]{1,0:T(8,128)(2,1)}) custom-call(s32[2]{0:T(128)} %pad_add_fusion.me_ref, bf16[8,4,256,128]{3,2,1,0:T(8,128)(2,1)} %bitcast.105, bf16[256,256]{1,0:T(8,128)(2,1)} %get-tuple-element.292.unroute_ref, bf16[256,1024]{1,0:T(8,128)(2,1)} %cot_ref.1, ...), custom_call_target="tpu_custom_call" | custom-call | flops 805306368 | bytes 5242880 | tf_op jit(solution)/shard_map/backward_rows/pallas_call | solution.py:392
  357.2 5.2 %all-to-all-start.1 = ((bf16[8,128,256]{2,1,0:T(8,128)(2,1)}), bf16[8,128,256]{2,1,0:T(8,128)(2,1)S(1)}, u32[]{:S(2)}, u32[]{:S(2)}) async-start(bf16[8,128,256]{2,1,0:T(8,128)(2,1)} %bitcast.118), calls=%async_computation.2 | async-start | bytes 1048576 | tf_op jit(solution)/shard_map/all_to_all | solution.py:1295
  365.8 5.8 %weight_grads.6 = f32[1,2,1024,1024]{3,2,1,0:T(8,128)} custom-call(bf16[2,1024,512]{2,1,0:T(8,128)(2,1)} %get-tuple-element.444.left_ref, bf16[1024,1024]{1,0:T(8,128)(2,1)} %get-tuple-element.446.right_ref, f32[1,2,1024,1024]{3,2,1,0:T(8,128)} %weight_grads.4.refs_0_), custom_call_target="tpu_custom_call", output_to_operand_aliasing={{}: (2, {})} | custom-call | flops 2147483648 | bytes 8388608 | tf_op jit(solution)/shard_map/weight_grads/pallas_call | solution.py:1193
  383.1 29.4 %attend_back.1 = (bf16[272,1024]{1,0:T(8,128)(2,1)}, bf16[272,1024]{1,0:T(8,128)(2,1)}, bf16[272,1024]{1,0:T(8,128)(2,1)}, bf16[272,1024]{1,0:T(8,128)(2,1)}, bf...) custom-call(s32[8]{0:T(128)} %stack.95.order_ref, ...), custom_call_target="tpu_custom_call" | custom-call | flops 5368709120 | bytes 5242880 | tf_op jit(solution)/shard_map/attend_back/pallas_call | solution.py:736
  415.1 4.7 collective-permute-start.84
  423.0 7.0 %project_grads.1 = bf16[1024,384]{1,0:T(8,128)(2,1)} custom-call(s32[8]{0:T(128)} %stack.95.order_ref, bf16[8,256,128]{2,1,0:T(8,128)(2,1)} %get-tuple-element.467.dq_ref, bf16[8,256,128]{2,1,0:T(8,128)(2,1)} %get-tuple-element.468.dk_ref, bf16[8,256,128]{2,1,0:T(8,128)(2,1)} %get-tuple-element.469.dv_ref, ...), custom_call_target="tpu_custom_call" | custom-call | flops 1610612736 | bytes 6553600 | tf_op jit(solution)/shard_map/project_grads/pallas_call | solution.py:795
  433.8 5.1 %collective-permute-start.88 = (bf16[272,1024]{1,0:T(8,128)(2,1)S(1)}, bf16[272,1024]{1,0:T(8,128)(2,1)S(1)}, u32[]{:S(2)}, u32[]{:S(2)}) collective-permute-start(bf16[272,1024]{1,0:T(8,128)(2,1)S(1)} %get-tuple-element.549), channel_id=1, source_target_pairs={{0,2},{1,3},{2,4},{3,5},{8,10},{9,11},{10,12},{11,13},{16,18},{17,... | collective-permute-start | bytes 1671176 | tf_op jit(solution)/shard_map/ppermute | solution.py:1449
  444.5 4.9 collective-permute-done.92
  457.6 6.3 %collective-permute-start.94 = (bf16[272,1024]{1,0:T(8,128)(2,1)}, bf16[272,1024]{1,0:T(8,128)(2,1)S(1)}, u32[]{:S(2)}, u32[]{:S(2)}) collective-permute-start(bf16[272,1024]{1,0:T(8,128)(2,1)} %add_convert_fusion.1), channel_id=1, source_target_pairs={{0,2},{1,3},{2,4},{3,5},{4,6},{5,7},{8,10},{9,11},{10,12},{11,13},... | collective-permute-start | bytes 1671176 | tf_op jit(solution)/shard_map/ppermute | solution.py:1449
  464.0 6.1 %weight_grads.7 = f32[1,2,1024,1024]{3,2,1,0:T(8,128)} custom-call(bf16[1024,1024]{1,0:T(8,128)(2,1)} %get-tuple-element.487.left_ref, bf16[2,1024,512]{2,1,0:T(8,128)(2,1)} %get-tuple-element.488.right_ref, f32[1,2,1024,1024]{3,2,1,0:T(8,128)} %weight_grads.5.refs_0_), custom_call_target="tpu_custom_call", output_to_operand_aliasing={{}: (2, {})} | custom-call | flops 2147483648 | bytes 8388608 | tf_op jit(solution)/shard_map/weight_grads/pallas_call | solution.py:1193
  (501 shorter events, 238.1 us)
Async XLA Ops:
  7.2 124.1 %all-gather.2.cloned.1.call-start = ((), (), s32[]{:S(2)}) async-start(), calls=%async_computation.5 | async-start | bytes 2359296 | tf_op jit(solution)/shard_map/all_gather | solution.py:1287
  7.8 17.3 %collective-permute-start.1 = (bf16[256,1024]{1,0:T(8,128)(2,1)}, bf16[256,1024]{1,0:T(8,128)(2,1)S(1)}, u32[]{:S(2)}, u32[]{:S(2)}) collective-permute-start(bf16[256,1024]{1,0:T(8,128)(2,1)} %tokens_ref.1), channel_id=1, source_target_pairs={{2,0},{3,1},{4,2},{5,3},{6,4},{7,5},{10,8},{11,9},{12,10},{13,11},... | collective-permute-start | bytes 1572872 | tf_op jit(solution)/shard_map/ppermute | solution.py:1326
  9.1 17.3 %collective-permute-start = (bf16[256,1024]{1,0:T(8,128)(2,1)}, bf16[256,1024]{1,0:T(8,128)(2,1)S(1)}, u32[]{:S(2)}, u32[]{:S(2)}) collective-permute-start(bf16[256,1024]{1,0:T(8,128)(2,1)} %tokens_ref.1), channel_id=1, source_target_pairs={{0,2},{1,3},{2,4},{3,5},{4,6},{5,7},{8,10},{9,11},{10,12},{11,13},... | collective-permute-start | bytes 1572872 | tf_op jit(solution)/shard_map/ppermute | solution.py:1325
  27.0 18.4 %collective-permute-start.5 = (bf16[256,1024]{1,0:T(8,128)(2,1)S(1)}, bf16[256,1024]{1,0:T(8,128)(2,1)S(1)}, u32[]{:S(2)}, u32[]{:S(2)}) collective-permute-start(bf16[256,1024]{1,0:T(8,128)(2,1)S(1)} %collective-permute-done.1), channel_id=1, source_target_pairs={{2,0},{3,1},{4,2},{5,3},{10,8},{11,9},{12,10},{13,11},{18,16},{19,... | collective-permute-start | bytes 1572872 | tf_op jit(solution)/shard_map/ppermute | solution.py:1326
  52.3 13.2 %collective-permute-start.11 = (bf16[256,1024]{1,0:T(8,128)(2,1)S(1)}, bf16[256,1024]{1,0:T(8,128)(2,1)}, u32[]{:S(2)}, u32[]{:S(2)}) collective-permute-start(bf16[256,1024]{1,0:T(8,128)(2,1)S(1)} %collective-permute-done.5), channel_id=1, source_target_pairs={{2,0},{3,1},{10,8},{11,9},{18,16},{19,17},{26,24},{27,25}} | collective-permute-start | bytes 1572872 | tf_op jit(solution)/shard_map/ppermute | solution.py:1326
  78.8 28.7 %all-to-all-start = ((bf16[8,32,1024]{2,1,0:T(8,128)(2,1)}), bf16[8,32,1024]{2,1,0:T(8,128)(2,1)S(1)}, u32[]{:S(2)}, u32[]{:S(2)}) async-start(bf16[8,32,1024]{2,1,0:T(8,128)(2,1)} %bitcast.37), calls=%async_computation | async-start | bytes 1048576 | tf_op jit(solution)/shard_map/all_to_all | solution.py:1295
  82.4 289.2 %reduce-scatter.3.cloned.1.call-start = ((), (), s32[]{:S(2)}) async-start(), calls=%async_computation.6 | async-start | bytes 2621440 | tf_op jit(solution)/shard_map/reduce_scatter | solution.py:1420
  107.6 18.1 %collective-permute-start.28 = (bf16[128,1024]{1,0:T(8,128)(2,1)S(1)}, bf16[128,1024]{1,0:T(8,128)(2,1)S(1)}, u32[]{:S(2)}, u32[]{:S(2)}) collective-permute-start(bf16[128,1024]{1,0:T(8,128)(2,1)S(1)} %get-tuple-element.353.refs_4_), channel_id=1, source_target_pairs={{0,16},{8,24},{16,0},{24,8},{1,17},{9,25},{17,1},{25,9},{2,18},{10... | collective-permute-start | bytes 786440 | tf_op jit(solution)/shard_map/ppermute | solution.py:29
  110.0 15.7 %collective-permute-start.27 = (bf16[128,1024]{1,0:T(8,128)(2,1)S(1)}, bf16[128,1024]{1,0:T(8,128)(2,1)S(1)}, u32[]{:S(2)}, u32[]{:S(2)}) collective-permute-start(bf16[128,1024]{1,0:T(8,128)(2,1)S(1)} %get-tuple-element.349.refs_0_), channel_id=1, source_target_pairs={{0,8},{8,0},{16,24},{24,16},{1,9},{9,1},{17,25},{25,17},{2,10},{10... | collective-permute-start | bytes 786440 | tf_op jit(solution)/shard_map/ppermute | solution.py:29
  125.9 14.3 %collective-permute-start.37 = (bf16[128,1024]{1,0:T(8,128)(2,1)S(1)}, bf16[128,1024]{1,0:T(8,128)(2,1)S(1)}, u32[]{:S(2)}, u32[]{:S(2)}) collective-permute-start(bf16[128,1024]{1,0:T(8,128)(2,1)S(1)} %collective-permute-done.27.refs_1_), channel_id=1, source_target_pairs={{0,16},{8,24},{16,0},{24,8},{1,17},{9,25},{17,1},{25,9},{2,18},{10... | collective-permute-start | bytes 786440 | tf_op jit(solution)/shard_map/ppermute | solution.py:29
  127.8 14.4 %collective-permute-start.38 = (bf16[128,1024]{1,0:T(8,128)(2,1)S(1)}, bf16[128,1024]{1,0:T(8,128)(2,1)S(1)}, u32[]{:S(2)}, u32[]{:S(2)}) collective-permute-start(bf16[128,1024]{1,0:T(8,128)(2,1)S(1)} %get-tuple-element.353.refs_4_), channel_id=1, source_target_pairs={{0,8},{8,0},{16,24},{24,16},{1,9},{9,1},{17,25},{25,17},{2,10},{10... | collective-permute-start | bytes 786440 | tf_op jit(solution)/shard_map/ppermute | solution.py:29
  129.3 15.1 %collective-permute-start.39 = (bf16[128,1024]{1,0:T(8,128)(2,1)S(1)}, bf16[128,1024]{1,0:T(8,128)(2,1)S(1)}, u32[]{:S(2)}, u32[]{:S(2)}) collective-permute-start(bf16[128,1024]{1,0:T(8,128)(2,1)S(1)} %collective-permute-done.28.refs_6_), channel_id=1, source_target_pairs={{0,8},{8,0},{16,24},{24,16},{1,9},{9,1},{17,25},{25,17},{2,10},{10... | collective-permute-start | bytes 786440 | tf_op jit(solution)/shard_map/ppermute | solution.py:29
  161.8 16.2 %collective-permute-start.41 = (bf16[128,1152]{1,0:T(8,128)(2,1)}, bf16[128,1152]{1,0:T(8,128)(2,1)S(1)}, u32[]{:S(2)}, u32[]{:S(2)}) collective-permute-start(bf16[128,1152]{1,0:T(8,128)(2,1)} %get-tuple-element.346.refs_0_.refs_16_), channel_id=1, source_target_pairs={{0,16},{8,24},{16,0},{24,8},{1,17},{9,25},{17,1},{25,9},{2,18},{10... | collective-permute-start | bytes 884744 | tf_op jit(solution)/shard_map/ppermute | solution.py:29
  163.6 14.5 %collective-permute-start.43 = (bf16[128,1152]{1,0:T(8,128)(2,1)}, bf16[128,1152]{1,0:T(8,128)(2,1)S(1)}, u32[]{:S(2)}, u32[]{:S(2)}) collective-permute-start(bf16[128,1152]{1,0:T(8,128)(2,1)} %get-tuple-element.347.refs_4_.refs_20_), channel_id=1, source_target_pairs={{0,8},{8,0},{16,24},{24,16},{1,9},{9,1},{17,25},{25,17},{2,10},{10... | collective-permute-start | bytes 884744 | tf_op jit(solution)/shard_map/ppermute | solution.py:29
  195.9 13.0 %collective-permute-start.46 = (bf16[128,1024]{1,0:T(8,128)(2,1)}, bf16[128,1024]{1,0:T(8,128)(2,1)S(1)}, u32[]{:S(2)}, u32[]{:S(2)}) collective-permute-start(bf16[128,1024]{1,0:T(8,128)(2,1)} %get-tuple-element.359), channel_id=1, source_target_pairs={{0,8},{8,0},{16,24},{24,16},{1,9},{9,1},{17,25},{25,17},{2,10},{10... | collective-permute-start | bytes 786440 | tf_op jit(solution)/shard_map/ppermute | solution.py:29
  197.4 12.7 %collective-permute-start.49 = (bf16[128,1024]{1,0:T(8,128)(2,1)}, bf16[128,1024]{1,0:T(8,128)(2,1)S(1)}, u32[]{:S(2)}, u32[]{:S(2)}) collective-permute-start(bf16[128,1024]{1,0:T(8,128)(2,1)} %get-tuple-element.363), channel_id=1, source_target_pairs={{0,16},{8,24},{16,0},{24,8},{1,17},{9,25},{17,1},{25,9},{2,18},{10... | collective-permute-start | bytes 786440 | tf_op jit(solution)/shard_map/ppermute | solution.py:29
  219.7 12.5 %collective-permute-start.53 = (bf16[128,1024]{1,0:T(8,128)(2,1)}, bf16[128,1024]{1,0:T(8,128)(2,1)S(1)}, u32[]{:S(2)}, u32[]{:S(2)}) collective-permute-start(bf16[128,1024]{1,0:T(8,128)(2,1)} %get-tuple-element.366.refs_8_), channel_id=1, source_target_pairs={{0,16},{8,24},{16,0},{24,8},{1,17},{9,25},{17,1},{25,9},{2,18},{10... | collective-permute-start | bytes 786440 | tf_op jit(solution)/shard_map/ppermute | solution.py:29
  254.6 18.8 %collective-permute-start.58 = (bf16[128,1024]{1,0:T(8,128)(2,1)}, bf16[128,1024]{1,0:T(8,128)(2,1)S(1)}, u32[]{:S(2)}, u32[]{:S(2)}) collective-permute-start(bf16[128,1024]{1,0:T(8,128)(2,1)} %get-tuple-element.372), channel_id=1, source_target_pairs={{0,8},{8,0},{16,24},{24,16},{1,9},{9,1},{17,25},{25,17},{2,10},{10... | collective-permute-start | bytes 786440 | tf_op jit(solution)/shard_map/ppermute | solution.py:29
  256.1 17.3 %collective-permute-start.61 = (bf16[128,1024]{1,0:T(8,128)(2,1)}, bf16[128,1024]{1,0:T(8,128)(2,1)S(1)}, u32[]{:S(2)}, u32[]{:S(2)}) collective-permute-start(bf16[128,1024]{1,0:T(8,128)(2,1)} %get-tuple-element.376), channel_id=1, source_target_pairs={{0,16},{8,24},{16,0},{24,8},{1,17},{9,25},{17,1},{25,9},{2,18},{10... | collective-permute-start | bytes 786440 | tf_op jit(solution)/shard_map/ppermute | solution.py:29
  260.5 12.9 %collective-permute-start.60 = (bf16[128,1024]{1,0:T(8,128)(2,1)S(1)}, bf16[128,1024]{1,0:T(8,128)(2,1)S(1)}, u32[]{:S(2)}, u32[]{:S(2)}) collective-permute-start(bf16[128,1024]{1,0:T(8,128)(2,1)S(1)} %add_convert_fusion.9), channel_id=1, source_target_pairs={{0,16},{8,24},{16,0},{24,8},{1,17},{9,25},{17,1},{25,9},{2,18},{10... | collective-permute-start | bytes 786440 | tf_op jit(solution)/shard_map/ppermute | solution.py:29
  280.3 13.6 %collective-permute-start.65 = (bf16[128,1024]{1,0:T(8,128)(2,1)}, bf16[128,1024]{1,0:T(8,128)(2,1)S(1)}, u32[]{:S(2)}, u32[]{:S(2)}) collective-permute-start(bf16[128,1024]{1,0:T(8,128)(2,1)} %get-tuple-element.394.refs_0_), channel_id=1, source_target_pairs={{0,16},{8,24},{16,0},{24,8},{1,17},{9,25},{17,1},{25,9},{2,18},{10... | collective-permute-start | bytes 786440 | tf_op jit(solution)/shard_map/ppermute | solution.py:29
  308.3 13.2 %collective-permute-start.70 = (bf16[128,1152]{1,0:T(8,128)(2,1)}, bf16[128,1152]{1,0:T(8,128)(2,1)S(1)}, u32[]{:S(2)}, u32[]{:S(2)}) collective-permute-start(bf16[128,1152]{1,0:T(8,128)(2,1)} %get-tuple-element.404), channel_id=1, source_target_pairs={{0,8},{8,0},{16,24},{24,16},{1,9},{9,1},{17,25},{25,17},{2,10},{10... | collective-permute-start | bytes 884744 | tf_op jit(solution)/shard_map/ppermute | solution.py:29
  357.2 20.6 %all-to-all-start.1 = ((bf16[8,128,256]{2,1,0:T(8,128)(2,1)}), bf16[8,128,256]{2,1,0:T(8,128)(2,1)S(1)}, u32[]{:S(2)}, u32[]{:S(2)}) async-start(bf16[8,128,256]{2,1,0:T(8,128)(2,1)} %bitcast.118), calls=%async_computation.2 | async-start | bytes 1048576 | tf_op jit(solution)/shard_map/all_to_all | solution.py:1295
  362.4 68.8 %reduce-scatter.5.cloned.1.call-start = ((), (), s32[]{:S(2)}) async-start(), calls=%async_computation.7 | async-start | bytes 2359296 | tf_op jit(solution)/shard_map/reduce_scatter | solution.py:1437
  378.6 33.9 %all-to-all-start.2 = ((bf16[8,32,1024]{2,1,0:T(8,128)(2,1)}), bf16[8,32,1024]{2,1,0:T(8,128)(2,1)S(1)}, u32[]{:S(2)}, u32[]{:S(2)}) async-start(bf16[8,32,1024]{2,1,0:T(8,128)(2,1)} %bitcast.46), calls=%async_computation.3 | async-start | bytes 1048576 | tf_op jit(solution)/shard_map/all_to_all | solution.py:1295
  413.6 17.6 %collective-permute-start.87 = (bf16[272,1024]{1,0:T(8,128)(2,1)}, bf16[272,1024]{1,0:T(8,128)(2,1)}, u32[]{:S(2)}, u32[]{:S(2)}) collective-permute-start(bf16[272,1024]{1,0:T(8,128)(2,1)} %get-tuple-element.473), channel_id=1, source_target_pairs={{0,1},{1,0},{2,3},{3,2},{4,5},{5,4},{6,7},{7,6},{8,9},{9,8},{10,11... | collective-permute-start | bytes 1671176 | tf_op jit(solution)/shard_map/ppermute | solution.py:29
  415.1 16.1 %collective-permute-start.84 = (bf16[272,1024]{1,0:T(8,128)(2,1)S(1)}, bf16[272,1024]{1,0:T(8,128)(2,1)}, u32[]{:S(2)}, u32[]{:S(2)}) collective-permute-start(bf16[272,1024]{1,0:T(8,128)(2,1)S(1)} %add_convert_fusion.5), channel_id=1, source_target_pairs={{0,2},{1,3},{8,10},{9,11},{16,18},{17,19},{24,26},{25,27}} | collective-permute-start | bytes 1671176 | tf_op jit(solution)/shard_map/ppermute | solution.py:1449
  433.1 21.2 %collective-permute-start.89 = (bf16[272,1024]{1,0:T(8,128)(2,1)S(1)}, bf16[272,1024]{1,0:T(8,128)(2,1)S(1)}, u32[]{:S(2)}, u32[]{:S(2)}) collective-permute-start(bf16[272,1024]{1,0:T(8,128)(2,1)S(1)} %get-tuple-element.548), channel_id=1, source_target_pairs={{4,2},{5,3},{6,4},{7,5},{12,10},{13,11},{14,12},{15,13},{20,18},{2... | collective-permute-start | bytes 1671176 | tf_op jit(solution)/shard_map/ppermute | solution.py:1452
  433.8 20.5 %collective-permute-start.88 = (bf16[272,1024]{1,0:T(8,128)(2,1)S(1)}, bf16[272,1024]{1,0:T(8,128)(2,1)S(1)}, u32[]{:S(2)}, u32[]{:S(2)}) collective-permute-start(bf16[272,1024]{1,0:T(8,128)(2,1)S(1)} %get-tuple-element.549), channel_id=1, source_target_pairs={{0,2},{1,3},{2,4},{3,5},{8,10},{9,11},{10,12},{11,13},{16,18},{17,... | collective-permute-start | bytes 1671176 | tf_op jit(solution)/shard_map/ppermute | solution.py:1449
  449.5 25.7 %collective-permute-start.93 = (bf16[272,1024]{1,0:T(8,128)(2,1)}, bf16[272,1024]{1,0:T(8,128)(2,1)S(1)}, u32[]{:S(2)}, u32[]{:S(2)}) collective-permute-start(bf16[272,1024]{1,0:T(8,128)(2,1)} %get-tuple-element.481), channel_id=1, source_target_pairs={{0,1},{1,0},{2,3},{3,2},{4,5},{5,4},{6,7},{7,6},{8,9},{9,8},{10,11... | collective-permute-start | bytes 1671176 | tf_op jit(solution)/shard_map/ppermute | solution.py:29
  456.3 17.5 %collective-permute-start.95 = (bf16[272,1024]{1,0:T(8,128)(2,1)}, bf16[272,1024]{1,0:T(8,128)(2,1)S(1)}, u32[]{:S(2)}, u32[]{:S(2)}) collective-permute-start(bf16[272,1024]{1,0:T(8,128)(2,1)} %add_convert_fusion), channel_id=1, source_target_pairs={{2,0},{3,1},{4,2},{5,3},{6,4},{7,5},{10,8},{11,9},{12,10},{13,11},... | collective-permute-start | bytes 1671176 | tf_op jit(solution)/shard_map/ppermute | solution.py:1452
  457.6 17.5 %collective-permute-start.94 = (bf16[272,1024]{1,0:T(8,128)(2,1)}, bf16[272,1024]{1,0:T(8,128)(2,1)S(1)}, u32[]{:S(2)}, u32[]{:S(2)}) collective-permute-start(bf16[272,1024]{1,0:T(8,128)(2,1)} %add_convert_fusion.1), channel_id=1, source_target_pairs={{0,2},{1,3},{2,4},{3,5},{4,6},{5,7},{8,10},{9,11},{10,12},{11,13},... | collective-permute-start | bytes 1671176 | tf_op jit(solution)/shard_map/ppermute | solution.py:1449
  (175 other events, 1714.4 us)
Sparse Core Ops, SparseCore 0:
  69.3 39.0 all-gather.1
  327.9 36.9 reduce-scatter.2
  377.9 37.6 reduce-scatter.4

commit v4 on v3

--- a/solution.py
+++ b/solution.py
@@ -282,6 +282,7 @@
         out_specs=[VMEM] * 3,
         out_shape=[shape((tok, width), F32)] + [shape((tok // 2, width), BF)] * 2,
         cost_estimate=pl.CostEstimate(flops=20 * tok * width, bytes_accessed=12 * tok * width, transcendentals=0),
+        compiler_params=params(20),
         name="between_experts",
     )(experts, stream, *sums)
 
@@ -362,7 +363,7 @@
         held[pl.ds(pl.multiple_of((me_ref[1] ^ m) * rows, rows), rows), :] = piece[...]
 
 
-def backward_kernel(total, me_ref, tiles_ref, unroute_ref, cot_ref, cent_ref, onehot_ref, turned_ref, gate_ref, residual_ref, *refs):
+def backward_kernel(total, me_ref, tiles_ref, unroute_ref, cot_ref, cent_ref, onehot_ref, gate_ref, residual_ref, *refs):
     pieces, (out_ref, low_ref, cent_out, ctx_ref, back_ref) = refs[:total], refs[total:]
     place_pieces(pieces, me_ref, back_ref)
     width = cot_ref.shape[1]
@@ -378,9 +379,9 @@
     for n in range(rows_n):
         ctx_ref[n * part : (n + 1) * part, :] = dot(tile_rows(tiles_ref, n), low, NT).astype(BF)
     cent_out[...] = lax.dot_general(
-        turned_ref[...].astype(F32),
+        onehot_ref[...].astype(F32),
         grad_logit * residual_ref[...].astype(BF).astype(F32),
-        NN,
+        (((0,), (0,)), ((), ())),
         precision=lax.Precision.HIGHEST,
         preferred_element_type=F32,
     )
@@ -391,7 +392,7 @@
     total = len(pieces)
     return pl.pallas_call(
         functools.partial(backward_kernel, total),
-        in_specs=[SMEM] + [VMEM] * (8 + total),
+        in_specs=[SMEM] + [VMEM] * (7 + total),
         out_specs=[VMEM] * 4,
         out_shape=[
             shape((tok, width), F32),
@@ -404,7 +405,7 @@
             flops=3 * tok * width * width, bytes_accessed=2 * width * width + 12 * tok * width, transcendentals=0
         ),
         name="backward_rows",
-    )(me, tiles, unroute, cot, cent, onehot, onehot.T, gate, residual, *pieces)
+    )(me, tiles, unroute, cot, cent, onehot, gate, residual, *pieces)
 
 
 def finish_kernel(stream_ref, branch_ref, experts_ref, out_ref):
@@ -621,7 +622,6 @@
     q_raw, k_all, v_all, kt_all, g_raw, q_all, grad_all, delta_all, dq_all, out_all, normed_all, small_all, first_ref = refs[3:16]
     sems, normed_sems, out_sems, small_sems = refs[16:]
     unused, rows, width = out_all.shape
-    normed_copies = begin([(normed_in[n], normed_all.at[order_ref[n]]) for n in range(total)], normed_sems)
     fw = q_raw.shape[2]
     head = fw // heads
     span = qb * rows
@@ -638,6 +638,7 @@
             (grad_in.at[n], g_raw.at[n // qb, :, pl.ds((n % qb) * rows, rows)]),
         ]
     copies = begin(pairs, sems)
+    normed_copies = begin([(normed_in[n], normed_all.at[order_ref[n]]) for n in range(total)], normed_sems)
     lasts = [jnp.max(ends_ref[i]).astype(jnp.int32) for i in range(total // qb)]
     for j in range(total // kb):
         first_ref[j] = sum((last <= j * kb * rows).astype(jnp.int32) for last in lasts)
@@ -838,7 +839,7 @@
     return pre_act * below, below + pre_act * bell
 
 
-def weight_copies(sub, w_in, w_back, first, second, sems):
+def weight_copies(sub, w_in, w_back, first, second, sems, between=lambda n: None, turns=(0, 1)):
     count, unused, chunk = first.shape
 
     def copy(n, which):
@@ -848,8 +849,9 @@
         return pltpu.make_async_copy(w_back.at[0, sub, at, :], second.at[n], sems.at[2 * n + 1])
 
     for n in range(count):
-        copy(n, 0).start()
-        copy(n, 1).start()
+        copy(n, turns[0]).start()
+        between(n)
+        copy(n, turns[1]).start()
     return copy
 
 
@@ -960,22 +962,33 @@
     held, cot, gate, held_grad, first, second, hidden, grad_pre, total, low_grad = refs[5:15]
     sem_w, sem_x, sem_c, sem_g, sem_p, sem_r = refs[15:]
     chunks, unused, chunk = first.shape
-    weights = weight_copies(sub, w_in, w_back, first, second, sem_w)
     arriving = begin(piece_pairs(pieces, held), sem_x)
     width = held.shape[1]
-    early = begin(piece_pairs(cot_in, cot), sem_c)
-    early += begin(piece_pairs(gates, gate, width), sem_g)
-    finish(early)
-    held_grad[...] = (
-        cot[...].astype(F32) * jnp.sum(gate[...].astype(F32), axis=1, keepdims=True)
-    ).astype(BF)
+    early = []
+
+    def load_early(n):
+        if n == 0:
+            early.extend(begin(piece_pairs(cot_in, cot), sem_c))
+            early.extend(begin(piece_pairs(gates, gate, width), sem_g))
+
+    weights = weight_copies(sub, w_in, w_back, first, second, sem_w, load_early)
     finish(arriving)
-    leaving = begin([(held, all_ref), (held_grad, grad_all_ref)], sem_r.at[pl.ds(0, 2)])
+    leaving = begin([(held, all_ref)], sem_r.at[pl.ds(0, 1)])
+    scaled = [(held_grad, grad_all_ref)]
     kept = [(hidden, hidden_ref), (grad_pre, pre_ref)]
 
     def step(n, unused):
         weights(n, 0).wait()
         pre_act = dot(held[...], first[n]) + bias_ref[n].astype(F32)
+
+        @pl.when(n == 0)
+        def scale_grads():
+            finish(early)
+            held_grad[...] = (
+                cot[...].astype(F32) * jnp.sum(gate[...].astype(F32), axis=1, keepdims=True)
+            ).astype(BF)
+            begin(scaled, sem_r.at[pl.ds(1, 1)])
+
         weights(n, 1).wait()
         grad_hidden = dot(held_grad[...], second[n], NT)
         value, rise = gelu_pair(pre_act)
@@ -991,7 +1004,7 @@
     low_grad[...] = total[...].astype(BF)
     leaving += begin(back_pairs(grad_outs, low_grad), sem_p)
 
-    finish(leaving)
+    finish(leaving + copies_of(scaled, sem_r.at[pl.ds(1, 1)]))
     for n in range(chunks):
         finish(copies_of([(h.at[n], o.at[n]) for h, o in kept], sem_r.at[pl.ds(2 * n + 2, 2)]))
 
@@ -1106,8 +1119,10 @@
     sem_w, sem_s, sem_g, sem_p, sem_r = refs[10:]
     chunks, unused, chunk = first.shape
     arriving_grad = begin(piece_pairs(grads, held_grad), sem_g)
-    weights = weight_copies(sub, w_in, w_back, first, second, sem_w)
-    begin([(slope_in.at[n], slope.at[n]) for n in range(chunks)], sem_s)
+    slopes = lambda n: pltpu.make_async_copy(slope_in.at[n], slope.at[n], sem_s.at[n])
+    weights = weight_copies(
+        sub, w_in, w_back, first, second, sem_w, lambda n: slopes(n).start(), (1, 0)
+    )
     low_grad[:, held_grad.shape[1] :] = logit_ref[...]
     finish(arriving_grad)
     leaving = begin([(held_grad, grad_all_ref)], sem_r.at[pl.ds(0, 1)])
@@ -1115,7 +1130,7 @@
     def step(n, unused):
         weights(n, 1).wait()
         grad_hidden = dot(held_grad[...], second[n], NT)
-        pltpu.make_async_copy(slope_in.at[n], slope.at[n], sem_s.at[n]).wait()
+        slopes(n).wait()
         back = (grad_hidden * slope[n]).astype(BF)
         grad_pre[n] = back
         bias_out[n] = jnp.sum(back.astype(F32), axis=0, keepdims=True)
@@ -1332,7 +1347,16 @@
         near = jnp.where(z < 2, left_1, right_1)
         near_s = swap(near)
         small = jnp.concatenate(direct_gather(jnp.stack([small, small_s]), "row", rows_n), axis=1)
-        right_2, left_2, near, near_s, small = together(right_2, left_2, near, near_s, small)
+        from_z = [
+            z,
+            jnp.where(z % 2 == 0, 1, 2),
+            jnp.where(z < 2, jnp.where(z == 0, 2, 0), jnp.where(z == 2, 3, 1)),
+            jnp.where(z < 2, 3, 0),
+        ]
+        order = jnp.stack([at * 2 + (core ^ n) for at in from_z for n in range(2)]).astype(jnp.int32)
+        right_2, left_2, near, near_s, small, order, out_order, me = together(
+            right_2, left_2, near, near_s, small, order, out_order, me
+        )
         right_3, left_3 = move_right(right_2, 3), move_left(left_2, 3)
         middle = jnp.where(
             z < 2, jnp.where(z == 0, left_2, right_1), jnp.where(z == 2, left_1, right_2)
@@ -1351,19 +1375,12 @@
         small = reorder(reorder(jnp.stack(small), z, chips).transpose(1, 0, 2, 3), core, 2)
         gain_attn, shift_attn, full_centroids, ids = small_params(small.transpose(1, 0, 2, 3))
         tiles = gather_tiles(after(tile_rows_own, far))
-        early = project(
-            [tokens, tokens_s, near, near_s, middle, middle_s], gain_attn, shift_attn, w_cat, scale
+        cot_own = exchange(after(moved_cot, far_s))
+        projected = project(
+            [tokens, tokens_s, near, near_s, middle, middle_s, far, far_s],
+            gain_attn, shift_attn, w_cat, scale,
         )
-        cot_own = exchange(after(moved_cot, early[1]))
-        late = project([far, far_s], gain_attn, shift_attn, w_cat, scale)
-        from_z = [
-            z,
-            jnp.where(z % 2 == 0, 1, 2),
-            jnp.where(z < 2, jnp.where(z == 0, 2, 0), jnp.where(z == 2, 3, 1)),
-            jnp.where(z < 2, 3, 0),
-        ]
-        order = jnp.stack([at * 2 + (core ^ n) for at in from_z for n in range(2)]).astype(jnp.int32)
-        projected = list(zip(early, late))
+        projected = [(p,) for p in projected]
     else:
         small = jnp.concatenate(direct_gather(small, "row", rows_n))
         small = lax.all_gather(small, "col", axis=0, tiled=True)

time: 501 us -> 495 us (0.988)
    pallas_call x2 -> x1, Pallas kernels: 12.2 us -> 9.44 us  [project(): pl.pallas_call(functools.partial(project_kernel, scale, count), in_specs=...]
    unnamed x212 -> x208, local copies, waits for them, and re-layouts: 11 us -> 10.5 us
  transfers between devices with their start and end apart: 105 -> 105, of which waited for: 50 -> 47; matrix products, arithmetic and copies ran while one was open for 6% -> 6% of each run, Pallas kernels for 24% -> 24%
where the time goes in v4:
time: 495 us; the launch traced here: 486 us
  Pallas kernels  167 us (34%)
  starting transfers between devices  141 us (28%)
  waiting for transfers between devices  121 us (24%)
  other arithmetic  21 us (4%)
  local copies, waits for them, and re-layouts  17.4 us (4%)
  between operations  16 us (3%)
    ppermute x87, starting transfers between devices, send_xor(): return lax.ppermute(value, axis, [(i, i ^ mask) for i in range(size)])  97.8 us
    ppermute x87, waiting for transfers between devices, send_xor(): return lax.ppermute(value, axis, [(i, i ^ mask) for i in range(size)])  96 us
    pallas_call x1, Pallas kernels, attend_back(): pl.pallas_call(functools.partial(attend_back_kernel, heads, scale, total,...  30.7 us
    pallas_call x4, Pallas kernels, weight_grads(): pl.pallas_call(functools.partial(weight_grads_kernel, chunked_left), grid...  23.7 us
    pallas_call x1, Pallas kernels, attend(): pl.pallas_call(functools.partial(attend_kernel, heads, total, groups, qb,...  18.7 us
    ppermute x3, starting transfers between devices, shards(): lax.ppermute(v, 'col', right_pairs(0, min(s - 1, chips - 2), cols_n))  16.3 us
    pallas_call x1, Pallas kernels, expert_second(): pl.pallas_call(functools.partial(expert_second_kernel, sub, count), in_sp...  16 us
    ppermute x3, waiting for transfers between devices, shards(): lax.ppermute(v, 'col', left_pairs(1, chips - s, cols_n))  14.4 us
  transfers between devices with their start and end apart: 105, of which 47 were waited for; matrix products, arithmetic and copies ran while one was open for 6% of the time, Pallas kernels for 24%

profile of v4, /device:TPU:0, one launch (start us, length us, event | category | flops | bytes accessed | tf_op | source)
XLA Modules:
  0.0 486.3 jit_solution(11457816600111057856)
XLA Ops:
  9.0 5.2 %collective-permute-start = (bf16[256,1024]{1,0:T(8,128)(2,1)}, bf16[256,1024]{1,0:T(8,128)(2,1)S(1)}, u32[]{:S(2)}, u32[]{:S(2)}) collective-permute-start(bf16[256,1024]{1,0:T(8,128)(2,1)} %tokens_ref.1), channel_id=1, source_target_pairs={{0,2},{1,3},{2,4},{3,5},{4,6},{5,7},{8,10},{9,11},{10,12},{11,13},... | collective-permute-start | bytes 1572872 | tf_op jit(solution)/shard_map/ppermute | solution.py:1340
  19.6 5.4 %collective-permute-done.1 = bf16[256,1024]{1,0:T(8,128)(2,1)S(1)} collective-permute-done((bf16[256,1024]{1,0:T(8,128)(2,1)}, bf16[256,1024]{1,0:T(8,128)(2,1)S(1)}, u32[]{:S(2)}, u32[]{:S(2)}) %collective-permute-start.1) | collective-permute-done | bytes 524320 | tf_op jit(solution)/shard_map/ppermute | solution.py:1341
  37.3 8.1 %collective-permute-done.5 = bf16[256,1024]{1,0:T(8,128)(2,1)S(1)} collective-permute-done((bf16[256,1024]{1,0:T(8,128)(2,1)S(1)}, bf16[256,1024]{1,0:T(8,128)(2,1)S(1)}, u32[]{:S(2)}, u32[]{:S(2)}) %collective-permute-start.5) | collective-permute-done | bytes 524320 | tf_op jit(solution)/shard_map/ppermute | solution.py:1341
  76.2 9.4 %project.1 = (bf16[8,256,1024]{2,1,0:T(8,128)(2,1)}, bf16[8,256,128]{2,1,0:T(8,128)(2,1)}, bf16[8,256,128]{2,1,0:T(8,128)(2,1)}, bf16[8,256,128]{2,1,0:T(8,128)(...) custom-call(f32[1,1024]{1,0:T(1,128)} %reshape.196.gain_ref, f32[1,1024]{1,0:T(1,128)} %reshape.197.shift_ref, ...), custom_call_target="tpu_custom_call" | custom-call | flops 1631584256 | bytes 11796480 | tf_op jit(solution)/shard_map/project/pallas_call | solution.py:455
  85.6 18.7 %attend.1 = (bf16[128,256]{1,0:T(8,128)(2,1)}, bf16[128,256]{1,0:T(8,128)(2,1)}, bf16[128,256]{1,0:T(8,128)(2,1)}, bf16[128,256]{1,0:T(8,128)(2,1)}, bf16[128,25...) custom-call(s32[2]{0:T(128)} %pad_add_fusion.me_ref, ...), custom_call_target="tpu_custom_call" | custom-call | flops 2147483648 | bytes 2621440 | tf_op jit(solution)/shard_map/attend/pallas_call | solution.py:589
  126.5 4.2 forward_rows.1
  145.8 6.5 %collective-permute-done.33.refs_5_ = bf16[32,1152]{1,0:T(8,128)(2,1)S(1)} collective-permute-done((bf16[32,1152]{1,0:T(8,128)(2,1)}, bf16[32,1152]{1,0:T(8,128)(2,1)S(1)}, u32[]{:S(2)}, u32[]{:S(2)}) %collective-permute-start.33) | collective-permute-done | bytes 73760 | tf_op jit(solution)/shard_map/ppermute | solution.py:29
  159.8 6.0 %collective-permute-done.40.refs_1_.refs_17_ = bf16[128,1152]{1,0:T(8,128)(2,1)S(1)} collective-permute-done((bf16[128,1152]{1,0:T(8,128)(2,1)}, bf16[128,1152]{1,0:T(8,128)(2,1)S(1)}, u32[]{:S(2)}, u32[]{:S(2)}) %collective-permute-start.40) | collective-permute-done | bytes 294944 | tf_op jit(solution)/shard_map/ppermute | solution.py:29
  168.9 5.2 %collective-permute-done.41.refs_2_.refs_18_ = bf16[128,1152]{1,0:T(8,128)(2,1)S(1)} collective-permute-done((bf16[128,1152]{1,0:T(8,128)(2,1)}, bf16[128,1152]{1,0:T(8,128)(2,1)S(1)}, u32[]{:S(2)}, u32[]{:S(2)}) %collective-permute-start.41) | collective-permute-done | bytes 294944 | tf_op jit(solution)/shard_map/ppermute | solution.py:29
  174.2 4.6 collective-permute-done.42.refs_3_.refs_19_
  179.6 11.1 %expert_first.1 = (bf16[128,1024]{1,0:T(8,128)(2,1)}, bf16[128,1024]{1,0:T(8,128)(2,1)}, bf16[128,1024]{1,0:T(8,128)(2,1)}, bf16[128,1024]{1,0:T(8,128)(2,1)}, b...) custom-call(bf16[2,1,512]{2,1,0:T(2,128)(2,1)} %bitcast.135, ...), custom_call_target="tpu_custom_call" | custom-call | flops 4294967296 | bytes 8388608 | tf_op jit(solution)/shard_map/expert_first/pallas_call | solution.py:925
  194.9 5.4 %collective-permute-done.47 = bf16[128,1024]{1,0:T(8,128)(2,1)S(1)} collective-permute-done((bf16[128,1024]{1,0:T(8,128)(2,1)}, bf16[128,1024]{1,0:T(8,128)(2,1)S(1)}, u32[]{:S(2)}, u32[]{:S(2)}) %collective-permute-start.47) | collective-permute-done | bytes 262176 | tf_op jit(solution)/shard_map/ppermute | solution.py:29
  215.0 5.2 %collective-permute-done.52.refs_9_ = bf16[128,1024]{1,0:T(8,128)(2,1)S(1)} collective-permute-done((bf16[128,1024]{1,0:T(8,128)(2,1)S(1)}, bf16[128,1024]{1,0:T(8,128)(2,1)S(1)}, u32[]{:S(2)}, u32[]{:S(2)}) %collective-permute-start.52) | collective-permute-done | bytes 262176 | tf_op jit(solution)/shard_map/ppermute | solution.py:29
  229.4 16.0 %expert_second.1 = (bf16[128,1024]{1,0:T(8,128)(2,1)}, bf16[128,1024]{1,0:T(8,128)(2,1)}, bf16[128,1024]{1,0:T(8,128)(2,1)}, bf16[128,1024]{1,0:T(8,128)(2,1)}, ...) custom-call(bf16[2,1,512]{2,1,0:T(2,128)(2,1)} %bitcast.134, ...), custom_call_target="tpu_custom_call" | custom-call | flops 6442450944 | bytes 12582912 | tf_op jit(solution)/shard_map/expert_second/pallas_call | solution.py:1080
  249.5 4.0 collective-permute-done.59
  258.0 8.2 %expert_branch.1 = (bf16[1024,1024]{1,0:T(8,128)(2,1)}, bf16[1024,128]{1,0:T(8,128)(2,1)}) custom-call(s32[2]{0:T(128)} %pad_add_fusion.me_ref, bf16[2,1024,512]{2,1,0:T(8,128)(2,1)} %get-tuple-element.365.hidden_in.left_ref, bf16[1,2,1024,1024]{3,2,1,0:T(8,128)(2,1)} %w_back.7, bf16[128,1024]{1,0:T(8,128)(2,1)} %copy-done.16, bf16[128,1024]{1,0:T(8,128)(2,1)} %copy-done.34, ...), custom_call_target="tpu_custom_call" | custom-call | flops 2147483648 | bytes 8388608 | tf_op jit(solution)/shard_map/expert_branch/pallas_call | solution.py:1050
  280.2 5.8 %weight_grads.4.refs_0_ = f32[1,2,1024,1024]{3,2,1,0:T(8,128)} custom-call(bf16[2,1024,512]{2,1,0:T(8,128)(2,1)} %get-tuple-element.365.hidden_in.left_ref, bf16[1024,1024]{1,0:T(8,128)(2,1)} %get-tuple-element.388.right_ref), custom_call_target="tpu_custom_call" | custom-call | flops 2147483648 | bytes 8388608 | tf_op jit(solution)/shard_map/weight_grads/pallas_call | solution.py:1208
  287.0 12.8 %expert_back.1 = (bf16[128,1152]{1,0:T(8,128)(2,1)}, bf16[128,1152]{1,0:T(8,128)(2,1)}, bf16[128,1152]{1,0:T(8,128)(2,1)}, bf16[128,1152]{1,0:T(8,128)(2,1)}, bf...) custom-call(bf16[1024,128]{1,0:T(8,128)(2,1)} %get-tuple-element.376, ...), custom_call_target="tpu_custom_call" | custom-call | flops 4294967296 | bytes 10485760 | tf_op jit(solution)/shard_map/expert_back/pallas_call | solution.py:1156
  304.0 5.4 %collective-permute-done.71 = bf16[128,1152]{1,0:T(8,128)(2,1)S(1)} collective-permute-done((bf16[128,1152]{1,0:T(8,128)(2,1)}, bf16[128,1152]{1,0:T(8,128)(2,1)S(1)}, u32[]{:S(2)}, u32[]{:S(2)}) %collective-permute-start.71) | collective-permute-done | bytes 294944 | tf_op jit(solution)/shard_map/ppermute | solution.py:29
  320.6 4.3 leave_back.1
  325.0 4.7 collective-permute-start.77
  336.8 6.0 %weight_grads.5.refs_0_ = f32[1,2,1024,1024]{3,2,1,0:T(8,128)} custom-call(bf16[1024,1024]{1,0:T(8,128)(2,1)} %get-tuple-element.345.left_ref, bf16[2,1024,512]{2,1,0:T(8,128)(2,1)} %get-tuple-element.415.right_ref), custom_call_target="tpu_custom_call" | custom-call | flops 2147483648 | bytes 8388608 | tf_op jit(solution)/shard_map/weight_grads/pallas_call | solution.py:1208
  345.9 5.0 %backward_rows.1 = (f32[256,1024]{1,0:T(8,128)}, bf16[256,1024]{1,0:T(8,128)(2,1)}, f32[128,1024]{1,0:T(8,128)}, bf16[1024,256]{1,0:T(8,128)(2,1)}) custom-call(s32[2]{0:T(128)} %pad_add_fusion.me_ref, bf16[8,4,256,128]{3,2,1,0:T(8,128)(2,1)} %bitcast.109, bf16[256,256]{1,0:T(8,128)(2,1)} %get-tuple-element.289.unroute_ref, bf16[256,1024]{1,0:T(8,128)(2,1)} %cot_ref.1, ...), custom_call_target="tpu_custom_call" | custom-call | flops 805306368 | bytes 5242880 | tf_op jit(solution)/shard_map/backward_rows/pallas_call | solution.py:393
  350.8 5.2 %all-to-all-start.1 = ((bf16[8,128,256]{2,1,0:T(8,128)(2,1)}), bf16[8,128,256]{2,1,0:T(8,128)(2,1)S(1)}, u32[]{:S(2)}, u32[]{:S(2)}) async-start(bf16[8,128,256]{2,1,0:T(8,128)(2,1)} %bitcast.116), calls=%async_computation.2 | async-start | bytes 1048576 | tf_op jit(solution)/shard_map/all_to_all | solution.py:1310
  359.4 5.8 %weight_grads.6 = f32[1,2,1024,1024]{3,2,1,0:T(8,128)} custom-call(bf16[2,1024,512]{2,1,0:T(8,128)(2,1)} %get-tuple-element.438.left_ref, bf16[1024,1024]{1,0:T(8,128)(2,1)} %get-tuple-element.440.right_ref, f32[1,2,1024,1024]{3,2,1,0:T(8,128)} %weight_grads.4.refs_0_), custom_call_target="tpu_custom_call", output_to_operand_aliasing={{}: (2, {})} | custom-call | flops 2147483648 | bytes 8388608 | tf_op jit(solution)/shard_map/weight_grads/pallas_call | solution.py:1208
  376.0 30.7 %attend_back.1 = (bf16[272,1024]{1,0:T(8,128)(2,1)}, bf16[272,1024]{1,0:T(8,128)(2,1)}, bf16[272,1024]{1,0:T(8,128)(2,1)}, bf16[272,1024]{1,0:T(8,128)(2,1)}, bf...) custom-call(s32[8]{0:T(128)} %stack.97.order_ref, ...), custom_call_target="tpu_custom_call" | custom-call | flops 5368709120 | bytes 5242880 | tf_op jit(solution)/shard_map/attend_back/pallas_call | solution.py:737
  409.4 4.7 collective-permute-start.84
  417.3 6.9 %project_grads.1 = bf16[1024,384]{1,0:T(8,128)(2,1)} custom-call(s32[8]{0:T(128)} %stack.97.order_ref, bf16[8,256,128]{2,1,0:T(8,128)(2,1)} %get-tuple-element.461.dq_ref, bf16[8,256,128]{2,1,0:T(8,128)(2,1)} %get-tuple-element.462.dk_ref, bf16[8,256,128]{2,1,0:T(8,128)(2,1)} %get-tuple-element.463.dv_ref, ...), custom_call_target="tpu_custom_call" | custom-call | flops 1610612736 | bytes 6553600 | tf_op jit(solution)/shard_map/project_grads/pallas_call | solution.py:796
  428.1 5.1 %collective-permute-start.88 = (bf16[272,1024]{1,0:T(8,128)(2,1)S(1)}, bf16[272,1024]{1,0:T(8,128)(2,1)S(1)}, u32[]{:S(2)}, u32[]{:S(2)}) collective-permute-start(bf16[272,1024]{1,0:T(8,128)(2,1)S(1)} %get-tuple-element.543), channel_id=1, source_target_pairs={{0,2},{1,3},{2,4},{3,5},{8,10},{9,11},{10,12},{11,13},{16,18},{17,... | collective-permute-start | bytes 1671176 | tf_op jit(solution)/shard_map/ppermute | solution.py:1466
  438.1 5.5 %collective-permute-done.92 = bf16[256,512]{1,0:T(8,128)(2,1)S(1)} collective-permute-done((bf16[256,512]{1,0:T(8,128)(2,1)S(1)}, bf16[256,512]{1,0:T(8,128)(2,1)S(1)}, u32[]{:S(2)}, u32[]{:S(2)}) %collective-permute-start.92) | collective-permute-done | bytes 262176 | tf_op jit(solution)/shard_map/ppermute | solution.py:29
  449.8 6.4 %collective-permute-start.94 = (bf16[272,1024]{1,0:T(8,128)(2,1)}, bf16[272,1024]{1,0:T(8,128)(2,1)S(1)}, u32[]{:S(2)}, u32[]{:S(2)}) collective-permute-start(bf16[272,1024]{1,0:T(8,128)(2,1)} %add_convert_fusion.1), channel_id=1, source_target_pairs={{0,2},{1,3},{2,4},{3,5},{4,6},{5,7},{8,10},{9,11},{10,12},{11,13},... | collective-permute-start | bytes 1671176 | tf_op jit(solution)/shard_map/ppermute | solution.py:1466
  456.2 6.1 %weight_grads.7 = f32[1,2,1024,1024]{3,2,1,0:T(8,128)} custom-call(bf16[1024,1024]{1,0:T(8,128)(2,1)} %get-tuple-element.481.left_ref, bf16[2,1024,512]{2,1,0:T(8,128)(2,1)} %get-tuple-element.482.right_ref, f32[1,2,1024,1024]{3,2,1,0:T(8,128)} %weight_grads.5.refs_0_), custom_call_target="tpu_custom_call", output_to_operand_aliasing={{}: (2, {})} | custom-call | flops 2147483648 | bytes 8388608 | tf_op jit(solution)/shard_map/weight_grads/pallas_call | solution.py:1208
  (495 shorter events, 226.4 us)
Async XLA Ops:
  7.2 119.2 %all-gather.2.cloned.1.call-start = ((), (), s32[]{:S(2)}) async-start(), calls=%async_computation.5 | async-start | bytes 2359296 | tf_op jit(solution)/shard_map/all_gather | solution.py:1302
  7.7 17.3 %collective-permute-start.1 = (bf16[256,1024]{1,0:T(8,128)(2,1)}, bf16[256,1024]{1,0:T(8,128)(2,1)S(1)}, u32[]{:S(2)}, u32[]{:S(2)}) collective-permute-start(bf16[256,1024]{1,0:T(8,128)(2,1)} %tokens_ref.1), channel_id=1, source_target_pairs={{2,0},{3,1},{4,2},{5,3},{6,4},{7,5},{10,8},{11,9},{12,10},{13,11},... | collective-permute-start | bytes 1572872 | tf_op jit(solution)/shard_map/ppermute | solution.py:1341
  9.0 17.3 %collective-permute-start = (bf16[256,1024]{1,0:T(8,128)(2,1)}, bf16[256,1024]{1,0:T(8,128)(2,1)S(1)}, u32[]{:S(2)}, u32[]{:S(2)}) collective-permute-start(bf16[256,1024]{1,0:T(8,128)(2,1)} %tokens_ref.1), channel_id=1, source_target_pairs={{0,2},{1,3},{2,4},{3,5},{4,6},{5,7},{8,10},{9,11},{10,12},{11,13},... | collective-permute-start | bytes 1572872 | tf_op jit(solution)/shard_map/ppermute | solution.py:1340
  27.0 18.4 %collective-permute-start.5 = (bf16[256,1024]{1,0:T(8,128)(2,1)S(1)}, bf16[256,1024]{1,0:T(8,128)(2,1)S(1)}, u32[]{:S(2)}, u32[]{:S(2)}) collective-permute-start(bf16[256,1024]{1,0:T(8,128)(2,1)S(1)} %collective-permute-done.1), channel_id=1, source_target_pairs={{2,0},{3,1},{4,2},{5,3},{10,8},{11,9},{12,10},{13,11},{18,16},{19,... | collective-permute-start | bytes 1572872 | tf_op jit(solution)/shard_map/ppermute | solution.py:1341
  52.4 13.1 %collective-permute-start.11 = (bf16[256,1024]{1,0:T(8,128)(2,1)S(1)}, bf16[256,1024]{1,0:T(8,128)(2,1)S(1)}, u32[]{:S(2)}, u32[]{:S(2)}) collective-permute-start(bf16[256,1024]{1,0:T(8,128)(2,1)S(1)} %collective-permute-done.5), channel_id=1, source_target_pairs={{2,0},{3,1},{10,8},{11,9},{18,16},{19,17},{26,24},{27,25}} | collective-permute-start | bytes 1572872 | tf_op jit(solution)/shard_map/ppermute | solution.py:1341
  70.2 34.2 %all-to-all-start = ((bf16[8,32,1024]{2,1,0:T(8,128)(2,1)}), bf16[8,32,1024]{2,1,0:T(8,128)(2,1)S(1)}, u32[]{:S(2)}, u32[]{:S(2)}) async-start(bf16[8,32,1024]{2,1,0:T(8,128)(2,1)} %bitcast.36), calls=%async_computation | async-start | bytes 1048576 | tf_op jit(solution)/shard_map/all_to_all | solution.py:1310
  74.0 291.2 %reduce-scatter.3.cloned.1.call-start = ((), (), s32[]{:S(2)}) async-start(), calls=%async_computation.6 | async-start | bytes 2621440 | tf_op jit(solution)/shard_map/reduce_scatter | solution.py:1437
  104.5 16.9 %collective-permute-start.28 = (bf16[128,1024]{1,0:T(8,128)(2,1)S(1)}, bf16[128,1024]{1,0:T(8,128)(2,1)S(1)}, u32[]{:S(2)}, u32[]{:S(2)}) collective-permute-start(bf16[128,1024]{1,0:T(8,128)(2,1)S(1)} %get-tuple-element.350.refs_4_), channel_id=1, source_target_pairs={{0,16},{8,24},{16,0},{24,8},{1,17},{9,25},{17,1},{25,9},{2,18},{10... | collective-permute-start | bytes 786440 | tf_op jit(solution)/shard_map/ppermute | solution.py:29
  106.1 15.3 %collective-permute-start.27 = (bf16[128,1024]{1,0:T(8,128)(2,1)S(1)}, bf16[128,1024]{1,0:T(8,128)(2,1)S(1)}, u32[]{:S(2)}, u32[]{:S(2)}) collective-permute-start(bf16[128,1024]{1,0:T(8,128)(2,1)S(1)} %get-tuple-element.346.refs_0_), channel_id=1, source_target_pairs={{0,8},{8,0},{16,24},{24,16},{1,9},{9,1},{17,25},{25,17},{2,10},{10... | collective-permute-start | bytes 786440 | tf_op jit(solution)/shard_map/ppermute | solution.py:29
  122.6 13.3 %collective-permute-start.37 = (bf16[128,1024]{1,0:T(8,128)(2,1)S(1)}, bf16[128,1024]{1,0:T(8,128)(2,1)S(1)}, u32[]{:S(2)}, u32[]{:S(2)}) collective-permute-start(bf16[128,1024]{1,0:T(8,128)(2,1)S(1)} %collective-permute-done.27.refs_1_), channel_id=1, source_target_pairs={{0,16},{8,24},{16,0},{24,8},{1,17},{9,25},{17,1},{25,9},{2,18},{10... | collective-permute-start | bytes 786440 | tf_op jit(solution)/shard_map/ppermute | solution.py:29
  123.5 14.3 %collective-permute-start.38 = (bf16[128,1024]{1,0:T(8,128)(2,1)S(1)}, bf16[128,1024]{1,0:T(8,128)(2,1)S(1)}, u32[]{:S(2)}, u32[]{:S(2)}) collective-permute-start(bf16[128,1024]{1,0:T(8,128)(2,1)S(1)} %get-tuple-element.350.refs_4_), channel_id=1, source_target_pairs={{0,8},{8,0},{16,24},{24,16},{1,9},{9,1},{17,25},{25,17},{2,10},{10... | collective-permute-start | bytes 786440 | tf_op jit(solution)/shard_map/ppermute | solution.py:29
  125.7 14.5 %collective-permute-start.39 = (bf16[128,1024]{1,0:T(8,128)(2,1)S(1)}, bf16[128,1024]{1,0:T(8,128)(2,1)S(1)}, u32[]{:S(2)}, u32[]{:S(2)}) collective-permute-start(bf16[128,1024]{1,0:T(8,128)(2,1)S(1)} %collective-permute-done.28.refs_6_), channel_id=1, source_target_pairs={{0,8},{8,0},{16,24},{24,16},{1,9},{9,1},{17,25},{25,17},{2,10},{10... | collective-permute-start | bytes 786440 | tf_op jit(solution)/shard_map/ppermute | solution.py:29
  130.8 13.1 %collective-permute-start.30 = (bf16[32,1152]{1,0:T(8,128)(2,1)}, bf16[32,1152]{1,0:T(8,128)(2,1)S(1)}, u32[]{:S(2)}, u32[]{:S(2)}) collective-permute-start(bf16[32,1152]{1,0:T(8,128)(2,1)} %get-tuple-element.325), channel_id=1, source_target_pairs={{0,2},{1,3},{2,0},{3,1},{4,6},{5,7},{6,4},{7,5},{8,10},{9,11},{10,... | collective-permute-start | bytes 221192 | tf_op jit(solution)/shard_map/ppermute | solution.py:29
  158.2 16.0 %collective-permute-start.41 = (bf16[128,1152]{1,0:T(8,128)(2,1)}, bf16[128,1152]{1,0:T(8,128)(2,1)S(1)}, u32[]{:S(2)}, u32[]{:S(2)}) collective-permute-start(bf16[128,1152]{1,0:T(8,128)(2,1)} %get-tuple-element.343.refs_0_.refs_16_), channel_id=1, source_target_pairs={{0,16},{8,24},{16,0},{24,8},{1,17},{9,25},{17,1},{25,9},{2,18},{10... | collective-permute-start | bytes 884744 | tf_op jit(solution)/shard_map/ppermute | solution.py:29
  159.7 14.5 %collective-permute-start.43 = (bf16[128,1152]{1,0:T(8,128)(2,1)}, bf16[128,1152]{1,0:T(8,128)(2,1)S(1)}, u32[]{:S(2)}, u32[]{:S(2)}) collective-permute-start(bf16[128,1152]{1,0:T(8,128)(2,1)} %get-tuple-element.344.refs_4_.refs_20_), channel_id=1, source_target_pairs={{0,8},{8,0},{16,24},{24,16},{1,9},{9,1},{17,25},{25,17},{2,10},{10... | collective-permute-start | bytes 884744 | tf_op jit(solution)/shard_map/ppermute | solution.py:29
  191.9 14.0 %collective-permute-start.46 = (bf16[128,1024]{1,0:T(8,128)(2,1)}, bf16[128,1024]{1,0:T(8,128)(2,1)S(1)}, u32[]{:S(2)}, u32[]{:S(2)}) collective-permute-start(bf16[128,1024]{1,0:T(8,128)(2,1)} %get-tuple-element.356), channel_id=1, source_target_pairs={{0,8},{8,0},{16,24},{24,16},{1,9},{9,1},{17,25},{25,17},{2,10},{10... | collective-permute-start | bytes 786440 | tf_op jit(solution)/shard_map/ppermute | solution.py:29
  246.9 19.4 %collective-permute-start.58 = (bf16[128,1024]{1,0:T(8,128)(2,1)}, bf16[128,1024]{1,0:T(8,128)(2,1)S(1)}, u32[]{:S(2)}, u32[]{:S(2)}) collective-permute-start(bf16[128,1024]{1,0:T(8,128)(2,1)} %get-tuple-element.369), channel_id=1, source_target_pairs={{0,8},{8,0},{16,24},{24,16},{1,9},{9,1},{17,25},{25,17},{2,10},{10... | collective-permute-start | bytes 786440 | tf_op jit(solution)/shard_map/ppermute | solution.py:29
  248.0 18.3 %collective-permute-start.61 = (bf16[128,1024]{1,0:T(8,128)(2,1)}, bf16[128,1024]{1,0:T(8,128)(2,1)S(1)}, u32[]{:S(2)}, u32[]{:S(2)}) collective-permute-start(bf16[128,1024]{1,0:T(8,128)(2,1)} %get-tuple-element.373), channel_id=1, source_target_pairs={{0,16},{8,24},{16,0},{24,8},{1,17},{9,25},{17,1},{25,9},{2,18},{10... | collective-permute-start | bytes 786440 | tf_op jit(solution)/shard_map/ppermute | solution.py:29
  272.9 13.1 %collective-permute-start.65 = (bf16[128,1024]{1,0:T(8,128)(2,1)}, bf16[128,1024]{1,0:T(8,128)(2,1)S(1)}, u32[]{:S(2)}, u32[]{:S(2)}) collective-permute-start(bf16[128,1024]{1,0:T(8,128)(2,1)} %get-tuple-element.391.refs_0_), channel_id=1, source_target_pairs={{0,16},{8,24},{16,0},{24,8},{1,17},{9,25},{17,1},{25,9},{2,18},{10... | collective-permute-start | bytes 786440 | tf_op jit(solution)/shard_map/ppermute | solution.py:29
  300.8 13.2 %collective-permute-start.70 = (bf16[128,1152]{1,0:T(8,128)(2,1)}, bf16[128,1152]{1,0:T(8,128)(2,1)S(1)}, u32[]{:S(2)}, u32[]{:S(2)}) collective-permute-start(bf16[128,1152]{1,0:T(8,128)(2,1)} %get-tuple-element.401), channel_id=1, source_target_pairs={{0,8},{8,0},{16,24},{24,16},{1,9},{9,1},{17,25},{25,17},{2,10},{10... | collective-permute-start | bytes 884744 | tf_op jit(solution)/shard_map/ppermute | solution.py:29
  329.7 13.1 %collective-permute-start.78 = (bf16[32,1152]{1,0:T(8,128)(2,1)}, bf16[32,1152]{1,0:T(8,128)(2,1)S(1)}, u32[]{:S(2)}, u32[]{:S(2)}) collective-permute-start(bf16[32,1152]{1,0:T(8,128)(2,1)} %get-tuple-element.419), channel_id=1, source_target_pairs={{0,3},{1,2},{2,1},{3,0},{4,7},{5,6},{6,5},{7,4},{8,11},{9,10},{10,... | collective-permute-start | bytes 221192 | tf_op jit(solution)/shard_map/ppermute | solution.py:29
  329.8 13.0 %collective-permute-start.79 = (bf16[32,1152]{1,0:T(8,128)(2,1)}, bf16[32,1152]{1,0:T(8,128)(2,1)S(1)}, u32[]{:S(2)}, u32[]{:S(2)}) collective-permute-start(bf16[32,1152]{1,0:T(8,128)(2,1)} %get-tuple-element.420), channel_id=1, source_target_pairs={{0,4},{1,5},{2,6},{3,7},{4,0},{5,1},{6,2},{7,3},{8,12},{9,13},{10,... | collective-permute-start | bytes 221192 | tf_op jit(solution)/shard_map/ppermute | solution.py:29
  350.8 20.6 %all-to-all-start.1 = ((bf16[8,128,256]{2,1,0:T(8,128)(2,1)}), bf16[8,128,256]{2,1,0:T(8,128)(2,1)S(1)}, u32[]{:S(2)}, u32[]{:S(2)}) async-start(bf16[8,128,256]{2,1,0:T(8,128)(2,1)} %bitcast.116), calls=%async_computation.2 | async-start | bytes 1048576 | tf_op jit(solution)/shard_map/all_to_all | solution.py:1310
  356.1 69.4 %reduce-scatter.5.cloned.1.call-start = ((), (), s32[]{:S(2)}) async-start(), calls=%async_computation.7 | async-start | bytes 2359296 | tf_op jit(solution)/shard_map/reduce_scatter | solution.py:1454
  372.2 34.5 %all-to-all-start.2 = ((bf16[8,32,1024]{2,1,0:T(8,128)(2,1)}), bf16[8,32,1024]{2,1,0:T(8,128)(2,1)S(1)}, u32[]{:S(2)}, u32[]{:S(2)}) async-start(bf16[8,32,1024]{2,1,0:T(8,128)(2,1)} %bitcast.45), calls=%async_computation.3 | async-start | bytes 1048576 | tf_op jit(solution)/shard_map/all_to_all | solution.py:1310
  407.8 17.6 %collective-permute-start.87 = (bf16[272,1024]{1,0:T(8,128)(2,1)}, bf16[272,1024]{1,0:T(8,128)(2,1)}, u32[]{:S(2)}, u32[]{:S(2)}) collective-permute-start(bf16[272,1024]{1,0:T(8,128)(2,1)} %get-tuple-element.467), channel_id=1, source_target_pairs={{0,1},{1,0},{2,3},{3,2},{4,5},{5,4},{6,7},{7,6},{8,9},{9,8},{10,11... | collective-permute-start | bytes 1671176 | tf_op jit(solution)/shard_map/ppermute | solution.py:29
  409.4 16.1 %collective-permute-start.84 = (bf16[272,1024]{1,0:T(8,128)(2,1)S(1)}, bf16[272,1024]{1,0:T(8,128)(2,1)}, u32[]{:S(2)}, u32[]{:S(2)}) collective-permute-start(bf16[272,1024]{1,0:T(8,128)(2,1)S(1)} %add_convert_fusion.5), channel_id=1, source_target_pairs={{0,2},{1,3},{8,10},{9,11},{16,18},{17,19},{24,26},{25,27}} | collective-permute-start | bytes 1671176 | tf_op jit(solution)/shard_map/ppermute | solution.py:1466
  427.4 19.1 %collective-permute-start.89 = (bf16[272,1024]{1,0:T(8,128)(2,1)S(1)}, bf16[272,1024]{1,0:T(8,128)(2,1)S(1)}, u32[]{:S(2)}, u32[]{:S(2)}) collective-permute-start(bf16[272,1024]{1,0:T(8,128)(2,1)S(1)} %get-tuple-element.542), channel_id=1, source_target_pairs={{4,2},{5,3},{6,4},{7,5},{12,10},{13,11},{14,12},{15,13},{20,18},{2... | collective-permute-start | bytes 1671176 | tf_op jit(solution)/shard_map/ppermute | solution.py:1469
  428.1 18.4 %collective-permute-start.88 = (bf16[272,1024]{1,0:T(8,128)(2,1)S(1)}, bf16[272,1024]{1,0:T(8,128)(2,1)S(1)}, u32[]{:S(2)}, u32[]{:S(2)}) collective-permute-start(bf16[272,1024]{1,0:T(8,128)(2,1)S(1)} %get-tuple-element.543), channel_id=1, source_target_pairs={{0,2},{1,3},{2,4},{3,5},{8,10},{9,11},{10,12},{11,13},{16,18},{17,... | collective-permute-start | bytes 1671176 | tf_op jit(solution)/shard_map/ppermute | solution.py:1466
  443.7 24.0 %collective-permute-start.93 = (bf16[272,1024]{1,0:T(8,128)(2,1)}, bf16[272,1024]{1,0:T(8,128)(2,1)S(1)}, u32[]{:S(2)}, u32[]{:S(2)}) collective-permute-start(bf16[272,1024]{1,0:T(8,128)(2,1)} %get-tuple-element.475), channel_id=1, source_target_pairs={{0,1},{1,0},{2,3},{3,2},{4,5},{5,4},{6,7},{7,6},{8,9},{9,8},{10,11... | collective-permute-start | bytes 1671176 | tf_op jit(solution)/shard_map/ppermute | solution.py:29
  448.5 17.9 %collective-permute-start.95 = (bf16[272,1024]{1,0:T(8,128)(2,1)}, bf16[272,1024]{1,0:T(8,128)(2,1)S(1)}, u32[]{:S(2)}, u32[]{:S(2)}) collective-permute-start(bf16[272,1024]{1,0:T(8,128)(2,1)} %add_convert_fusion), channel_id=1, source_target_pairs={{2,0},{3,1},{4,2},{5,3},{6,4},{7,5},{10,8},{11,9},{12,10},{13,11},... | collective-permute-start | bytes 1671176 | tf_op jit(solution)/shard_map/ppermute | solution.py:1469
  449.8 17.8 %collective-permute-start.94 = (bf16[272,1024]{1,0:T(8,128)(2,1)}, bf16[272,1024]{1,0:T(8,128)(2,1)S(1)}, u32[]{:S(2)}, u32[]{:S(2)}) collective-permute-start(bf16[272,1024]{1,0:T(8,128)(2,1)} %add_convert_fusion.1), channel_id=1, source_target_pairs={{0,2},{1,3},{2,4},{3,5},{4,6},{5,7},{8,10},{9,11},{10,12},{11,13},... | collective-permute-start | bytes 1671176 | tf_op jit(solution)/shard_map/ppermute | solution.py:1466
  (173 other events, 1590.7 us)
Sparse Core Ops, SparseCore 0:
  68.3 39.4 all-gather.1
  320.1 38.5 reduce-scatter.2
  371.6 37.7 reduce-scatter.4

commit v5 on v4

--- a/solution.py
+++ b/solution.py
@@ -426,11 +426,14 @@
     blocks, outs, refs = refs[:count], refs[count : count + 6], refs[count + 6 :]
     x_all, held, sems, out_sems = refs[0], refs[1:7], refs[7], refs[8]
     fw = w_ref.shape[1] // 3
-    copies = begin([(b, x_all.at[n]) for n, b in enumerate(blocks)], sems)
-    leaving = []
-    for n in range(count):
-        copies[n].wait()
-        unit_rows, unused = layer_stats(x_all[n].astype(F32))
+    begin([(b, x_all.at[n]) for n, b in enumerate(blocks)], sems)
+
+    def leaving(n):
+        return copies_of([(h.at[n], o.at[n]) for h, o in zip(held, outs)], out_sems.at[pl.ds(6 * n, 6)])
+
+    def one(n, unused):
+        pltpu.make_async_copy(blocks[0], x_all.at[n], sems.at[n]).wait()
+        unit_rows, unused_root = layer_stats(x_all[n].astype(F32))
         normed = (unit_rows * gain_ref[...] + shift_ref[...]).astype(BF)
         held[0][n] = normed
         out = dot(normed, w_ref[...])
@@ -441,10 +444,13 @@
         held[3][n] = values.astype(BF)
         held[4][n] = keys.T.astype(BF)
         held[5][n] = values.T.astype(BF)
-        leaving += begin(
-            [(h.at[n], o.at[n]) for h, o in zip(held, outs)], out_sems.at[pl.ds(6 * n, 6)]
-        )
-    finish(leaving)
+        for copy in leaving(n):
+            copy.start()
+        return unused
+
+    lax.fori_loop(0, count, one, 0)
+    for n in range(count):
+        finish(leaving(n))
 
 
 def project(blocks, gain, shift, w, scale):
@@ -767,7 +773,7 @@
 
 
 def project_grads_kernel(total, groups, parts, order_ref, dq_ref, dk_ref, dv_ref, *refs):
-    normed_in, (out_ref, normed_all, sems) = views(refs[:groups]), refs[groups:]
+    normed_in, (out_ref, normed_all, grads_all, sems) = views(refs[:groups]), refs[groups:]
     rows = dq_ref.shape[1]
     copies = begin(
         [
@@ -776,18 +782,20 @@
         ],
         sems,
     )
-    grads = jnp.concatenate(
+    grads_all[...] = jnp.concatenate(
         [ref[...].reshape(total * rows, ref.shape[2]) for ref in (dq_ref, dk_ref, dv_ref)], axis=1
     )
     finish(copies)
     step = out_ref.shape[0] // parts
-    for n in range(parts):
-        out_ref[n * step : (n + 1) * step, :] = lax.dot_general(
-            normed_all[:, n * step : (n + 1) * step],
-            grads,
-            (((0,), (0,)), ((), ())),
-            preferred_element_type=F32,
+
+    def one(n, unused):
+        at = pl.ds(pl.multiple_of(n * step, step), step)
+        out_ref[at, :] = lax.dot_general(
+            normed_all[:, at], grads_all[...], (((0,), (0,)), ((), ())), preferred_element_type=F32
         ).astype(BF)
+        return unused
+
+    lax.fori_loop(0, parts, one, 0)
 
 
 def project_grads(dq, dk, dv, normed, order, parts):
@@ -798,7 +806,11 @@
         in_specs=[SMEM] + [VMEM] * 3 + [ANY] * len(normed),
         out_specs=VMEM,
         out_shape=shape((width, 3 * fw), BF),
-        scratch_shapes=[pltpu.VMEM((total * rows, width), BF), pltpu.SemaphoreType.DMA((total,))],
+        scratch_shapes=[
+            pltpu.VMEM((total * rows, width), BF),
+            pltpu.VMEM((total * rows, 3 * fw), BF),
+            pltpu.SemaphoreType.DMA((total,)),
+        ],
         cost_estimate=pl.CostEstimate(
             flops=2 * total * rows * width * 3 * fw,
             bytes_accessed=2 * total * rows * (width + 3 * fw) + 2 * width * 3 * fw,

time: 495 us -> 490 us (0.990)
  transfers between devices with their start and end apart: 105 -> 105, of which waited for: 47 -> 48; matrix products, arithmetic and copies ran while one was open for 6% -> 6% of each run, Pallas kernels for 24% -> 24%
where the time goes in v5:
time: 490 us; the launch traced here: 486 us
  Pallas kernels  167 us (34%)
  starting transfers between devices  141 us (29%)
  waiting for transfers between devices  121 us (25%)
  other arithmetic  21 us (4%)
  local copies, waits for them, and re-layouts  17.4 us (4%)
  between operations  15.9 us (3%)
    ppermute x87, starting transfers between devices, send_xor(): return lax.ppermute(value, axis, [(i, i ^ mask) for i in range(size)])  97.3 us
    ppermute x87, waiting for transfers between devices, send_xor(): return lax.ppermute(value, axis, [(i, i ^ mask) for i in range(size)])  96.1 us
    pallas_call x1, Pallas kernels, attend_back(): pl.pallas_call(functools.partial(attend_back_kernel, heads, scale, total,...  30.7 us
    pallas_call x4, Pallas kernels, weight_grads(): pl.pallas_call(functools.partial(weight_grads_kernel, chunked_left), grid...  23.5 us
    pallas_call x1, Pallas kernels, attend(): pl.pallas_call(functools.partial(attend_kernel, heads, total, groups, qb,...  18.2 us
    ppermute x3, starting transfers between devices, shards(): lax.ppermute(v, 'col', right_pairs(0, min(s - 1, chips - 2), cols_n))  16.3 us
    pallas_call x1, Pallas kernels, expert_second(): pl.pallas_call(functools.partial(expert_second_kernel, sub, count), in_sp...  16 us
    ppermute x3, waiting for transfers between devices, shards(): lax.ppermute(v, 'col', left_pairs(1, chips - s, cols_n))  14.4 us
  transfers between devices with their start and end apart: 105, of which 48 were waited for; matrix products, arithmetic and copies ran while one was open for 6% of the time, Pallas kernels for 24%

profile of v5, /device:TPU:0, one launch (start us, length us, event | category | flops | bytes accessed | tf_op | source)
XLA Modules:
  0.0 485.8 jit_solution(7095891713452287199)
XLA Ops:
  9.0 5.2 %collective-permute-start = (bf16[256,1024]{1,0:T(8,128)(2,1)}, bf16[256,1024]{1,0:T(8,128)(2,1)S(1)}, u32[]{:S(2)}, u32[]{:S(2)}) collective-permute-start(bf16[256,1024]{1,0:T(8,128)(2,1)} %tokens_ref.1), channel_id=1, source_target_pairs={{0,2},{1,3},{2,4},{3,5},{4,6},{5,7},{8,10},{9,11},{10,12},{11,13},... | collective-permute-start | bytes 1572872 | tf_op jit(solution)/shard_map/ppermute | solution.py:1352
  19.6 5.4 %collective-permute-done.1 = bf16[256,1024]{1,0:T(8,128)(2,1)S(1)} collective-permute-done((bf16[256,1024]{1,0:T(8,128)(2,1)}, bf16[256,1024]{1,0:T(8,128)(2,1)S(1)}, u32[]{:S(2)}, u32[]{:S(2)}) %collective-permute-start.1) | collective-permute-done | bytes 524320 | tf_op jit(solution)/shard_map/ppermute | solution.py:1353
  37.3 8.1 %collective-permute-done.5 = bf16[256,1024]{1,0:T(8,128)(2,1)S(1)} collective-permute-done((bf16[256,1024]{1,0:T(8,128)(2,1)S(1)}, bf16[256,1024]{1,0:T(8,128)(2,1)S(1)}, u32[]{:S(2)}, u32[]{:S(2)}) %collective-permute-start.5) | collective-permute-done | bytes 524320 | tf_op jit(solution)/shard_map/ppermute | solution.py:1353
  76.7 9.4 %project.1 = (bf16[8,256,1024]{2,1,0:T(8,128)(2,1)}, bf16[8,256,128]{2,1,0:T(8,128)(2,1)}, bf16[8,256,128]{2,1,0:T(8,128)(2,1)}, bf16[8,256,128]{2,1,0:T(8,128)(...) custom-call(f32[1,1024]{1,0:T(1,128)} %reshape.196.gain_ref, f32[1,1024]{1,0:T(1,128)} %reshape.197.shift_ref, ...), custom_call_target="tpu_custom_call" | custom-call | flops 1631584256 | bytes 11796480 | tf_op jit(solution)/shard_map/project/pallas_call | solution.py:461
  86.1 18.2 %attend.1 = (bf16[128,256]{1,0:T(8,128)(2,1)}, bf16[128,256]{1,0:T(8,128)(2,1)}, bf16[128,256]{1,0:T(8,128)(2,1)}, bf16[128,256]{1,0:T(8,128)(2,1)}, bf16[128,25...) custom-call(s32[2]{0:T(128)} %pad_add_fusion.me_ref, ...), custom_call_target="tpu_custom_call" | custom-call | flops 2147483648 | bytes 2621440 | tf_op jit(solution)/shard_map/attend/pallas_call | solution.py:595
  126.4 4.2 forward_rows.1
  145.6 4.4 collective-permute-done.32.refs_4_
  159.7 6.0 %collective-permute-done.40.refs_1_.refs_17_ = bf16[128,1152]{1,0:T(8,128)(2,1)S(1)} collective-permute-done((bf16[128,1152]{1,0:T(8,128)(2,1)}, bf16[128,1152]{1,0:T(8,128)(2,1)S(1)}, u32[]{:S(2)}, u32[]{:S(2)}) %collective-permute-start.40) | collective-permute-done | bytes 294944 | tf_op jit(solution)/shard_map/ppermute | solution.py:29
  168.9 5.2 %collective-permute-done.41.refs_2_.refs_18_ = bf16[128,1152]{1,0:T(8,128)(2,1)S(1)} collective-permute-done((bf16[128,1152]{1,0:T(8,128)(2,1)}, bf16[128,1152]{1,0:T(8,128)(2,1)S(1)}, u32[]{:S(2)}, u32[]{:S(2)}) %collective-permute-start.41) | collective-permute-done | bytes 294944 | tf_op jit(solution)/shard_map/ppermute | solution.py:29
  174.1 4.6 collective-permute-done.42.refs_3_.refs_19_
  179.5 11.1 %expert_first.1 = (bf16[128,1024]{1,0:T(8,128)(2,1)}, bf16[128,1024]{1,0:T(8,128)(2,1)}, bf16[128,1024]{1,0:T(8,128)(2,1)}, bf16[128,1024]{1,0:T(8,128)(2,1)}, b...) custom-call(bf16[2,1,512]{2,1,0:T(2,128)(2,1)} %bitcast.135, ...), custom_call_target="tpu_custom_call" | custom-call | flops 4294967296 | bytes 8388608 | tf_op jit(solution)/shard_map/expert_first/pallas_call | solution.py:937
  194.8 5.4 %collective-permute-done.47 = bf16[128,1024]{1,0:T(8,128)(2,1)S(1)} collective-permute-done((bf16[128,1024]{1,0:T(8,128)(2,1)}, bf16[128,1024]{1,0:T(8,128)(2,1)S(1)}, u32[]{:S(2)}, u32[]{:S(2)}) %collective-permute-start.47) | collective-permute-done | bytes 262176 | tf_op jit(solution)/shard_map/ppermute | solution.py:29
  214.9 5.2 %collective-permute-done.52.refs_9_ = bf16[128,1024]{1,0:T(8,128)(2,1)S(1)} collective-permute-done((bf16[128,1024]{1,0:T(8,128)(2,1)S(1)}, bf16[128,1024]{1,0:T(8,128)(2,1)S(1)}, u32[]{:S(2)}, u32[]{:S(2)}) %collective-permute-start.52) | collective-permute-done | bytes 262176 | tf_op jit(solution)/shard_map/ppermute | solution.py:29
  229.3 16.0 %expert_second.1 = (bf16[128,1024]{1,0:T(8,128)(2,1)}, bf16[128,1024]{1,0:T(8,128)(2,1)}, bf16[128,1024]{1,0:T(8,128)(2,1)}, bf16[128,1024]{1,0:T(8,128)(2,1)}, ...) custom-call(bf16[2,1,512]{2,1,0:T(2,128)(2,1)} %bitcast.134, ...), custom_call_target="tpu_custom_call" | custom-call | flops 6442450944 | bytes 12582912 | tf_op jit(solution)/shard_map/expert_second/pallas_call | solution.py:1092
  249.5 4.0 collective-permute-done.59
  258.0 8.2 %expert_branch.1 = (bf16[1024,1024]{1,0:T(8,128)(2,1)}, bf16[1024,128]{1,0:T(8,128)(2,1)}) custom-call(s32[2]{0:T(128)} %pad_add_fusion.me_ref, bf16[2,1024,512]{2,1,0:T(8,128)(2,1)} %get-tuple-element.365.hidden_in.left_ref, bf16[1,2,1024,1024]{3,2,1,0:T(8,128)(2,1)} %w_back.7, bf16[128,1024]{1,0:T(8,128)(2,1)} %copy-done.16, bf16[128,1024]{1,0:T(8,128)(2,1)} %copy-done.34, ...), custom_call_target="tpu_custom_call" | custom-call | flops 2147483648 | bytes 8388608 | tf_op jit(solution)/shard_map/expert_branch/pallas_call | solution.py:1062
  280.2 5.8 %weight_grads.4.refs_0_ = f32[1,2,1024,1024]{3,2,1,0:T(8,128)} custom-call(bf16[2,1024,512]{2,1,0:T(8,128)(2,1)} %get-tuple-element.365.hidden_in.left_ref, bf16[1024,1024]{1,0:T(8,128)(2,1)} %get-tuple-element.388.right_ref), custom_call_target="tpu_custom_call" | custom-call | flops 2147483648 | bytes 8388608 | tf_op jit(solution)/shard_map/weight_grads/pallas_call | solution.py:1220
  287.0 12.8 %expert_back.1 = (bf16[128,1152]{1,0:T(8,128)(2,1)}, bf16[128,1152]{1,0:T(8,128)(2,1)}, bf16[128,1152]{1,0:T(8,128)(2,1)}, bf16[128,1152]{1,0:T(8,128)(2,1)}, bf...) custom-call(bf16[1024,128]{1,0:T(8,128)(2,1)} %get-tuple-element.376, ...), custom_call_target="tpu_custom_call" | custom-call | flops 4294967296 | bytes 10485760 | tf_op jit(solution)/shard_map/expert_back/pallas_call | solution.py:1168
  303.9 5.4 %collective-permute-done.71 = bf16[128,1152]{1,0:T(8,128)(2,1)S(1)} collective-permute-done((bf16[128,1152]{1,0:T(8,128)(2,1)}, bf16[128,1152]{1,0:T(8,128)(2,1)S(1)}, u32[]{:S(2)}, u32[]{:S(2)}) %collective-permute-start.71) | collective-permute-done | bytes 294944 | tf_op jit(solution)/shard_map/ppermute | solution.py:29
  320.6 4.3 leave_back.1
  324.9 4.7 collective-permute-start.77
  336.3 6.0 %weight_grads.5.refs_0_ = f32[1,2,1024,1024]{3,2,1,0:T(8,128)} custom-call(bf16[1024,1024]{1,0:T(8,128)(2,1)} %get-tuple-element.345.left_ref, bf16[2,1024,512]{2,1,0:T(8,128)(2,1)} %get-tuple-element.415.right_ref), custom_call_target="tpu_custom_call" | custom-call | flops 2147483648 | bytes 8388608 | tf_op jit(solution)/shard_map/weight_grads/pallas_call | solution.py:1220
  345.4 5.0 %backward_rows.1 = (f32[256,1024]{1,0:T(8,128)}, bf16[256,1024]{1,0:T(8,128)(2,1)}, f32[128,1024]{1,0:T(8,128)}, bf16[1024,256]{1,0:T(8,128)(2,1)}) custom-call(s32[2]{0:T(128)} %pad_add_fusion.me_ref, bf16[8,4,256,128]{3,2,1,0:T(8,128)(2,1)} %bitcast.109, bf16[256,256]{1,0:T(8,128)(2,1)} %get-tuple-element.289.unroute_ref, bf16[256,1024]{1,0:T(8,128)(2,1)} %cot_ref.1, ...), custom_call_target="tpu_custom_call" | custom-call | flops 805306368 | bytes 5242880 | tf_op jit(solution)/shard_map/backward_rows/pallas_call | solution.py:393
  350.3 5.2 %all-to-all-start.1 = ((bf16[8,128,256]{2,1,0:T(8,128)(2,1)}), bf16[8,128,256]{2,1,0:T(8,128)(2,1)S(1)}, u32[]{:S(2)}, u32[]{:S(2)}) async-start(bf16[8,128,256]{2,1,0:T(8,128)(2,1)} %bitcast.116), calls=%async_computation.2 | async-start | bytes 1048576 | tf_op jit(solution)/shard_map/all_to_all | solution.py:1322
  358.9 5.8 %weight_grads.6 = f32[1,2,1024,1024]{3,2,1,0:T(8,128)} custom-call(bf16[2,1024,512]{2,1,0:T(8,128)(2,1)} %get-tuple-element.438.left_ref, bf16[1024,1024]{1,0:T(8,128)(2,1)} %get-tuple-element.440.right_ref, f32[1,2,1024,1024]{3,2,1,0:T(8,128)} %weight_grads.4.refs_0_), custom_call_target="tpu_custom_call", output_to_operand_aliasing={{}: (2, {})} | custom-call | flops 2147483648 | bytes 8388608 | tf_op jit(solution)/shard_map/weight_grads/pallas_call | solution.py:1220
  375.5 30.7 %attend_back.1 = (bf16[272,1024]{1,0:T(8,128)(2,1)}, bf16[272,1024]{1,0:T(8,128)(2,1)}, bf16[272,1024]{1,0:T(8,128)(2,1)}, bf16[272,1024]{1,0:T(8,128)(2,1)}, bf...) custom-call(s32[8]{0:T(128)} %stack.97.order_ref, ...), custom_call_target="tpu_custom_call" | custom-call | flops 5368709120 | bytes 5242880 | tf_op jit(solution)/shard_map/attend_back/pallas_call | solution.py:743
  408.9 4.8 collective-permute-start.84
  416.8 7.6 %project_grads.1 = bf16[1024,384]{1,0:T(8,128)(2,1)} custom-call(s32[8]{0:T(128)} %stack.97.order_ref, bf16[8,256,128]{2,1,0:T(8,128)(2,1)} %get-tuple-element.461.dq_ref, bf16[8,256,128]{2,1,0:T(8,128)(2,1)} %get-tuple-element.462.dk_ref, bf16[8,256,128]{2,1,0:T(8,128)(2,1)} %get-tuple-element.463.dv_ref, ...), custom_call_target="tpu_custom_call" | custom-call | flops 1610612736 | bytes 6553600 | tf_op jit(solution)/shard_map/project_grads/pallas_call | solution.py:804
  427.6 5.1 %collective-permute-start.88 = (bf16[272,1024]{1,0:T(8,128)(2,1)S(1)}, bf16[272,1024]{1,0:T(8,128)(2,1)S(1)}, u32[]{:S(2)}, u32[]{:S(2)}) collective-permute-start(bf16[272,1024]{1,0:T(8,128)(2,1)S(1)} %get-tuple-element.543), channel_id=1, source_target_pairs={{0,2},{1,3},{2,4},{3,5},{8,10},{9,11},{10,12},{11,13},{16,18},{17,... | collective-permute-start | bytes 1671176 | tf_op jit(solution)/shard_map/ppermute | solution.py:1478
  437.6 5.5 %collective-permute-done.92 = bf16[256,512]{1,0:T(8,128)(2,1)S(1)} collective-permute-done((bf16[256,512]{1,0:T(8,128)(2,1)S(1)}, bf16[256,512]{1,0:T(8,128)(2,1)S(1)}, u32[]{:S(2)}, u32[]{:S(2)}) %collective-permute-start.92) | collective-permute-done | bytes 262176 | tf_op jit(solution)/shard_map/ppermute | solution.py:29
  449.3 6.4 %collective-permute-start.94 = (bf16[272,1024]{1,0:T(8,128)(2,1)}, bf16[272,1024]{1,0:T(8,128)(2,1)S(1)}, u32[]{:S(2)}, u32[]{:S(2)}) collective-permute-start(bf16[272,1024]{1,0:T(8,128)(2,1)} %add_convert_fusion.1), channel_id=1, source_target_pairs={{0,2},{1,3},{2,4},{3,5},{4,6},{5,7},{8,10},{9,11},{10,12},{11,13},... | collective-permute-start | bytes 1671176 | tf_op jit(solution)/shard_map/ppermute | solution.py:1478
  455.7 5.9 %weight_grads.7 = f32[1,2,1024,1024]{3,2,1,0:T(8,128)} custom-call(bf16[1024,1024]{1,0:T(8,128)(2,1)} %get-tuple-element.481.left_ref, bf16[2,1024,512]{2,1,0:T(8,128)(2,1)} %get-tuple-element.482.right_ref, f32[1,2,1024,1024]{3,2,1,0:T(8,128)} %weight_grads.5.refs_0_), custom_call_target="tpu_custom_call", output_to_operand_aliasing={{}: (2, {})} | custom-call | flops 2147483648 | bytes 8388608 | tf_op jit(solution)/shard_map/weight_grads/pallas_call | solution.py:1220
  (495 shorter events, 228.2 us)
Async XLA Ops:
  7.2 119.2 %all-gather.2.cloned.1.call-start = ((), (), s32[]{:S(2)}) async-start(), calls=%async_computation.5 | async-start | bytes 2359296 | tf_op jit(solution)/shard_map/all_gather | solution.py:1314
  7.7 17.3 %collective-permute-start.1 = (bf16[256,1024]{1,0:T(8,128)(2,1)}, bf16[256,1024]{1,0:T(8,128)(2,1)S(1)}, u32[]{:S(2)}, u32[]{:S(2)}) collective-permute-start(bf16[256,1024]{1,0:T(8,128)(2,1)} %tokens_ref.1), channel_id=1, source_target_pairs={{2,0},{3,1},{4,2},{5,3},{6,4},{7,5},{10,8},{11,9},{12,10},{13,11},... | collective-permute-start | bytes 1572872 | tf_op jit(solution)/shard_map/ppermute | solution.py:1353
  9.0 17.3 %collective-permute-start = (bf16[256,1024]{1,0:T(8,128)(2,1)}, bf16[256,1024]{1,0:T(8,128)(2,1)S(1)}, u32[]{:S(2)}, u32[]{:S(2)}) collective-permute-start(bf16[256,1024]{1,0:T(8,128)(2,1)} %tokens_ref.1), channel_id=1, source_target_pairs={{0,2},{1,3},{2,4},{3,5},{4,6},{5,7},{8,10},{9,11},{10,12},{11,13},... | collective-permute-start | bytes 1572872 | tf_op jit(solution)/shard_map/ppermute | solution.py:1352
  27.0 18.4 %collective-permute-start.5 = (bf16[256,1024]{1,0:T(8,128)(2,1)S(1)}, bf16[256,1024]{1,0:T(8,128)(2,1)S(1)}, u32[]{:S(2)}, u32[]{:S(2)}) collective-permute-start(bf16[256,1024]{1,0:T(8,128)(2,1)S(1)} %collective-permute-done.1), channel_id=1, source_target_pairs={{2,0},{3,1},{4,2},{5,3},{10,8},{11,9},{12,10},{13,11},{18,16},{19,... | collective-permute-start | bytes 1572872 | tf_op jit(solution)/shard_map/ppermute | solution.py:1353
  52.4 13.1 %collective-permute-start.11 = (bf16[256,1024]{1,0:T(8,128)(2,1)S(1)}, bf16[256,1024]{1,0:T(8,128)(2,1)S(1)}, u32[]{:S(2)}, u32[]{:S(2)}) collective-permute-start(bf16[256,1024]{1,0:T(8,128)(2,1)S(1)} %collective-permute-done.5), channel_id=1, source_target_pairs={{2,0},{3,1},{10,8},{11,9},{18,16},{19,17},{26,24},{27,25}} | collective-permute-start | bytes 1572872 | tf_op jit(solution)/shard_map/ppermute | solution.py:1353
  70.2 34.1 %all-to-all-start = ((bf16[8,32,1024]{2,1,0:T(8,128)(2,1)}), bf16[8,32,1024]{2,1,0:T(8,128)(2,1)S(1)}, u32[]{:S(2)}, u32[]{:S(2)}) async-start(bf16[8,32,1024]{2,1,0:T(8,128)(2,1)} %bitcast.36), calls=%async_computation | async-start | bytes 1048576 | tf_op jit(solution)/shard_map/all_to_all | solution.py:1322
  74.0 290.7 %reduce-scatter.3.cloned.1.call-start = ((), (), s32[]{:S(2)}) async-start(), calls=%async_computation.6 | async-start | bytes 2621440 | tf_op jit(solution)/shard_map/reduce_scatter | solution.py:1449
  104.4 16.9 %collective-permute-start.28 = (bf16[128,1024]{1,0:T(8,128)(2,1)S(1)}, bf16[128,1024]{1,0:T(8,128)(2,1)S(1)}, u32[]{:S(2)}, u32[]{:S(2)}) collective-permute-start(bf16[128,1024]{1,0:T(8,128)(2,1)S(1)} %get-tuple-element.350.refs_4_), channel_id=1, source_target_pairs={{0,16},{8,24},{16,0},{24,8},{1,17},{9,25},{17,1},{25,9},{2,18},{10... | collective-permute-start | bytes 786440 | tf_op jit(solution)/shard_map/ppermute | solution.py:29
  106.0 15.3 %collective-permute-start.27 = (bf16[128,1024]{1,0:T(8,128)(2,1)S(1)}, bf16[128,1024]{1,0:T(8,128)(2,1)S(1)}, u32[]{:S(2)}, u32[]{:S(2)}) collective-permute-start(bf16[128,1024]{1,0:T(8,128)(2,1)S(1)} %get-tuple-element.346.refs_0_), channel_id=1, source_target_pairs={{0,8},{8,0},{16,24},{24,16},{1,9},{9,1},{17,25},{25,17},{2,10},{10... | collective-permute-start | bytes 786440 | tf_op jit(solution)/shard_map/ppermute | solution.py:29
  122.4 13.4 %collective-permute-start.37 = (bf16[128,1024]{1,0:T(8,128)(2,1)S(1)}, bf16[128,1024]{1,0:T(8,128)(2,1)S(1)}, u32[]{:S(2)}, u32[]{:S(2)}) collective-permute-start(bf16[128,1024]{1,0:T(8,128)(2,1)S(1)} %collective-permute-done.27.refs_1_), channel_id=1, source_target_pairs={{0,16},{8,24},{16,0},{24,8},{1,17},{9,25},{17,1},{25,9},{2,18},{10... | collective-permute-start | bytes 786440 | tf_op jit(solution)/shard_map/ppermute | solution.py:29
  123.4 14.4 %collective-permute-start.38 = (bf16[128,1024]{1,0:T(8,128)(2,1)S(1)}, bf16[128,1024]{1,0:T(8,128)(2,1)S(1)}, u32[]{:S(2)}, u32[]{:S(2)}) collective-permute-start(bf16[128,1024]{1,0:T(8,128)(2,1)S(1)} %get-tuple-element.350.refs_4_), channel_id=1, source_target_pairs={{0,8},{8,0},{16,24},{24,16},{1,9},{9,1},{17,25},{25,17},{2,10},{10... | collective-permute-start | bytes 786440 | tf_op jit(solution)/shard_map/ppermute | solution.py:29
  125.6 14.5 %collective-permute-start.39 = (bf16[128,1024]{1,0:T(8,128)(2,1)S(1)}, bf16[128,1024]{1,0:T(8,128)(2,1)S(1)}, u32[]{:S(2)}, u32[]{:S(2)}) collective-permute-start(bf16[128,1024]{1,0:T(8,128)(2,1)S(1)} %collective-permute-done.28.refs_6_), channel_id=1, source_target_pairs={{0,8},{8,0},{16,24},{24,16},{1,9},{9,1},{17,25},{25,17},{2,10},{10... | collective-permute-start | bytes 786440 | tf_op jit(solution)/shard_map/ppermute | solution.py:29
  130.8 13.1 %collective-permute-start.30 = (bf16[32,1152]{1,0:T(8,128)(2,1)}, bf16[32,1152]{1,0:T(8,128)(2,1)S(1)}, u32[]{:S(2)}, u32[]{:S(2)}) collective-permute-start(bf16[32,1152]{1,0:T(8,128)(2,1)} %get-tuple-element.325), channel_id=1, source_target_pairs={{0,2},{1,3},{2,0},{3,1},{4,6},{5,7},{6,4},{7,5},{8,10},{9,11},{10,... | collective-permute-start | bytes 221192 | tf_op jit(solution)/shard_map/ppermute | solution.py:29
  158.1 16.0 %collective-permute-start.41 = (bf16[128,1152]{1,0:T(8,128)(2,1)}, bf16[128,1152]{1,0:T(8,128)(2,1)S(1)}, u32[]{:S(2)}, u32[]{:S(2)}) collective-permute-start(bf16[128,1152]{1,0:T(8,128)(2,1)} %get-tuple-element.343.refs_0_.refs_16_), channel_id=1, source_target_pairs={{0,16},{8,24},{16,0},{24,8},{1,17},{9,25},{17,1},{25,9},{2,18},{10... | collective-permute-start | bytes 884744 | tf_op jit(solution)/shard_map/ppermute | solution.py:29
  159.6 14.5 %collective-permute-start.43 = (bf16[128,1152]{1,0:T(8,128)(2,1)}, bf16[128,1152]{1,0:T(8,128)(2,1)S(1)}, u32[]{:S(2)}, u32[]{:S(2)}) collective-permute-start(bf16[128,1152]{1,0:T(8,128)(2,1)} %get-tuple-element.344.refs_4_.refs_20_), channel_id=1, source_target_pairs={{0,8},{8,0},{16,24},{24,16},{1,9},{9,1},{17,25},{25,17},{2,10},{10... | collective-permute-start | bytes 884744 | tf_op jit(solution)/shard_map/ppermute | solution.py:29
  165.7 13.0 %collective-permute-start.42 = (bf16[128,1152]{1,0:T(8,128)(2,1)S(1)}, bf16[128,1152]{1,0:T(8,128)(2,1)S(1)}, u32[]{:S(2)}, u32[]{:S(2)}) collective-permute-start(bf16[128,1152]{1,0:T(8,128)(2,1)S(1)} %collective-permute-done.40.refs_1_.refs_17_), channel_id=1, source_target_pairs={{0,16},{8,24},{16,0},{24,8},{1,17},{9,25},{17,1},{25,9},{2,18},{10... | collective-permute-start | bytes 884744 | tf_op jit(solution)/shard_map/ppermute | solution.py:29
  191.8 14.0 %collective-permute-start.46 = (bf16[128,1024]{1,0:T(8,128)(2,1)}, bf16[128,1024]{1,0:T(8,128)(2,1)S(1)}, u32[]{:S(2)}, u32[]{:S(2)}) collective-permute-start(bf16[128,1024]{1,0:T(8,128)(2,1)} %get-tuple-element.356), channel_id=1, source_target_pairs={{0,8},{8,0},{16,24},{24,16},{1,9},{9,1},{17,25},{25,17},{2,10},{10... | collective-permute-start | bytes 786440 | tf_op jit(solution)/shard_map/ppermute | solution.py:29
  212.7 13.0 %collective-permute-start.53 = (bf16[128,1024]{1,0:T(8,128)(2,1)S(1)}, bf16[128,1024]{1,0:T(8,128)(2,1)S(1)}, u32[]{:S(2)}, u32[]{:S(2)}) collective-permute-start(bf16[128,1024]{1,0:T(8,128)(2,1)S(1)} %get-tuple-element.363.refs_8_), channel_id=1, source_target_pairs={{0,16},{8,24},{16,0},{24,8},{1,17},{9,25},{17,1},{25,9},{2,18},{10... | collective-permute-start | bytes 786440 | tf_op jit(solution)/shard_map/ppermute | solution.py:29
  246.8 19.4 %collective-permute-start.58 = (bf16[128,1024]{1,0:T(8,128)(2,1)}, bf16[128,1024]{1,0:T(8,128)(2,1)S(1)}, u32[]{:S(2)}, u32[]{:S(2)}) collective-permute-start(bf16[128,1024]{1,0:T(8,128)(2,1)} %get-tuple-element.369), channel_id=1, source_target_pairs={{0,8},{8,0},{16,24},{24,16},{1,9},{9,1},{17,25},{25,17},{2,10},{10... | collective-permute-start | bytes 786440 | tf_op jit(solution)/shard_map/ppermute | solution.py:29
  247.9 18.3 %collective-permute-start.61 = (bf16[128,1024]{1,0:T(8,128)(2,1)}, bf16[128,1024]{1,0:T(8,128)(2,1)S(1)}, u32[]{:S(2)}, u32[]{:S(2)}) collective-permute-start(bf16[128,1024]{1,0:T(8,128)(2,1)} %get-tuple-element.373), channel_id=1, source_target_pairs={{0,16},{8,24},{16,0},{24,8},{1,17},{9,25},{17,1},{25,9},{2,18},{10... | collective-permute-start | bytes 786440 | tf_op jit(solution)/shard_map/ppermute | solution.py:29
  272.9 13.1 %collective-permute-start.65 = (bf16[128,1024]{1,0:T(8,128)(2,1)}, bf16[128,1024]{1,0:T(8,128)(2,1)S(1)}, u32[]{:S(2)}, u32[]{:S(2)}) collective-permute-start(bf16[128,1024]{1,0:T(8,128)(2,1)} %get-tuple-element.391.refs_0_), channel_id=1, source_target_pairs={{0,16},{8,24},{16,0},{24,8},{1,17},{9,25},{17,1},{25,9},{2,18},{10... | collective-permute-start | bytes 786440 | tf_op jit(solution)/shard_map/ppermute | solution.py:29
  300.8 13.2 %collective-permute-start.70 = (bf16[128,1152]{1,0:T(8,128)(2,1)}, bf16[128,1152]{1,0:T(8,128)(2,1)S(1)}, u32[]{:S(2)}, u32[]{:S(2)}) collective-permute-start(bf16[128,1152]{1,0:T(8,128)(2,1)} %get-tuple-element.401), channel_id=1, source_target_pairs={{0,8},{8,0},{16,24},{24,16},{1,9},{9,1},{17,25},{25,17},{2,10},{10... | collective-permute-start | bytes 884744 | tf_op jit(solution)/shard_map/ppermute | solution.py:29
  350.3 20.6 %all-to-all-start.1 = ((bf16[8,128,256]{2,1,0:T(8,128)(2,1)}), bf16[8,128,256]{2,1,0:T(8,128)(2,1)S(1)}, u32[]{:S(2)}, u32[]{:S(2)}) async-start(bf16[8,128,256]{2,1,0:T(8,128)(2,1)} %bitcast.116), calls=%async_computation.2 | async-start | bytes 1048576 | tf_op jit(solution)/shard_map/all_to_all | solution.py:1322
  355.5 69.4 %reduce-scatter.5.cloned.1.call-start = ((), (), s32[]{:S(2)}) async-start(), calls=%async_computation.7 | async-start | bytes 2359296 | tf_op jit(solution)/shard_map/reduce_scatter | solution.py:1466
  371.7 34.5 %all-to-all-start.2 = ((bf16[8,32,1024]{2,1,0:T(8,128)(2,1)}), bf16[8,32,1024]{2,1,0:T(8,128)(2,1)S(1)}, u32[]{:S(2)}, u32[]{:S(2)}) async-start(bf16[8,32,1024]{2,1,0:T(8,128)(2,1)} %bitcast.45), calls=%async_computation.3 | async-start | bytes 1048576 | tf_op jit(solution)/shard_map/all_to_all | solution.py:1322
  407.3 17.6 %collective-permute-start.87 = (bf16[272,1024]{1,0:T(8,128)(2,1)}, bf16[272,1024]{1,0:T(8,128)(2,1)}, u32[]{:S(2)}, u32[]{:S(2)}) collective-permute-start(bf16[272,1024]{1,0:T(8,128)(2,1)} %get-tuple-element.467), channel_id=1, source_target_pairs={{0,1},{1,0},{2,3},{3,2},{4,5},{5,4},{6,7},{7,6},{8,9},{9,8},{10,11... | collective-permute-start | bytes 1671176 | tf_op jit(solution)/shard_map/ppermute | solution.py:29
  408.9 16.1 %collective-permute-start.84 = (bf16[272,1024]{1,0:T(8,128)(2,1)S(1)}, bf16[272,1024]{1,0:T(8,128)(2,1)}, u32[]{:S(2)}, u32[]{:S(2)}) collective-permute-start(bf16[272,1024]{1,0:T(8,128)(2,1)S(1)} %add_convert_fusion.5), channel_id=1, source_target_pairs={{0,2},{1,3},{8,10},{9,11},{16,18},{17,19},{24,26},{25,27}} | collective-permute-start | bytes 1671176 | tf_op jit(solution)/shard_map/ppermute | solution.py:1478
  426.9 19.1 %collective-permute-start.89 = (bf16[272,1024]{1,0:T(8,128)(2,1)S(1)}, bf16[272,1024]{1,0:T(8,128)(2,1)S(1)}, u32[]{:S(2)}, u32[]{:S(2)}) collective-permute-start(bf16[272,1024]{1,0:T(8,128)(2,1)S(1)} %get-tuple-element.542), channel_id=1, source_target_pairs={{4,2},{5,3},{6,4},{7,5},{12,10},{13,11},{14,12},{15,13},{20,18},{2... | collective-permute-start | bytes 1671176 | tf_op jit(solution)/shard_map/ppermute | solution.py:1481
  427.6 18.4 %collective-permute-start.88 = (bf16[272,1024]{1,0:T(8,128)(2,1)S(1)}, bf16[272,1024]{1,0:T(8,128)(2,1)S(1)}, u32[]{:S(2)}, u32[]{:S(2)}) collective-permute-start(bf16[272,1024]{1,0:T(8,128)(2,1)S(1)} %get-tuple-element.543), channel_id=1, source_target_pairs={{0,2},{1,3},{2,4},{3,5},{8,10},{9,11},{10,12},{11,13},{16,18},{17,... | collective-permute-start | bytes 1671176 | tf_op jit(solution)/shard_map/ppermute | solution.py:1478
  443.1 24.0 %collective-permute-start.93 = (bf16[272,1024]{1,0:T(8,128)(2,1)}, bf16[272,1024]{1,0:T(8,128)(2,1)S(1)}, u32[]{:S(2)}, u32[]{:S(2)}) collective-permute-start(bf16[272,1024]{1,0:T(8,128)(2,1)} %get-tuple-element.475), channel_id=1, source_target_pairs={{0,1},{1,0},{2,3},{3,2},{4,5},{5,4},{6,7},{7,6},{8,9},{9,8},{10,11... | collective-permute-start | bytes 1671176 | tf_op jit(solution)/shard_map/ppermute | solution.py:29
  448.0 17.8 %collective-permute-start.95 = (bf16[272,1024]{1,0:T(8,128)(2,1)}, bf16[272,1024]{1,0:T(8,128)(2,1)S(1)}, u32[]{:S(2)}, u32[]{:S(2)}) collective-permute-start(bf16[272,1024]{1,0:T(8,128)(2,1)} %add_convert_fusion), channel_id=1, source_target_pairs={{2,0},{3,1},{4,2},{5,3},{6,4},{7,5},{10,8},{11,9},{12,10},{13,11},... | collective-permute-start | bytes 1671176 | tf_op jit(solution)/shard_map/ppermute | solution.py:1481
  449.3 17.8 %collective-permute-start.94 = (bf16[272,1024]{1,0:T(8,128)(2,1)}, bf16[272,1024]{1,0:T(8,128)(2,1)S(1)}, u32[]{:S(2)}, u32[]{:S(2)}) collective-permute-start(bf16[272,1024]{1,0:T(8,128)(2,1)} %add_convert_fusion.1), channel_id=1, source_target_pairs={{0,2},{1,3},{2,4},{3,5},{4,6},{5,7},{8,10},{9,11},{10,12},{11,13},... | collective-permute-start | bytes 1671176 | tf_op jit(solution)/shard_map/ppermute | solution.py:1478
  (173 other events, 1588.7 us)
Sparse Core Ops, SparseCore 0:
  68.3 39.4 all-gather.1
  320.0 38.1 reduce-scatter.2
  371.1 38.0 reduce-scatter.4
